TPU v7x, 32 devices: a whole 2x2x4 slice. The times are simulated.
32 devices in a mesh: dp: 4 (over z), fsdp: 8 (over y, x, core).
Axes of the slice: x: 2, y: 2, z: 4, core: 2. Of those that a mesh axis runs over, the one named last changes fastest.
Arguments:
- tokens: bfloat16 [8192, 1024], P(('dp', 'fsdp')), may hold values from -6 to 6
- cotangent: bfloat16 [8192, 1024], P(('dp', 'fsdp')), may hold values from -6 to 6
- teacher: bfloat16 [8192, 1024], P(('dp', 'fsdp')), may hold values from -6 to 6
- valid_mask: int32 [8192], P(('dp', 'fsdp')), may hold values from 0 to 1, as said below
- deal_rows: int32 [8192], P(('dp', 'fsdp')), may hold values from 0 to 8191, as said below
- lengths: int32 [64, 3], P(('dp', 'fsdp')), may hold values from 1 to 96, 128 in all within a row
- w_in: bfloat16 [1024, 4096], P(('dp', 'fsdp')), may hold values from -0.1875 to 0.1875
- w_beta: bfloat16 [1024, 8], P(('dp', 'fsdp')), may hold values from -0.1875 to 0.1875
- conv_kernel: bfloat16 [4, 3072], P(None, ('dp', 'fsdp')), may hold values from -3 to 3
- w_out: bfloat16 [1024, 1024], P(('dp', 'fsdp')), may hold values from -0.1875 to 0.1875
- norm_gain: bfloat16 [1024], P(('dp', 'fsdp')), may hold values from 0.25 to 1.75
- out_gain: bfloat16 [128], replicated, may hold values from 0.25 to 1.75
- ffn_gain: bfloat16 [1024], P(('dp', 'fsdp')), may hold values from 0.25 to 1.75
- w_gu: bfloat16 [1024, 5632], P(('dp', 'fsdp')), may hold values from -0.1875 to 0.1875
- w_down: bfloat16 [2816, 1024], P(('dp', 'fsdp')), may hold values from -0.109375 to 0.109375
Outputs:
- output: bfloat16 [8192, 1024], P(('dp', 'fsdp'))
- input_grad: bfloat16 [8192, 1024], P(('dp', 'fsdp'))
- grad_w_in: float32 [1024, 4096], P(('dp', 'fsdp'))
- grad_w_beta: float32 [1024, 8], P(('dp', 'fsdp'))
- grad_conv_kernel: float32 [4, 3072], P(None, ('dp', 'fsdp'))
- grad_w_out: float32 [1024, 1024], P(('dp', 'fsdp'))
- grad_norm_gain: float32 [1024], P(('dp', 'fsdp'))
- grad_out_gain: float32 [128], replicated
- grad_ffn_gain: float32 [1024], P(('dp', 'fsdp'))
- grad_w_gu: float32 [1024, 5632], P(('dp', 'fsdp'))
- grad_w_down: float32 [2816, 1024], P(('dp', 'fsdp'))
- loss: float32 [], replicated
Inputs may be any that keep to these rules, and one draw needn't show every extreme that they name: deal_rows is a permutation of 0 .. 8191. Dealt rows d * 256 to (d+1) * 256 - 1 belong to device d (dp+fsdp order, dp slowest), and each device's arriving rows go exactly 8 to every device. Each row gives the lengths of the 3 sequences that fill one block of 128 dealt rows, in order; the largest of each row is 96. `valid_mask`: the first arriving row of each device is 1.
All inputs are finite; a program needn't handle non-finite values.
Results may differ from a plain program's by a relative error of at most 0.0097.
Values may be sent and summed in bfloat16 or wider, within the bound.
A program may use at most 128 MiB of HBM per device.

v0:
```python
import jax
import jax.numpy as jnp
from jax import lax
from jax.sharding import PartitionSpec as P

D = 1024
HEADS = 8
HEAD_DIM = 128
FF = 2816
CONV = 4
SPAN = 64


highest_precision = lax.Precision.HIGHEST


def rms_norm(values, gains):
    return values * lax.rsqrt(jnp.mean(values * values, axis=-1, keepdims=True) + 1e-05) * gains


def segment_ids(length_row, row_count):
    ends_at = jnp.cumsum(length_row)
    places = jnp.arange(row_count, dtype=jnp.int32)
    return jnp.sum((places[:, None] >= ends_at[None, :]).astype(jnp.int32), axis=1)


def short_conv(projected, kernel, segment):
    row_count = projected.shape[0]
    total = projected * kernel[CONV - 1]
    for offset in range(1, CONV):
        moved = jnp.concatenate(
            [jnp.zeros((offset, projected.shape[1]), jnp.float32), projected[: row_count - offset]],
            axis=0,
        )
        seg_moved = jnp.concatenate(
            [jnp.full((offset,), -1, jnp.int32), segment[: row_count - offset]]
        )
        same_seq = (seg_moved == segment).astype(jnp.float32)
        total = total + moved * kernel[CONV - 1 - offset] * same_seq[:, None]
    return jax.nn.silu(total)


def delta_rule(queries, keys_in, values, strength, segment):
    row_count, head_count, per_head_width = queries.shape
    span_count = row_count // SPAN

    def blocked(array):
        return jnp.swapaxes(array.reshape(span_count, SPAN, head_count, -1), 1, 2)

    q_all, k_all, v_all = (blocked(queries), blocked(keys_in), blocked(values))
    b_all = jnp.swapaxes(strength.reshape(span_count, SPAN, head_count), 1, 2)
    s_all = segment.reshape(span_count, SPAN)
    p_all = jnp.concatenate([jnp.full((1,), -1, jnp.int32), s_all[:-1, -1]])
    strict_lower = jnp.tril(jnp.ones((SPAN, SPAN), jnp.float32), -1)
    with_diag = jnp.tril(jnp.ones((SPAN, SPAN), jnp.float32))
    identity = jnp.eye(SPAN, dtype=jnp.float32)

    def advance(running_state, sliced):
        query_window, key_window, v_span, b_span, s_span, p_span = sliced
        same_seq = (s_span[:, None] == s_span[None, :]).astype(jnp.float32)
        carried_state = (s_span == p_span).astype(jnp.float32)
        final_sequence = (s_span == s_span[-1]).astype(jnp.float32)
        retain_state = carried_state[-1]
        key_gram = jnp.einsum("hik,hjk->hij", key_window, key_window, precision=highest_precision)
        system = identity + key_gram * same_seq * strict_lower * b_span[:, :, None]
        right_side = (
            jnp.concatenate([v_span, key_window * carried_state[None, :, None]], axis=-1)
            * b_span[:, :, None]
        )
        solved_system = jax.scipy.linalg.solve_triangular(
            system, right_side, lower=True, unit_diagonal=True
        )
        pseudo_target = solved_system[..., :per_head_width] - jnp.einsum(
            "arg,agw->arw",
            solved_system[..., per_head_width:],
            running_state,
            precision=highest_precision,
        )
        scores = (
            jnp.einsum("hik,hjk->hij", query_window, key_window, precision=highest_precision)
            * same_seq
            * with_diag
        )
        result_output = jnp.einsum(
            "arg,agw->arw",
            query_window * carried_state[None, :, None],
            running_state,
            precision=highest_precision,
        )
        result_output = result_output + jnp.einsum(
            "hij,hjv->hiv", scores, pseudo_target, precision=highest_precision
        )
        updated_state = retain_state * running_state + jnp.einsum(
            "cen,cer->cnr",
            key_window * final_sequence[None, :, None],
            pseudo_target,
            precision=highest_precision,
        )
        return (updated_state, result_output)

    initial = jnp.zeros((head_count, per_head_width, per_head_width), jnp.float32)
    final_state, outputs = lax.scan(advance, initial, (q_all, k_all, v_all, b_all, s_all, p_all))
    return jnp.swapaxes(outputs, 1, 2).reshape(row_count, head_count, per_head_width)


def mixer_core(projected, beta_pre, kernel, gains_out, segment):
    row_count = projected.shape[0]
    mixed = short_conv(projected[:, : 3 * D], kernel, segment)
    queries = mixed[:, :D].reshape(row_count, HEADS, HEAD_DIM)
    keys_in = mixed[:, D : 2 * D].reshape(row_count, HEADS, HEAD_DIM)
    values = mixed[:, 2 * D :].reshape(row_count, HEADS, HEAD_DIM)
    queries = (
        queries
        * lax.rsqrt(jnp.sum(queries * queries, axis=-1, keepdims=True) + 1e-06)
        * HEAD_DIM ** (-0.5)
    )
    keys_in = keys_in * lax.rsqrt(jnp.sum(keys_in * keys_in, axis=-1, keepdims=True) + 1e-06)
    strength = jax.nn.sigmoid(beta_pre)
    core = delta_rule(queries, keys_in, values, strength, segment)
    gate_part = projected[:, 3 * D :].reshape(row_count, HEADS, HEAD_DIM)
    normed = rms_norm(core, gains_out) * jax.nn.silu(gate_part)
    return normed.reshape(row_count, D)


def gated_unit(both_parts):
    return jax.nn.silu(both_parts[:, :FF]) * both_parts[:, FF:]


def times_t(left, right):
    return lax.dot_general(
        left, right, (((1,), (1,)), ((), ())), preferred_element_type=jnp.float32
    )


def over_rows(left, right):
    return lax.dot_general(
        left, right, (((0,), (0,)), ((), ())), preferred_element_type=jnp.float32
    )


def local(
    tokens,
    cotangent,
    teacher,
    valid_mask,
    deal_rows,
    lengths,
    w_in,
    w_beta,
    conv_kernel,
    w_out,
    norm_gain,
    out_gain,
    ffn_gain,
    w_gu,
    w_down,
):
    shards = lax.axis_size(("dp", "fsdp"))
    rows_dev = tokens.shape[0]
    share = rows_dev // shards
    batches = lengths.shape[0]
    rows_mb = rows_dev // batches
    counted = lax.psum(jnp.sum(valid_mask.astype(jnp.float32)), ("dp", "fsdp"))
    loss_weight = rows_dev * shards / counted
    target = deal_rows // rows_dev
    sorting = jnp.argsort(target, stable=True)
    spot = (deal_rows % rows_dev)[sorting]

    def by_peer(array):
        return array[sorting].reshape((shards, share) + array.shape[1:])

    send_x = by_peer(tokens)
    send_g = by_peer(cotangent)
    send_t = by_peer(teacher)
    send_m = by_peer(valid_mask)
    send_p = spot.reshape(shards, share)
    incoming = (
        lax.all_to_all(send_x, ("dp", "fsdp"), split_axis=0, concat_axis=0, tiled=True),
        lax.all_to_all(send_g, ("dp", "fsdp"), split_axis=0, concat_axis=0, tiled=True),
        lax.all_to_all(send_t, ("dp", "fsdp"), split_axis=0, concat_axis=0, tiled=True),
        lax.all_to_all(send_m, ("dp", "fsdp"), split_axis=0, concat_axis=0, tiled=True),
        lax.all_to_all(send_p, ("dp", "fsdp"), split_axis=0, concat_axis=0, tiled=True),
    )
    arrived = incoming[4].reshape(rows_dev)

    def settle(array):
        flat_rows = array.reshape((rows_dev,) + array.shape[2:])
        return jnp.zeros(flat_rows.shape, flat_rows.dtype).at[arrived].set(flat_rows)

    inputs_local = settle(incoming[0])
    grads_local = settle(incoming[1]).astype(jnp.float32)
    teacher_local = settle(incoming[2]).astype(jnp.float32)
    mask_local = settle(incoming[3]).astype(jnp.float32)
    held = None
    gain_out_f = out_gain.astype(jnp.float32)
    kept_in, kept_proj, kept_beta, kept_on, kept_dz = ([], [], [], [], [])
    kept_ffn_in, kept_dgu, kept_hid, kept_df = ([], [], [], [])
    outputs_kept, grads_kept = ([], [])
    kernel_grad = jnp.zeros((CONV, 3 * D), jnp.float32)
    out_gain_grad = jnp.zeros((HEAD_DIM,), jnp.float32)
    norm_grad = jnp.zeros((D,), jnp.float32)
    ffn_norm_grad = jnp.zeros((D,), jnp.float32)
    loss_part = jnp.zeros((), jnp.float32)
    for step_index in range(batches):
        held = (
            (
                lax.all_gather(w_in, ("dp", "fsdp"), axis=0, tiled=True),
                lax.all_gather(w_beta, ("dp", "fsdp"), axis=0, tiled=True),
                lax.all_gather(conv_kernel, ("dp", "fsdp"), axis=1, tiled=True),
                lax.all_gather(w_out, ("dp", "fsdp"), axis=0, tiled=True),
                lax.all_gather(norm_gain, ("dp", "fsdp"), axis=0, tiled=True),
            ),
            (
                lax.all_gather(w_gu, ("dp", "fsdp"), axis=0, tiled=True),
                lax.all_gather(w_down, ("dp", "fsdp"), axis=0, tiled=True),
                lax.all_gather(ffn_gain, ("dp", "fsdp"), axis=0, tiled=True),
            ),
        )
        (win_full, wbeta_full, kernel_full, wout_full, gain_one), (
            wgu_full,
            wdown_full,
            gain_two,
        ) = held
        lower_row = step_index * rows_mb
        rows_in = inputs_local[lower_row : lower_row + rows_mb].astype(jnp.float32)
        rows_grad = grads_local[lower_row : lower_row + rows_mb]
        rows_teacher = teacher_local[lower_row : lower_row + rows_mb]
        rows_mask = mask_local[lower_row : lower_row + rows_mb]
        segment = segment_ids(lengths[step_index], rows_mb)
        normed_one, norm_pull = jax.vjp(rms_norm, rows_in, gain_one.astype(jnp.float32))
        normed_in = normed_one.astype(jnp.bfloat16)
        projected = jnp.dot(normed_in, win_full, preferred_element_type=jnp.float32)
        beta_pre = jnp.dot(normed_in, wbeta_full, preferred_element_type=jnp.float32)

        def core_fn(proj_in, beta_in, kernel_in, gains_in):
            return mixer_core(proj_in, beta_in, kernel_in, gains_in, segment)

        mixed_f, core_pull = jax.vjp(
            core_fn, projected, beta_pre, kernel_full.astype(jnp.float32), gain_out_f
        )
        mixed_out = mixed_f.astype(jnp.bfloat16)
        resid = rows_in + jnp.dot(mixed_out, wout_full, preferred_element_type=jnp.float32)
        normed_two, norm_two_pull = jax.vjp(rms_norm, resid, gain_two.astype(jnp.float32))
        normed_ffn = normed_two.astype(jnp.bfloat16)
        both_parts = jnp.dot(normed_ffn, wgu_full, preferred_element_type=jnp.float32)
        hidden_f, unit_pull = jax.vjp(gated_unit, both_parts)
        hidden = hidden_f.astype(jnp.bfloat16)
        result_output = resid + jnp.dot(hidden, wdown_full, preferred_element_type=jnp.float32)
        errors = result_output - rows_teacher
        loss_part = loss_part + jnp.sum(rows_mask[:, None] * errors * errors)
        grad_result = rows_grad + loss_weight * rows_mask[:, None] * errors
        grad_ffn_out = grad_result.astype(jnp.bfloat16)
        (grad_both,) = unit_pull(times_t(grad_ffn_out, wdown_full))
        grad_gu = grad_both.astype(jnp.bfloat16)
        grad_resid, grad_gain_two = norm_two_pull(times_t(grad_gu, wgu_full))
        grad_resid = grad_resid + grad_result
        grad_mix = grad_resid.astype(jnp.bfloat16)
        grad_proj, grad_beta, grad_kernel, grad_gains = core_pull(times_t(grad_mix, wout_full))
        grad_proj_b = grad_proj.astype(jnp.bfloat16)
        grad_beta_b = grad_beta.astype(jnp.bfloat16)
        grad_norm_in = times_t(grad_proj_b, win_full) + times_t(grad_beta_b, wbeta_full)
        grad_rows, grad_gain_one = norm_pull(grad_norm_in)
        grad_rows = grad_resid + grad_rows
        out_gain_grad = out_gain_grad + grad_gains
        kernel_grad = kernel_grad + grad_kernel
        norm_grad = norm_grad + grad_gain_one
        ffn_norm_grad = ffn_norm_grad + grad_gain_two
        kept_in.append(normed_in)
        kept_proj.append(grad_proj_b)
        kept_beta.append(grad_beta_b)
        kept_on.append(mixed_out)
        kept_dz.append(grad_mix)
        kept_ffn_in.append(normed_ffn)
        kept_dgu.append(grad_gu)
        kept_hid.append(hidden)
        kept_df.append(grad_ffn_out)
        outputs_kept.append(result_output.astype(jnp.bfloat16))
        grads_kept.append(grad_rows.astype(jnp.bfloat16))
    ffn_parts = (
        lax.psum_scatter(
            over_rows(jnp.concatenate(kept_ffn_in), jnp.concatenate(kept_dgu)),
            ("dp", "fsdp"),
            scatter_dimension=0,
            tiled=True,
        ),
        lax.psum_scatter(
            over_rows(jnp.concatenate(kept_hid), jnp.concatenate(kept_df)),
            ("dp", "fsdp"),
            scatter_dimension=0,
            tiled=True,
        ),
        lax.psum_scatter(ffn_norm_grad, ("dp", "fsdp"), scatter_dimension=0, tiled=True),
    )
    all_in = jnp.concatenate(kept_in)
    mixer_parts = (
        lax.psum_scatter(
            over_rows(all_in, jnp.concatenate(kept_proj)),
            ("dp", "fsdp"),
            scatter_dimension=0,
            tiled=True,
        ),
        lax.psum_scatter(
            over_rows(all_in, jnp.concatenate(kept_beta)),
            ("dp", "fsdp"),
            scatter_dimension=0,
            tiled=True,
        ),
        lax.psum_scatter(kernel_grad, ("dp", "fsdp"), scatter_dimension=1, tiled=True),
        lax.psum_scatter(
            over_rows(jnp.concatenate(kept_on), jnp.concatenate(kept_dz)),
            ("dp", "fsdp"),
            scatter_dimension=0,
            tiled=True,
        ),
        lax.psum_scatter(norm_grad, ("dp", "fsdp"), scatter_dimension=0, tiled=True),
    )
    loss_sum, out_gain_total = lax.psum((loss_part, out_gain_grad), ("dp", "fsdp"))
    loss_value = loss_sum / (D * counted)
    outputs_local = jnp.concatenate(outputs_kept)
    input_local = jnp.concatenate(grads_kept)
    back_y = outputs_local[arrived].reshape(shards, share, D)
    back_dx = input_local[arrived].reshape(shards, share, D)
    returned = (
        lax.all_to_all(back_y, ("dp", "fsdp"), split_axis=0, concat_axis=0, tiled=True),
        lax.all_to_all(back_dx, ("dp", "fsdp"), split_axis=0, concat_axis=0, tiled=True),
    )
    output = (
        jnp.zeros((rows_dev, D), jnp.bfloat16).at[sorting].set(returned[0].reshape(rows_dev, D))
    )
    input_grad = (
        jnp.zeros((rows_dev, D), jnp.bfloat16).at[sorting].set(returned[1].reshape(rows_dev, D))
    )
    return (
        output,
        input_grad,
        mixer_parts[0],
        mixer_parts[1],
        mixer_parts[2],
        mixer_parts[3],
        mixer_parts[4],
        out_gain_total,
        ffn_parts[2],
        ffn_parts[0],
        ffn_parts[1],
        loss_value,
    )


def solution(mesh):
    in_specs = (
        P(("dp", "fsdp"), None),
        P(("dp", "fsdp"), None),
        P(("dp", "fsdp"), None),
        P(("dp", "fsdp")),
        P(("dp", "fsdp")),
        P(("dp", "fsdp"), None),
        P(("dp", "fsdp"), None),
        P(("dp", "fsdp"), None),
        P(None, ("dp", "fsdp")),
        P(("dp", "fsdp"), None),
        P(("dp", "fsdp")),
        P(),
        P(("dp", "fsdp")),
        P(("dp", "fsdp"), None),
        P(("dp", "fsdp"), None),
    )
    out_specs = (
        P(("dp", "fsdp"), None),
        P(("dp", "fsdp"), None),
        P(("dp", "fsdp"), None),
        P(("dp", "fsdp"), None),
        P(None, ("dp", "fsdp")),
        P(("dp", "fsdp"), None),
        P(("dp", "fsdp")),
        P(),
        P(("dp", "fsdp")),
        P(("dp", "fsdp"), None),
        P(("dp", "fsdp"), None),
        P(),
    )
    return jax.shard_map(local, mesh=mesh, in_specs=in_specs, out_specs=out_specs, check_vma=False)
```

profile of v0, /device:TPU:0, one launch (start us, length us, event | category | flops | bytes accessed | tf_op | source)
XLA Modules:
  0.0 1917.2 jit_solution(1307186365684419281)
XLA Ops:
  44.0 43.6 %psum.21 = f32[]{:T(128)} all-reduce(f32[]{:T(128)} %convert_reduce_fusion.2), channel_id=1, replica_groups=mesh['dp'=4,'fsdp'=8] {'dp','fsdp'}, use_global_device_ids=true, to_apply=%region_23.25 | all-reduce | flops 1 | bytes 8 | tf_op jit(solution)/shard_map/psum | solution.py:163
  90.0 39.0 %all-reduce.47 = (bf16[1024]{0:T(1024)(128)(2,1)S(1)}, bf16[1024]{0:T(1024)(128)(2,1)S(1)}) all-reduce(bf16[1024]{0:T(1024)(128)(2,1)S(1)} %dynamic-update-slice, bf16[1024]{0:T(1024)(128)(2,1)S(1)} %dynamic-update-slice.1), channel_id=1, replica_groups=mesh['dp'=4,'fsdp'=8] {'dp','fsdp'}, use_global_device_ids=true, to_apply=%add.42 | all-reduce | flops 2048 | bytes 8192
  131.9 40.9 %all-gather = bf16[32,96,4]{1,2,0:T(4,128)(2,1)S(1)} all-gather(bf16[1,96,4]{1,2,0:T(4,128)(2,1)S(1)} %bitcast.1049), channel_id=1, replica_groups=mesh['dp'=4,'fsdp'=8] {'dp','fsdp'}, dimensions={0}, use_global_device_ids=true | all-gather | bytes 25344 | tf_op jit(solution)/shard_map/all_gather | solution.py:209
  176.6 46.3 %all-gather.1 = bf16[32,32,8]{1,2,0:T(8,128)(2,1)S(1)} all-gather(bf16[1,32,8]{1,2,0:T(8,128)(2,1)S(1)} %bitcast.1048), channel_id=1, replica_groups=mesh['dp'=4,'fsdp'=8] {'dp','fsdp'}, dimensions={0}, use_global_device_ids=true | all-gather | bytes 16896 | tf_op jit(solution)/shard_map/all_gather | solution.py:208
  241.2 17.4 all-to-all-done.1
  301.9 119.1 %while.142 = (s32[]{:T(128)}, f32[8,128,128]{2,1,0:T(8,128)S(1)}, f32[2,8,64,128]{3,2,1,0:T(8,128)}, f32[2,1,64,64]{3,2,1,0:T(8,128)S(1)}, f32[2,8,64,1]{2,1,3,0...) while((s32[]{:T(128)}, f32[8,128,128]{2,1,0:T(8,128)S(1)}, ...), condition=%wide.region_8.10_spmd.clone, body=%wide.region_7.9_spmd.clone.sunk | while | flops 555668032 | bytes 35384152 | solution.py:102
  309.6 40.7 %custom-call.36 = f32[8,1,64,64]{2,3,1,0:T(8,128)} custom-call(f32[8,1,64,64]{3,2,1,0:T(8,128)} %add_bitcast_fusion.4), custom_call_target="InvertDiagBlocksLowerTriangular" | custom-call | tf_op jit(solution)/shard_map/jvp()/while/body/eval_jaxpr/jit(_solve_triangular)/vmap()/triangular_solve | solution.py:70
  369.1 40.7 %custom-call.36 = f32[8,1,64,64]{2,3,1,0:T(8,128)} custom-call(f32[8,1,64,64]{3,2,1,0:T(8,128)} %add_bitcast_fusion.4), custom_call_target="InvertDiagBlocksLowerTriangular" | custom-call | tf_op jit(solution)/shard_map/jvp()/while/body/eval_jaxpr/jit(_solve_triangular)/vmap()/triangular_solve | solution.py:70
  441.7 131.8 %while.143 = (s32[]{:T(128)}, f32[8,128,128]{2,1,0:T(8,128)S(1)}, f32[2,8,64,128]{3,2,1,0:T(8,128)}, f32[2,1,64,64]{3,2,1,0:T(8,128)}, f32[2,8,64,1]{2,1,3,0:T(8...) while((s32[]{:T(128)}, f32[8,128,128]{2,1,0:T(8,128)S(1)}, ...), condition=%wide.region_17.19_spmd.clone, body=%wide.region_16.18_spmd.clone.sunk | while | flops 555668032 | bytes 50327408 | solution.py:102
  464.1 40.7 %custom-call.37 = f32[8,1,64,64]{2,3,1,0:T(8,128)} custom-call(f32[8,1,64,64]{3,2,1,0:T(8,128)} %add_bitcast_fusion.5), custom_call_target="InvertDiagBlocksLowerTriangular" | custom-call | tf_op jit(solution)/shard_map/jvp()/while/body/eval_jaxpr/jit(_solve_triangular)/vmap()/triangular_solve | solution.py:70
  523.9 40.7 %custom-call.37 = f32[8,1,64,64]{2,3,1,0:T(8,128)} custom-call(f32[8,1,64,64]{3,2,1,0:T(8,128)} %add_bitcast_fusion.5), custom_call_target="InvertDiagBlocksLowerTriangular" | custom-call | tf_op jit(solution)/shard_map/jvp()/while/body/eval_jaxpr/jit(_solve_triangular)/vmap()/triangular_solve | solution.py:70
  638.0 134.1 %while.145 = (s32[]{:T(128)}, f32[8,128,128]{2,1,0:T(8,128)S(1)}, f32[2,8,64,128]{3,1,2,0:T(8,128)}, f32[2,8,64,128]{3,1,2,0:T(8,128)}, f32[2,8,64,128]{3,2,1,0:...) while((s32[]{:T(128)}, f32[8,128,128]{2,1,0:T(8,128)S(1)}, ...), condition=%wide.region_40.43_spmd.clone, body=%wide.region_37.42_spmd.clone.sunk | while | flops 1135111680 | bytes 54217612 | solution.py:102
  656.8 40.7 %custom-call.39 = f32[8,1,64,64]{2,3,1,0:T(8,128)} custom-call(f32[8,1,64,64]{3,2,1,0:T(8,128)} %fusion.635), custom_call_target="InvertDiagBlocksLowerTriangular" | custom-call | tf_op jit(solution)/shard_map/transpose(jvp())/while/body/eval_jaxpr/jit(_solve_triangular)/vmap()/triangular_solve | solution.py:70
  723.8 40.7 %custom-call.39 = f32[8,1,64,64]{2,3,1,0:T(8,128)} custom-call(f32[8,1,64,64]{3,2,1,0:T(8,128)} %fusion.635), custom_call_target="InvertDiagBlocksLowerTriangular" | custom-call | tf_op jit(solution)/shard_map/transpose(jvp())/while/body/eval_jaxpr/jit(_solve_triangular)/vmap()/triangular_solve | solution.py:70
  780.1 136.0 %while.144 = (s32[]{:T(128)}, f32[8,128,128]{2,1,0:T(8,128)S(1)}, f32[2,8,64,128]{3,1,2,0:T(8,128)}, f32[2,8,64,128]{3,1,2,0:T(8,128)}, f32[2,8,64,128]{3,2,1,0:...) while((s32[]{:T(128)}, f32[8,128,128]{2,1,0:T(8,128)S(1)}, ...), condition=%wide.region_31.34_spmd.clone, body=%wide.region_28.33_spmd.clone.sunk | while | flops 1135111680 | bytes 40585832 | solution.py:102
  799.7 40.7 %custom-call.38 = f32[8,1,64,64]{2,3,1,0:T(8,128)} custom-call(f32[8,1,64,64]{3,2,1,0:T(8,128)} %fusion.596), custom_call_target="InvertDiagBlocksLowerTriangular" | custom-call | tf_op jit(solution)/shard_map/transpose(jvp())/while/body/eval_jaxpr/jit(_solve_triangular)/vmap()/triangular_solve | solution.py:70
  867.4 40.7 %custom-call.38 = f32[8,1,64,64]{2,3,1,0:T(8,128)} custom-call(f32[8,1,64,64]{3,2,1,0:T(8,128)} %fusion.596), custom_call_target="InvertDiagBlocksLowerTriangular" | custom-call | tf_op jit(solution)/shard_map/transpose(jvp())/while/body/eval_jaxpr/jit(_solve_triangular)/vmap()/triangular_solve | solution.py:70
  973.4 9.7 fusion.268
  1014.7 40.8 %all-reduce.46 = (f32[1024]{0:T(1024)S(1)}, f32[128]{0:T(128)}, f32[1024]{0:T(1024)S(1)}, f32[]{:T(128)}) all-reduce(f32[1024]{0:T(1024)S(1)} %add.532, f32[128]{0:T(128)S(1)} %add.533, f32[1024]{0:T(1024)S(1)} %add.534, f32[]{:T(128)S(6)} %add.535), channel_id=6, replica_groups=mesh['dp'=4,'fsdp'=8] {'dp','fsdp'}, use_global_device_ids=true, to_apply=%region_59.62.clone | all-reduce | flops 2177 | bytes 17416
  1058.8 124.1 %reduce-scatter.19.cloned.1.call-done = f32[32,8]{1,0:T(8,128)} async-done(((f32[1024,8]{1,0:T(8,128)}), f32[32,8]{1,0:T(8,128)}) %reduce-scatter.19.cloned.1.call-update) | async-done | bytes 1040
  1189.5 133.2 %reduce-scatter.13.cloned.1.call-done = f32[32,1024]{1,0:T(8,128)} async-done(((f32[1024,1024]{1,0:T(8,128)}), f32[32,1024]{1,0:T(8,128)}) %reduce-scatter.13.cloned.1.call-update) | async-done | bytes 131088 | tf_op jit(solution)/shard_map/reduce_scatter | solution.py:309
  1322.7 153.8 %reduce-scatter.17.cloned.1.call-done = f32[88,1024]{1,0:T(8,128)} async-done(((f32[2816,1024]{1,0:T(8,128)}), f32[88,1024]{1,0:T(8,128)}) %reduce-scatter.17.cloned.1.call-update) | async-done | bytes 360464 | tf_op jit(solution)/shard_map/reduce_scatter | solution.py:286
  1476.6 181.7 %reduce-scatter.11.cloned.1.call-done = f32[32,4096]{1,0:T(8,128)} async-done(((f32[1024,4096]{1,0:T(8,128)}), f32[32,4096]{1,0:T(8,128)}) %reduce-scatter.11.cloned.1.call-update) | async-done | bytes 524304 | tf_op jit(solution)/shard_map/reduce_scatter | solution.py:296
  1658.3 250.7 %reduce-scatter.15.cloned.1.call-done = f32[32,5632]{1,0:T(8,128)} async-done(((f32[1024,5632]{1,0:T(8,128)}), f32[32,5632]{1,0:T(8,128)}) %reduce-scatter.15.cloned.1.call-update) | async-done | bytes 720912 | tf_op jit(solution)/shard_map/reduce_scatter | solution.py:280
  (1200 shorter events, 473.8 us)
Async XLA Ops:
  7.2 254.2 %all-gather.7.cloned.1.call-start = ((), (), s32[]{:S(2)}) async-start(), calls=%async_computation.13 | async-start | bytes 8650752 | tf_op jit(solution)/shard_map/all_gather | solution.py:207
  7.9 572.3 %all-gather.9.cloned.1.call-start = ((), (), s32[]{:S(2)}) async-start(), calls=%async_computation.14 | async-start | bytes 2162688 | tf_op jit(solution)/shard_map/all_gather | solution.py:210
  8.7 575.5 %all-gather.11.cloned.1.call-start = ((), (), s32[]{:S(2)}) async-start(), calls=%async_computation.15 | async-start | bytes 11894784 | tf_op jit(solution)/shard_map/all_gather | solution.py:214
  15.9 14.4 all-to-all-start
  30.3 9.6 all-to-all-start.4
  34.9 52.7 %copy-start.16 = (bf16[256,1024]{1,0:T(8,128)(2,1)S(1)}, bf16[256,1024]{1,0:T(8,128)(2,1)}, u32[]{:S(2)}) copy-start(bf16[256,1024]{1,0:T(8,128)(2,1)} %param.30) | copy-start | bytes 1572868
  40.0 134.0 %all-to-all-start.5 = ((bf16[32,8,1024]{2,1,0:T(8,128)(2,1)}), bf16[32,8,1024]{2,1,0:T(8,128)(2,1)}, u32[]{:S(2)}, u32[]{:S(2)}) async-start(bf16[32,8,1024]{2,1,0:T(8,128)(2,1)} %bitcast.38), calls=%async_computation.5 | async-start | bytes 1048576 | tf_op jit(solution)/shard_map/all_to_all | solution.py:180
  43.3 554.4 %all-gather.13.cloned.1.call-start = ((), (), s32[]{:S(2)}) async-start(), calls=%async_computation.16 | async-start | bytes 5947392 | tf_op jit(solution)/shard_map/all_gather | solution.py:215
  128.9 131.7 %copy-start.190 = (f32[1024]{0:T(1024)}, f32[1024]{0:T(1024)S(1)}, u32[]{:S(2)}) copy-start(f32[1024]{0:T(1024)S(1)} %convert_element_type.260) | copy-start | bytes 12292
  129.0 47.6 %copy-start.231 = (bf16[32,8]{0,1:T(8,128)(2,1)S(1)}, bf16[32,8]{0,1:T(8,128)(2,1)}, u32[]{:S(2)}) copy-start(bf16[32,8]{0,1:T(8,128)(2,1)} %param.36) | copy-start | bytes 1540
  131.0 105.9 %copy-start.210 = (f32[128]{0:T(128)}, f32[128]{0:T(128)S(1)}, u32[]{:S(2)}) copy-start(f32[128]{0:T(128)S(1)} %convert_element_type.267) | copy-start | bytes 1540
  173.9 53.8 %all-to-all-start.3 = ((bf16[32,8,1024]{2,1,0:T(8,128)(2,1)}), bf16[32,8,1024]{2,1,0:T(8,128)(2,1)S(1)}, u32[]{:S(2)}, u32[]{:S(2)}) async-start(bf16[32,8,1024]{2,1,0:T(8,128)(2,1)} %bitcast.35), calls=%async_computation.3 | async-start | bytes 1048576 | tf_op jit(solution)/shard_map/all_to_all | solution.py:179
  227.7 30.8 %all-to-all-start.1 = ((bf16[32,8,1024]{2,1,0:T(8,128)(2,1)}), bf16[32,8,1024]{2,1,0:T(8,128)(2,1)S(1)}, u32[]{:S(2)}, u32[]{:S(2)}) async-start(bf16[32,8,1024]{2,1,0:T(8,128)(2,1)} %bitcast.2), calls=%async_computation.1 | async-start | bytes 1048576 | tf_op jit(solution)/shard_map/all_to_all | solution.py:178
  230.3 827.0 %reduce-scatter.21.cloned.1.call-start = ((), (), s32[]{:S(2)}) async-start(), calls=%async_computation.22 | async-start | bytes 1622016
  638.0 135.8 %copy-start.199 = (f32[128,8]{0,1:T(8,128)S(1)}, f32[128,8]{0,1:T(8,128)}, u32[]{:S(2)}) copy-start(f32[128,8]{0,1:T(8,128)} %copy-done.198) | copy-start | bytes 12292
  780.1 137.6 %copy-start.197 = (f32[128,8]{0,1:T(8,128)S(1)}, f32[128,8]{0,1:T(8,128)}, u32[]{:S(2)}) copy-start(f32[128,8]{0,1:T(8,128)} %copy-done.196) | copy-start | bytes 12292
  947.2 235.7 %reduce-scatter.19.cloned.1.call-start = ((), (), s32[]{:S(2)}) async-start(), calls=%async_computation.21 | async-start | bytes 540672
  948.5 374.3 %reduce-scatter.13.cloned.1.call-start = ((), (), s32[]{:S(2)}) async-start(), calls=%async_computation.18 | async-start | bytes 4325376 | tf_op jit(solution)/shard_map/reduce_scatter | solution.py:309
  951.3 525.3 %reduce-scatter.17.cloned.1.call-start = ((), (), s32[]{:S(2)}) async-start(), calls=%async_computation.20 | async-start | bytes 11894784 | tf_op jit(solution)/shard_map/reduce_scatter | solution.py:286
  958.6 699.7 %reduce-scatter.11.cloned.1.call-start = ((), (), s32[]{:S(2)}) async-start(), calls=%async_computation.17 | async-start | bytes 17301504 | tf_op jit(solution)/shard_map/reduce_scatter | solution.py:296
  971.5 937.5 %reduce-scatter.15.cloned.1.call-start = ((), (), s32[]{:S(2)}) async-start(), calls=%async_computation.19 | async-start | bytes 23789568 | tf_op jit(solution)/shard_map/reduce_scatter | solution.py:280
  986.1 23.2 %all-to-all-start.2 = ((bf16[32,8,1024]{2,1,0:T(8,128)(2,1)}), bf16[32,8,1024]{2,1,0:T(8,128)(2,1)S(1)}, u32[]{:S(2)}, u32[]{:S(2)}) async-start(bf16[32,8,1024]{2,1,0:T(8,128)(2,1)} %bitcast.33), calls=%async_computation.2 | async-start | bytes 1048576 | tf_op jit(solution)/shard_map/all_to_all | solution.py:324
  1009.4 899.7 %copy-start.1 = (bf16[256,1024]{1,0:T(8,128)(2,1)S(1)}, bf16[256,1024]{1,0:T(8,128)(2,1)}, u32[]{:S(2)}) copy-start(bf16[256,1024]{1,0:T(8,128)(2,1)} %param.31) | copy-start | bytes 1572868
  1009.4 177.6 %all-to-all-start.6 = ((bf16[32,8,1024]{2,1,0:T(8,128)(2,1)}), bf16[32,8,1024]{2,1,0:T(8,128)(2,1)S(1)}, u32[]{:S(2)}, u32[]{:S(2)}) async-start(bf16[32,8,1024]{2,1,0:T(8,128)(2,1)} %bitcast.54), calls=%async_computation.6 | async-start | bytes 1048576 | tf_op jit(solution)/shard_map/all_to_all | solution.py:325
  (319 other events, 1460.8 us)
Sparse Core Ops, SparseCore 0:
  10.9 88.5 all-gather.6
  102.3 55.2 all-gather.8
  160.5 102.5 all-gather.10
  265.8 66.3 all-gather.12
  947.3 99.8 reduce-scatter.20
  1049.9 133.0 reduce-scatter.18
  1185.9 136.8 reduce-scatter.12
  1325.7 150.7 reduce-scatter.16
  1479.6 178.6 reduce-scatter.10
  1661.1 247.8 reduce-scatter.14
where the time goes:
time: 1930 us; the launch traced here: 1920 us
  waiting for transfers between devices  876 us (45%)
  other arithmetic  419 us (22%)
  blocking collectives  211 us (11%)
  matrix products  200 us (10%)
  local copies, waits for them, and re-layouts  149 us (8%)
  starting transfers between devices  26.1 us (1%)
  between operations  21.3 us (1%)
    another operation x40, other arithmetic, advance(): jax.scipy.linalg.solve_triangular(system, right_side, lower=True, unit_di...  336 us
    reduce_scatter x1, waiting for transfers between devices, local(): lax.psum_scatter(over_rows(jnp.concatenate(kept_ffn_in), jnp.concatenate(...  251 us
    reduce_scatter x1, waiting for transfers between devices, local(): lax.psum_scatter(over_rows(all_in, jnp.concatenate(kept_proj)), ('dp', 'f...  182 us
    reduce_scatter x1, waiting for transfers between devices, local(): lax.psum_scatter(over_rows(jnp.concatenate(kept_hid), jnp.concatenate(kep...  154 us
    reduce_scatter x1, waiting for transfers between devices, local(): lax.psum_scatter(over_rows(jnp.concatenate(kept_on), jnp.concatenate(kept...  133 us
    unnamed x12, waiting for transfers between devices  126 us
    unnamed x2, blocking collectives  79.8 us
    all_gather x1, blocking collectives, local(): lax.all_gather(w_beta, ('dp', 'fsdp'), axis=0, tiled=True)  46.3 us
  transfers between devices with their start and end apart: 17, of which 9 were waited for; matrix products, arithmetic and copies ran while one was open for 21% of the time, Pallas kernels for 0%

commit v1 on v0

v1 whole, which is shorter than its diff:
```python
import functools

import jax
import jax.numpy as jnp
from jax import lax
from jax.experimental import pallas as pl
from jax.experimental.pallas import tpu as pltpu
from jax.sharding import PartitionSpec as P

D = 1024
HEADS = 8
HEAD_DIM = 128
FF = 2816
CONV = 4
AXES = ("dp", "fsdp")
F32 = jnp.float32
BF16 = jnp.bfloat16
PAIR = 2


def mm(left, right, lc, rc):
    return lax.dot_general(
        left,
        right,
        (((lc,), (rc,)), ((), ())),
        precision=lax.Precision.HIGHEST,
        preferred_element_type=F32,
    )


def sigmoid(v):
    return 1.0 / (1.0 + jnp.exp(-v))


def iota2(shape, axis):
    return lax.broadcasted_iota(jnp.int32, shape, axis)


def unit_lower_inverses(mats, size):
    row, col = iota2((size, size), 0), iota2((size, size), 1)
    eye = (row == col).astype(F32)
    inverses = None
    width = 1
    while width < size:
        corner = ((row // (2 * width)) == (col // (2 * width))) & (
            (row // width) == (col // width) + 1
        )
        edges = [jnp.where(corner, m, 0.0) for m in mats]
        if inverses is None:
            inverses = [eye - e for e in edges]
        else:
            right = [mm(e, x, 1, 0) for e, x in zip(edges, inverses)]
            inverses = [x - mm(x, r, 1, 0) for x, r in zip(inverses, right)]
        width *= 2
    return inverses


def conv_parts(src, taps, masks):
    rolled = [src]
    total = src * taps[CONV - 1 : CONV, :]
    for s in range(1, CONV):
        moved = pltpu.roll(src, s, 0) * masks[s]
        rolled.append(moved)
        total = total + moved * taps[CONV - 1 - s : CONV - s, :]
    return total, rolled


def l2_norm(c):
    inv = lax.rsqrt(jnp.sum(c * c, axis=-1, keepdims=True) + 1e-06)
    return c * inv, inv


def mixer_fwd_kernel(
    blocks, rows_mb,
    pq, pk, pv, pg, beta, tq, tk, tv, gain, mask, segc, segr,
    on_ref, o_ref, ainv_ref, u_ref, p_ref, l_ref,
):
    step = pl.program_id(0)
    masks = [None] + [mask[:, s : s + 1] for s in range(1, CONV)]
    cs = []
    for src, taps in ((pq, tq), (pk, tk), (pv, tv)):
        pre, _ = conv_parts(src[...], taps[...], masks)
        cs.append(pre * sigmoid(pre))
    cq, ck, cv = cs
    strengths = sigmoid(beta[...])
    lane = iota2(strengths.shape, 1)
    gate = pg[...]
    gate = gate * sigmoid(gate)
    row, col = iota2((rows_mb, rows_mb), 0), iota2((rows_mb, rows_mb), 1)
    systems = [(h, b) for h in range(PAIR) for b in range(blocks)]
    qs, ks, vs, bs, sames, lows = [], [], [], [], [], []
    for h, b in systems:
        rs = slice(b * rows_mb, (b + 1) * rows_mb)
        hs = slice(h * HEAD_DIM, (h + 1) * HEAD_DIM)
        q, _ = l2_norm(cq[rs, hs])
        k, _ = l2_norm(ck[rs, hs])
        qs.append(q * HEAD_DIM ** (-0.5))
        ks.append(k)
        vs.append(cv[rs, hs])
        bs.append(
            jnp.sum(jnp.where(lane == step * PAIR + h, strengths, 0.0), axis=1, keepdims=True)[rs]
        )
        sames.append(segc[rs, :] == segr[:, rs])
    for i in range(len(systems)):
        lows.append(jnp.where(sames[i] & (row > col), mm(ks[i], ks[i], 1, 1), 0.0))
    inverses = unit_lower_inverses([l * b for l, b in zip(lows, bs)], rows_mb)
    us = [mm(a, v * b, 1, 0) for a, v, b in zip(inverses, vs, bs)]
    ps = [
        jnp.where(same & (row >= col), mm(q, k, 1, 1), 0.0)
        for q, k, same in zip(qs, ks, sames)
    ]
    os = [mm(p, u, 1, 0) for p, u in zip(ps, us)]
    for i, (h, b) in enumerate(systems):
        rs = slice(b * rows_mb, (b + 1) * rows_mb)
        hs = slice(h * HEAD_DIM, (h + 1) * HEAD_DIM)
        o = os[i]
        inv = lax.rsqrt(jnp.mean(o * o, axis=-1, keepdims=True) + 1e-05)
        on_ref[rs, hs] = (o * inv * gain[...] * gate[rs, hs]).astype(BF16)
        o_ref[rs, hs] = o
        ainv_ref[h, b] = inverses[i]
        u_ref[h, b] = us[i]
        p_ref[h, b] = ps[i]
        l_ref[h, b] = lows[i]


def mixer_bwd_kernel(
    blocks, rows_mb,
    pq, pk, pv, pg, beta, tq, tk, tv, gain, mask, segc, segr,
    don_ref, o_ref, ainv_ref, u_ref, p_ref, l_ref,
    dq_ref, dk_ref, dv_ref, dg_ref, dbeta_ref, dtq, dtk, dtv, dgain_ref,
):
    step = pl.program_id(0)
    rows = blocks * rows_mb
    masks = [None] + [mask[:, s : s + 1] for s in range(1, CONV)]
    pres, rolls, cs, sig = [], [], [], []
    for src, taps in ((pq, tq), (pk, tk), (pv, tv)):
        pre, rolled = conv_parts(src[...], taps[...], masks)
        s = sigmoid(pre)
        pres.append(pre)
        rolls.append(rolled)
        sig.append(s)
        cs.append(pre * s)
    cq, ck, cv = cs
    strengths = sigmoid(beta[...])
    lane = iota2(strengths.shape, 1)
    row, col = iota2((rows_mb, rows_mb), 0), iota2((rows_mb, rows_mb), 1)
    gates = pg[...]
    gsig = sigmoid(gates)
    gate = gates * gsig
    dgate = gsig * (1.0 + gates * (1.0 - gsig))
    systems = [(h, b) for h in range(PAIR) for b in range(blocks)]
    part = []
    dgain = jnp.zeros((1, HEAD_DIM), F32)
    for h, b in systems:
        rs = slice(b * rows_mb, (b + 1) * rows_mb)
        hs = slice(h * HEAD_DIM, (h + 1) * HEAD_DIM)
        k, ik = l2_norm(ck[rs, hs])
        qn, iq = l2_norm(cq[rs, hs])
        v = cv[rs, hs]
        bb = jnp.sum(jnp.where(lane == step * PAIR + h, strengths, 0.0), axis=1, keepdims=True)[rs]
        same = segc[rs, :] == segr[:, rs]
        o = o_ref[rs, hs]
        don = don_ref[rs, hs]
        inv = lax.rsqrt(jnp.mean(o * o, axis=-1, keepdims=True) + 1e-05)
        no = o * inv
        scaled = don * gain[...]
        dg_ref[rs, hs] = (scaled * no * dgate[rs, hs]).astype(BF16)
        dgain = dgain + jnp.sum(don * no * gate[rs, hs], axis=0, keepdims=True)
        dno = scaled * gate[rs, hs]
        do = inv * (dno - no * jnp.mean(no * dno, axis=-1, keepdims=True))
        part.append([q_ for q_ in (qn, iq, k, ik, v, bb, same, do)])
    dus = [mm(p_ref[h, b], part[i][7], 0, 0) for i, (h, b) in enumerate(systems)]
    dps = [
        jnp.where(part[i][6] & (row >= col), mm(part[i][7], u_ref[h, b], 1, 1), 0.0)
        for i, (h, b) in enumerate(systems)
    ]
    drs = [mm(ainv_ref[h, b], dus[i], 0, 0) for i, (h, b) in enumerate(systems)]
    scale = HEAD_DIM ** (-0.5)
    dqs = [mm(dps[i], part[i][2], 1, 0) * scale for i in range(len(systems))]
    das = [mm(drs[i], u_ref[h, b], 1, 1) for i, (h, b) in enumerate(systems)]
    dks = [mm(dps[i], part[i][0] * scale, 0, 0) for i in range(len(systems))]
    dgs = []
    for i in range(len(systems)):
        g = jnp.where(part[i][6] & (row > col), das[i] * (-part[i][5]), 0.0)
        dgs.append(g + g.T)
    dks = [dks[i] + mm(dgs[i], part[i][2], 1, 0) for i in range(len(systems))]
    dbeta = jnp.zeros(strengths.shape, F32)
    dcs = [[], [], []]
    for i, (h, b) in enumerate(systems):
        qn, iq, k, ik, v, bb, same, do = part[i]
        dv = drs[i] * bb
        db = jnp.sum(drs[i] * v - das[i] * l_ref[h, b], axis=-1, keepdims=True)
        dbp = db * bb * (1.0 - bb)
        pieces = [dbp if b == c else jnp.zeros((rows_mb, 1), F32) for c in range(blocks)]
        column = jnp.concatenate(pieces, axis=0) if blocks > 1 else dbp
        dbeta = dbeta + jnp.where(lane == step * PAIR + h, column, 0.0)
        dcs[0].append(iq * (dqs[i] - qn * jnp.sum(qn * dqs[i], axis=-1, keepdims=True)))
        dcs[1].append(ik * (dks[i] - k * jnp.sum(k * dks[i], axis=-1, keepdims=True)))
        dcs[2].append(dv)
    for j, (out, dtap, taps) in enumerate(((dq_ref, dtq, tq), (dk_ref, dtk, tk), (dv_ref, dtv, tv))):
        whole = jnp.concatenate(
            [
                jnp.concatenate([dcs[j][h * blocks + b] for b in range(blocks)], axis=0)
                for h in range(PAIR)
            ],
            axis=1,
        )
        dpre = whole * (sig[j] * (1.0 + pres[j] * (1.0 - sig[j])))
        tap = taps[...]
        grad = dpre * tap[CONV - 1 : CONV, :]
        dtap[CONV - 1 : CONV, :] = jnp.sum(dpre * rolls[j][0], axis=0, keepdims=True)
        for s in range(1, CONV):
            dtap[CONV - 1 - s : CONV - s, :] = jnp.sum(dpre * rolls[j][s], axis=0, keepdims=True)
            grad = grad + pltpu.roll(dpre * masks[s], rows - s, 0) * tap[CONV - 1 - s : CONV - s, :]
        out[...] = grad.astype(BF16)

    @pl.when(step == 0)
    def _():
        dbeta_ref[...] = jnp.zeros_like(dbeta_ref)
        dgain_ref[...] = jnp.zeros_like(dgain_ref)

    dbeta_ref[...] += dbeta
    dgain_ref[...] += dgain


def mixer_specs(rows, blocks, rows_mb):
    width = PAIR * HEAD_DIM
    per = D // width
    col = lambda k: pl.BlockSpec((rows, width), lambda i, k=k: (0, k * per + i))
    tap = lambda k: pl.BlockSpec((CONV, width), lambda i, k=k: (0, k * per + i))
    full = lambda shape: pl.BlockSpec(shape, lambda i: (0,) * len(shape))
    ins = [col(0), col(1), col(2), col(3), full((rows, HEADS)), tap(0), tap(1), tap(2),
           full((1, HEAD_DIM)), full((rows, 8)), full((rows, 1)), full((1, rows))]
    mat = pl.BlockSpec((PAIR, blocks, rows_mb, rows_mb), lambda i: (i, 0, 0, 0))
    one = pl.BlockSpec((rows, width), lambda i: (0, i))
    otap = pl.BlockSpec((CONV, width), lambda i: (0, i))
    return ins, mat, one, otap, full


def mixer_forward(proj, beta_pre, taps, gain, mask, segc, segr, blocks):
    rows = proj.shape[0]
    rows_mb = rows // blocks
    ins, mat, one, _, _ = mixer_specs(rows, blocks, rows_mb)
    square = jax.ShapeDtypeStruct((HEADS, blocks, rows_mb, rows_mb), F32)
    return pl.pallas_call(
        functools.partial(mixer_fwd_kernel, blocks, rows_mb),
        grid=(HEADS // PAIR,),
        in_specs=ins,
        out_specs=[one, one, mat, mat, mat, mat],
        out_shape=[
            jax.ShapeDtypeStruct((rows, D), BF16),
            jax.ShapeDtypeStruct((rows, D), F32),
            square, square, square, square,
        ],
        compiler_params=pltpu.CompilerParams(vmem_limit_bytes=48 << 20),
        name="mixer_fwd",
    )(proj, proj, proj, proj, beta_pre, taps, taps, taps, gain, mask, segc, segr)


def mixer_backward(proj, beta_pre, taps, gain, mask, segc, segr, don, saved, blocks):
    rows = proj.shape[0]
    rows_mb = rows // blocks
    ins, mat, one, otap, full = mixer_specs(rows, blocks, rows_mb)
    tapshape = jax.ShapeDtypeStruct((CONV, D), F32)
    wide = jax.ShapeDtypeStruct((rows, D), BF16)
    return pl.pallas_call(
        functools.partial(mixer_bwd_kernel, blocks, rows_mb),
        grid=(HEADS // PAIR,),
        in_specs=ins + [one, one, mat, mat, mat, mat],
        out_specs=[one, one, one, one, full((rows, HEADS)), otap, otap, otap, full((1, HEAD_DIM))],
        out_shape=[
            wide, wide, wide, wide,
            jax.ShapeDtypeStruct((rows, HEADS), F32),
            tapshape, tapshape, tapshape,
            jax.ShapeDtypeStruct((1, HEAD_DIM), F32),
        ],
        compiler_params=pltpu.CompilerParams(vmem_limit_bytes=48 << 20),
        name="mixer_bwd",
    )(proj, proj, proj, proj, beta_pre, taps, taps, taps, gain, mask, segc, segr, don, *saved)


def nt(left, right):
    return lax.dot_general(left, right, (((1,), (1,)), ((), ())), preferred_element_type=F32)


def tn(left, right, dtype=F32):
    return lax.dot_general(left, right, (((0,), (0,)), ((), ())), preferred_element_type=dtype)


def nn(left, right):
    return jnp.dot(left, right, preferred_element_type=F32)


def rms(v):
    inv = lax.rsqrt(jnp.mean(v * v, axis=-1, keepdims=True) + 1e-05)
    return v * inv, inv


def rms_back(normed, inv, dn):
    return inv * (dn - normed * jnp.mean(normed * dn, axis=-1, keepdims=True))


def local(
    tokens, cotangent, teacher, valid_mask, deal_rows, lengths, w_in, w_beta, conv_kernel, w_out,
    norm_gain, out_gain, ffn_gain, w_gu, w_down,
):
    shards = lax.axis_size(AXES)
    rows = tokens.shape[0]
    share = rows // shards
    blocks = lengths.shape[0]
    rows_mb = rows // blocks
    small = w_beta.shape[0] * HEADS + CONV * conv_kernel.shape[1] + 2 * norm_gain.shape[0]

    target = deal_rows // rows
    spot = deal_rows % rows
    ahead = (target[None, :] == target[:, None]) & (
        jnp.arange(rows)[None, :] < jnp.arange(rows)[:, None]
    )
    slot = target * share + jnp.sum(ahead.astype(jnp.int32), axis=1)
    sort_t = (slot[:, None] == jnp.arange(rows)[None, :]).astype(BF16)
    sort = (slot[None, :] == jnp.arange(rows)[:, None]).astype(BF16)
    count_own = jnp.sum(valid_mask.astype(F32))
    lane = jnp.arange(128)[None, :]
    notes = jnp.where(
        lane == 0,
        valid_mask.astype(F32)[:, None],
        jnp.where(lane == 1, spot.astype(F32)[:, None], jnp.where(lane == 2, count_own, 0.0)),
    ).astype(BF16)
    packed = jnp.concatenate(
        [conv_kernel.reshape(-1), w_beta.reshape(-1), norm_gain, ffn_gain,
         jnp.zeros((share * 128 - small,), BF16)]
    ).reshape(1, share, 128)
    sorted_rows = nn(sort, jnp.concatenate([tokens, cotangent, teacher, notes], axis=1)).astype(BF16)
    message = jnp.concatenate(
        [sorted_rows.reshape(shards, share, -1), jnp.broadcast_to(packed, (shards, share, 128))],
        axis=2,
    )
    arrived = lax.all_to_all(message, AXES, split_axis=0, concat_axis=0, tiled=True)

    win = lax.all_gather(w_in, AXES, axis=0, tiled=True)
    wout = lax.all_gather(w_out, AXES, axis=0, tiled=True)
    wgu = lax.all_gather(w_gu, AXES, axis=0, tiled=True)
    wdown = lax.all_gather(w_down, AXES, axis=0, tiled=True)

    flat = arrived.reshape(rows, -1)
    info = flat[:, 3 * D : 3 * D + 128].astype(F32)
    place = info[:, 1].astype(jnp.int32)
    counted = jnp.sum(arrived[:, 0, 3 * D + 2].astype(F32))
    extra = arrived[:, :, 3 * D + 128 :].reshape(shards, share * 128)
    a, b, c = CONV * conv_kernel.shape[1], w_beta.shape[0] * HEADS, norm_gain.shape[0]
    taps = extra[:, :a].reshape(shards, CONV, -1).swapaxes(0, 1).reshape(CONV, 3 * D).astype(F32)
    wbeta = extra[:, a : a + b].reshape(D, HEADS)
    gain_one = extra[:, a + b : a + b + c].reshape(D).astype(F32)
    gain_two = extra[:, a + b + c : a + b + 2 * c].reshape(D).astype(F32)
    deal = (place[None, :] == jnp.arange(rows)[:, None]).astype(BF16)
    deal_t = (place[:, None] == jnp.arange(rows)[None, :]).astype(BF16)
    dealt = nn(deal, flat[:, : 3 * D + 128])
    x = dealt[:, :D]
    g = dealt[:, D : 2 * D]
    t = dealt[:, 2 * D : 3 * D]
    m = dealt[:, 3 * D : 3 * D + 1]

    ends = jnp.cumsum(lengths, axis=1)
    within = jnp.arange(rows_mb, dtype=jnp.int32)
    seg = jnp.sum((within[None, :, None] >= ends[:, None, :]).astype(jnp.int32), axis=2)
    seg = (seg + (lengths.shape[1] + 1) * jnp.arange(blocks, dtype=jnp.int32)[:, None]).reshape(rows)
    position = jnp.arange(rows, dtype=jnp.int32)
    mask = jnp.stack(
        [jnp.ones((rows,), F32)]
        + [((position >= s) & (jnp.roll(seg, s) == seg)).astype(F32) for s in range(1, CONV)]
        + [jnp.zeros((rows,), F32)] * (8 - CONV),
        axis=1,
    )
    segc, segr = seg[:, None], seg[None, :]
    gain_out = out_gain.astype(F32)[None, :]

    nx, rx = rms(x)
    a1 = (nx * gain_one).astype(BF16)
    proj = nn(a1, win)
    beta_pre = nn(a1, wbeta)
    on, *saved = mixer_forward(proj, beta_pre, taps, gain_out, mask, segc, segr, blocks)
    resid = x + nn(on, wout)
    nr, rr = rms(resid)
    a2 = (nr * gain_two).astype(BF16)
    gu = nn(a2, wgu)
    gate, up = gu[:, :FF], gu[:, FF:]
    sg = sigmoid(gate)
    hid = (gate * sg * up).astype(BF16)
    y = resid + nn(hid, wdown)
    errors = y - t
    loss_part = jnp.sum(m * errors * errors)
    dy = g + (rows * shards / counted) * m * errors
    df = dy.astype(BF16)
    dhid = nt(df, wdown)
    dgu = jnp.concatenate(
        [dhid * up * (sg * (1.0 + gate * (1.0 - sg))), dhid * (gate * sg)], axis=1
    ).astype(BF16)
    da2 = nt(dgu, wgu)
    d_gain_two = jnp.sum(da2 * nr, axis=0)
    dresid = dy + rms_back(nr, rr, gain_two * da2)
    dz = dresid.astype(BF16)
    don = nt(dz, wout)
    dpq, dpk, dpv, dpg, dbeta, dtq, dtk, dtv, d_gain_out = mixer_backward(
        proj, beta_pre, taps, gain_out, mask, segc, segr, don, saved, blocks
    )
    dproj = jnp.concatenate([dpq, dpk, dpv, dpg], axis=1)
    dbeta = dbeta.astype(BF16)
    da1 = nt(dproj, win) + nt(dbeta, wbeta)
    d_gain_one = jnp.sum(da1 * nx, axis=0)
    dx = dresid + rms_back(nx, rx, gain_one * da1)

    def scatter(v):
        return lax.psum_scatter(v, AXES, scatter_dimension=0, tiled=True).astype(F32)

    g_gu = scatter(tn(a2, dgu).astype(BF16))
    g_down = scatter(tn(hid, df).astype(BF16))
    g_in = scatter(tn(a1, dproj).astype(BF16))
    g_out = scatter(tn(on, dz).astype(BF16))

    d_taps = jnp.concatenate([dtq, dtk, dtv], axis=1)
    d_wbeta = tn(a1, dbeta)
    tail = jnp.concatenate([d_gain_out.reshape(-1), loss_part.reshape(1)])
    extra = jnp.concatenate(
        [
            d_taps.reshape(CONV, shards, -1).swapaxes(0, 1).reshape(shards, a),
            d_wbeta.reshape(shards, b),
            d_gain_one.reshape(shards, c),
            d_gain_two.reshape(shards, c),
            jnp.broadcast_to(tail[None], (shards, tail.shape[0])),
        ],
        axis=1,
    )
    padded = -(-extra.shape[1] // 128) * 128
    extra = jnp.pad(extra, ((0, 0), (0, padded - extra.shape[1])))
    summed = jnp.sum(
        lax.all_to_all(
            extra.reshape(shards, padded // 128, 128), AXES, split_axis=0, concat_axis=0, tiled=True
        ),
        axis=0,
    ).reshape(-1)
    g_taps = summed[:a].reshape(CONV, -1)
    g_beta = summed[a : a + b].reshape(-1, HEADS)
    g_gain_one = summed[a + b : a + b + c]
    g_gain_two = summed[a + b + c : a + b + 2 * c]
    g_gain_out = summed[a + b + 2 * c : a + b + 2 * c + HEAD_DIM]
    loss = summed[a + b + 2 * c + HEAD_DIM] / (D * counted)

    def give_back(v):
        sent = nn(deal_t, v.astype(BF16)).astype(BF16).reshape(shards, share, D)
        got = lax.all_to_all(sent, AXES, split_axis=0, concat_axis=0, tiled=True)
        return nn(sort_t, got.reshape(rows, D)).astype(BF16)

    output = give_back(y)
    input_grad = give_back(dx)
    return (
        output, input_grad, g_in, g_beta, g_taps, g_out, g_gain_one, g_gain_out, g_gain_two, g_gu,
        g_down, loss,
    )


def solution(mesh):
    both = P(AXES, None)
    flat = P(AXES)
    in_specs = (both, both, both, flat, flat, both, both, both, P(None, AXES), both, flat, P(), flat,
                both, both)
    out_specs = (both, both, both, both, P(None, AXES), both, flat, P(), flat, both, both, P())
    return jax.shard_map(local, mesh=mesh, in_specs=in_specs, out_specs=out_specs, check_vma=False)
```

time: 1930 us -> 940 us (0.49)
  other arithmetic: 419 us -> 17.5 us
  blocking collectives: 211 us -> 0 us
  waiting for transfers between devices: 876 us -> 746 us
  local copies, waits for them, and re-layouts: 149 us -> 21 us
  matrix products: 200 us -> 79.5 us
  Pallas kernels: 0 us -> 40.2 us
    another operation x42 -> x1, other arithmetic: 337 us -> 0.18 us  [local(): ends = jnp.cumsum(lengths, axis=1)]
    reduce_scatter x4, waiting for transfers between devices: 720 us -> 469 us  [scatter(): lax.psum_scatter(v, AXES, scatter_dimension=0, tiled=True).astype(F32)]
    all_gather x4, waiting for transfers between devices: 0.03 us -> 192 us  [the longest x1 89.3 us: local(): wgu = lax.all_gather(w_gu, AXES, axis=0, tiled=True)]
    unnamed x12 -> x8, waiting for transfers between devices: 126 us -> 2.65 us
    dot_general x100 -> x21, matrix products: 174 us -> 79.5 us  [the longest x11 34.6 us: nn(): return jnp.dot(left, right, preferred_element_type=F32)]
    all_gather x2 -> x0, blocking collectives: 87.2 us -> none  [the longest x1 46.3 us: local(): lax.all_gather(w_beta, ('dp', 'fsdp'), axis=0, tiled=True)]
    unnamed x2 -> x0, blocking collectives: 79.8 us -> none
    all_to_all x7 -> x4, waiting for transfers between devices: 29.9 us -> 82 us  [the longest x1 51.7 us: local(): lax.all_to_all(message, AXES, split_axis=0, concat_axis=0, tiled=True)]
  transfers between devices with their start and end apart: 17 -> 12, of which waited for: 9 -> 12; matrix products, arithmetic and copies ran while one was open for 21% -> 9% of each run, Pallas kernels for 0% -> 4%
where the time goes in v1:
time: 940 us; the launch traced here: 939 us
  waiting for transfers between devices  746 us (79%)
  matrix products  79.5 us (8%)
  Pallas kernels  40.2 us (4%)
  local copies, waits for them, and re-layouts  21 us (2%)
  between operations  17.8 us (2%)
  other arithmetic  17.5 us (2%)
  starting transfers between devices  17.2 us (2%)
    reduce_scatter x4, waiting for transfers between devices, scatter(): lax.psum_scatter(v, AXES, scatter_dimension=0, tiled=True).astype(F32)  469 us
    all_gather x1, waiting for transfers between devices, local(): wgu = lax.all_gather(w_gu, AXES, axis=0, tiled=True)  89.3 us
    all_gather x1, waiting for transfers between devices, local(): wdown = lax.all_gather(w_down, AXES, axis=0, tiled=True)  57.5 us
    all_to_all x1, waiting for transfers between devices, local(): lax.all_to_all(message, AXES, split_axis=0, concat_axis=0, tiled=True)  51.7 us
    dot_general x11, matrix products, nn(): return jnp.dot(left, right, preferred_element_type=F32)  34.6 us
    all_to_all x2, waiting for transfers between devices, give_back(): got = lax.all_to_all(sent, AXES, split_axis=0, concat_axis=0, tiled=True)  24.4 us
    all_gather x1, waiting for transfers between devices, local(): wout = lax.all_gather(w_out, AXES, axis=0, tiled=True)  24 us
    pallas_call x1, Pallas kernels, mixer_forward(): pl.pallas_call(functools.partial(mixer_fwd_kernel, blocks, rows_mb), grid...  23.2 us
  transfers between devices with their start and end apart: 12, of which 12 were waited for; matrix products, arithmetic and copies ran while one was open for 9% of the time, Pallas kernels for 4%

profile of v1, /device:TPU:0, one launch (start us, length us, event | category | flops | bytes accessed | tf_op | source)
XLA Modules:
  0.0 939.4 jit_solution(4395733659949940340)
XLA Ops:
  20.1 7.3 all-to-all-start
  29.7 51.7 %all-to-all-done = bf16[32,8,3328]{2,1,0:T(8,128)(2,1)S(1)} async-done(((bf16[32,8,3328]{2,1,0:T(8,128)(2,1)}), bf16[32,8,3328]{2,1,0:T(8,128)(2,1)S(1)}, u32[]{:S(2)}, u32[]{:S(2)}) %all-to-all-start) | async-done | bytes 1703968 | tf_op jit(solution)/shard_map/all_to_all | solution.py:338
  86.7 21.3 %all-gather.5.cloned.1.call-done = bf16[1024,4096]{1,0:T(8,128)(2,1)} async-done(((bf16[32,4096]{1,0:T(8,128)(2,1)}), bf16[1024,4096]{1,0:T(8,128)(2,1)}) %all-gather.5.cloned.1.call-update) | async-done | bytes 8388624 | tf_op jit(solution)/shard_map/all_gather | solution.py:340
  108.1 7.7 fusion.45.pq.pk.pv.pg
  115.8 23.2 %mixer_fwd.1 = (bf16[256,1024]{1,0:T(8,128)(2,1)S(1)}, f32[256,1024]{1,0:T(8,128)S(1)}, f32[8,2,128,128]{3,2,1,0:T(8,128)S(1)}, f32[8,2,128,128]{3,2,1,0:T(8,128...) custom-call(f32[256,4096]{1,0:T(8,128)} %fusion.45.pq.pk.pv.pg, f32[256,4096]{1,0:T(8,128)} %fusion.45.pq.pk.pv.pg, ...), custom_call_target="tpu_custom_call" | custom-call | tf_op jit(solution)/shard_map/mixer_fwd/pallas_call | solution.py:245
  141.9 24.0 %all-gather.7.cloned.1.call-done = bf16[1024,1024]{1,0:T(8,128)(2,1)} async-done(((bf16[32,1024]{1,0:T(8,128)(2,1)}), bf16[1024,1024]{1,0:T(8,128)(2,1)}) %all-gather.7.cloned.1.call-update) | async-done | bytes 2097168 | tf_op jit(solution)/shard_map/all_gather | solution.py:341
  169.5 89.3 %all-gather.9.cloned.1.call-done = bf16[1024,5632]{1,0:T(8,128)(2,1)} async-done(((bf16[32,5632]{1,0:T(8,128)(2,1)}), bf16[1024,5632]{1,0:T(8,128)(2,1)}) %all-gather.9.cloned.1.call-update) | async-done | bytes 11534352 | tf_op jit(solution)/shard_map/all_gather | solution.py:342
  258.8 6.4 fusion.43
  269.8 57.5 %all-gather.11.cloned.1.call-done = bf16[2816,1024]{1,0:T(8,128)(2,1)} async-done(((bf16[88,1024]{1,0:T(8,128)(2,1)}), bf16[2816,1024]{1,0:T(8,128)(2,1)}) %all-gather.11.cloned.1.call-update) | async-done | bytes 5767184 | tf_op jit(solution)/shard_map/all_gather | solution.py:343
  327.2 6.8 slice_add_fusion
  334.9 3.7 multiply_convert_fusion.1
  338.7 7.4 multiply_reduce_fusion
  349.6 5.8 convolution_convert_fusion.2
  358.1 17.0 %mixer_bwd.1 = (bf16[256,1024]{1,0:T(8,128)(2,1)S(1)}, bf16[256,1024]{1,0:T(8,128)(2,1)S(1)}, bf16[256,1024]{1,0:T(8,128)(2,1)S(1)}, bf16[256,1024]{1,0:T(8,128)...) custom-call(f32[256,4096]{1,0:T(8,128)} %fusion.45.pq.pk.pv.pg, ...), custom_call_target="tpu_custom_call" | custom-call | tf_op jit(solution)/shard_map/mixer_bwd/pallas_call | solution.py:266
  376.7 5.7 convolution_convert_fusion.1
  383.6 7.9 convolution_convert_fusion
  392.6 6.5 fusion.47
  409.4 5.9 all-to-all-done.3
  420.6 13.6 %all-to-all-done.1 = bf16[32,8,1024]{2,1,0:T(8,128)(2,1)S(1)} async-done(((bf16[32,8,1024]{2,1,0:T(8,128)(2,1)}), bf16[32,8,1024]{2,1,0:T(8,128)(2,1)S(1)}, u32[]{:S(2)}, u32[]{:S(2)}) %all-to-all-start.1) | async-done | bytes 524320 | tf_op jit(solution)/shard_map/all_to_all | solution.py:450
  443.2 10.8 %all-to-all-done.2 = bf16[32,8,1024]{2,1,0:T(8,128)(2,1)S(1)} async-done(((bf16[32,8,1024]{2,1,0:T(8,128)(2,1)}), bf16[32,8,1024]{2,1,0:T(8,128)(2,1)S(1)}, u32[]{:S(2)}, u32[]{:S(2)}) %all-to-all-start.2) | async-done | bytes 524320 | tf_op jit(solution)/shard_map/all_to_all | solution.py:450
  455.1 31.5 %reduce-scatter.7.cloned.1.call-done = bf16[32,1024]{1,0:T(8,128)(2,1)} async-done(((bf16[1024,1024]{1,0:T(8,128)(2,1)}), bf16[32,1024]{1,0:T(8,128)(2,1)}) %reduce-scatter.7.cloned.1.call-update) | async-done | bytes 65552 | tf_op jit(solution)/shard_map/reduce_scatter | solution.py:413
  488.1 141.1 %reduce-scatter.11.cloned.1.call-done = bf16[88,1024]{1,0:T(8,128)(2,1)} async-done(((bf16[2816,1024]{1,0:T(8,128)(2,1)}), bf16[88,1024]{1,0:T(8,128)(2,1)}) %reduce-scatter.11.cloned.1.call-update) | async-done | bytes 180240 | tf_op jit(solution)/shard_map/reduce_scatter | solution.py:413
  630.8 145.3 %reduce-scatter.5.cloned.1.call-done = bf16[32,4096]{1,0:T(8,128)(2,1)} async-done(((bf16[1024,4096]{1,0:T(8,128)(2,1)}), bf16[32,4096]{1,0:T(8,128)(2,1)}) %reduce-scatter.5.cloned.1.call-update) | async-done | bytes 262160 | tf_op jit(solution)/shard_map/reduce_scatter | solution.py:413
  777.9 151.5 %reduce-scatter.9.cloned.1.call-done = bf16[32,5632]{1,0:T(8,128)(2,1)} async-done(((bf16[1024,5632]{1,0:T(8,128)(2,1)}), bf16[32,5632]{1,0:T(8,128)(2,1)}) %reduce-scatter.9.cloned.1.call-update) | async-done | bytes 360464 | tf_op jit(solution)/shard_map/reduce_scatter | solution.py:413
  (151 shorter events, 72.6 us)
Async XLA Ops:
  7.2 100.9 %all-gather.5.cloned.1.call-start = ((), (), s32[]{:S(2)}) async-start(), calls=%async_computation.8 | async-start | bytes 8650752 | tf_op jit(solution)/shard_map/all_gather | solution.py:340
  7.9 158.0 %all-gather.7.cloned.1.call-start = ((), (), s32[]{:S(2)}) async-start(), calls=%async_computation.9 | async-start | bytes 2162688 | tf_op jit(solution)/shard_map/all_gather | solution.py:341
  8.7 250.2 %all-gather.9.cloned.1.call-start = ((), (), s32[]{:S(2)}) async-start(), calls=%async_computation.10 | async-start | bytes 11894784 | tf_op jit(solution)/shard_map/all_gather | solution.py:342
  9.4 317.8 %all-gather.11.cloned.1.call-start = ((), (), s32[]{:S(2)}) async-start(), calls=%async_computation.11 | async-start | bytes 5947392 | tf_op jit(solution)/shard_map/all_gather | solution.py:343
  18.7 8.7 copy-start.16
  18.7 11.0 %copy-start.18 = (bf16[128]{0:T(256)(128)(2,1)S(1)}, bf16[128]{0:T(256)(128)(2,1)}, u32[]{:S(2)}) copy-start(bf16[128]{0:T(256)(128)(2,1)} %param.26) | copy-start | bytes 772
  20.1 61.4 %all-to-all-start = ((bf16[32,8,3328]{2,1,0:T(8,128)(2,1)}), bf16[32,8,3328]{2,1,0:T(8,128)(2,1)S(1)}, u32[]{:S(2)}, u32[]{:S(2)}) async-start(bf16[32,8,3328]{2,1,0:T(8,128)(2,1)} %pad_maximum_fusion.3), calls=%async_computation | async-start | bytes 3407872 | tf_op jit(solution)/shard_map/all_to_all | solution.py:338
  27.4 459.2 %reduce-scatter.7.cloned.1.call-start = ((), (), s32[]{:S(2)}) async-start(), calls=%async_computation.13 | async-start | bytes 2162688 | tf_op jit(solution)/shard_map/reduce_scatter | solution.py:413
  84.5 1.8 copy-start.5
  86.4 29.3 %copy-start.10 = (bf16[256,1024]{1,0:T(8,128)(2,1)}, bf16[256,1024]{1,0:T(8,128)(2,1)S(1)}, u32[]{:S(2)}) copy-start(bf16[256,1024]{1,0:T(8,128)(2,1)S(1)} %multiply_convert_fusion.4) | copy-start | bytes 1572868
  265.2 2.5 copy-start.3
  327.2 6.8 copy-start.4
  327.2 7.7 copy-start.17
  334.0 12.1 %copy-start.12 = (f32[256,1024]{1,0:T(8,128)}, f32[256,1024]{1,0:T(8,128)S(1)}, u32[]{:S(2)}) copy-start(f32[256,1024]{1,0:T(8,128)S(1)} %get-tuple-element.110) | copy-start | bytes 3145732
  334.9 3.7 copy-start.6
  338.7 7.4 copy-start.15
  349.5 279.6 %reduce-scatter.11.cloned.1.call-start = ((), (), s32[]{:S(2)}) async-start(), calls=%async_computation.15 | async-start | bytes 5947392 | tf_op jit(solution)/shard_map/reduce_scatter | solution.py:413
  355.4 420.8 %reduce-scatter.5.cloned.1.call-start = ((), (), s32[]{:S(2)}) async-start(), calls=%async_computation.12 | async-start | bytes 8650752 | tf_op jit(solution)/shard_map/reduce_scatter | solution.py:413
  382.4 547.1 %reduce-scatter.9.cloned.1.call-start = ((), (), s32[]{:S(2)}) async-start(), calls=%async_computation.14 | async-start | bytes 11894784 | tf_op jit(solution)/shard_map/reduce_scatter | solution.py:413
  392.5 6.5 copy-start.13
  401.8 16.1 %copy-start.9 = (f32[256,1024]{1,0:T(8,128)S(1)}, f32[256,1024]{1,0:T(8,128)}, u32[]{:S(2)}) copy-start(f32[256,1024]{1,0:T(8,128)} %copy-done.8) | copy-start | bytes 3145732
  403.4 11.9 %all-to-all-start.3 = ((f32[32,7,128]{2,1,0:T(8,128)}), f32[32,7,128]{2,1,0:T(8,128)S(1)}, u32[]{:S(2)}, u32[]{:S(2)}) async-start(f32[32,7,128]{2,1,0:T(8,128)} %reshape.389), calls=%async_computation.4 | async-start | bytes 262144 | tf_op jit(solution)/shard_map/all_to_all | solution.py:436
  415.3 18.9 %all-to-all-start.1 = ((bf16[32,8,1024]{2,1,0:T(8,128)(2,1)}), bf16[32,8,1024]{2,1,0:T(8,128)(2,1)S(1)}, u32[]{:S(2)}, u32[]{:S(2)}) async-start(bf16[32,8,1024]{2,1,0:T(8,128)(2,1)} %fusion.12), calls=%async_computation.1 | async-start | bytes 1048576 | tf_op jit(solution)/shard_map/all_to_all | solution.py:450
  434.2 19.7 %all-to-all-start.2 = ((bf16[32,8,1024]{2,1,0:T(8,128)(2,1)}), bf16[32,8,1024]{2,1,0:T(8,128)(2,1)S(1)}, u32[]{:S(2)}, u32[]{:S(2)}) async-start(bf16[32,8,1024]{2,1,0:T(8,128)(2,1)} %fusion.13), calls=%async_computation.2 | async-start | bytes 1048576 | tf_op jit(solution)/shard_map/all_to_all | solution.py:450
  (7 other events, 8.1 us)
Sparse Core Ops, SparseCore 0:
  10.9 97.1 all-gather.4
  110.9 54.9 all-gather.6
  168.8 90.0 all-gather.8
  261.5 65.6 all-gather.10
  349.6 136.8 reduce-scatter.6
  488.8 140.2 reduce-scatter.10
  631.5 144.5 reduce-scatter.4
  778.6 150.8 reduce-scatter.8

commit v2 on v1

--- a/solution.py
+++ b/solution.py
@@ -16,6 +16,7 @@
 F32 = jnp.float32
 BF16 = jnp.bfloat16
 PAIR = 2
+MESH = pl.DeviceIdType.MESH
 
 
 def mm(left, right, lc, rc):
@@ -124,12 +125,11 @@
 
 
 def mixer_bwd_kernel(
-    blocks, rows_mb,
+    blocks, rows_mb, step,
     pq, pk, pv, pg, beta, tq, tk, tv, gain, mask, segc, segr,
     don_ref, o_ref, ainv_ref, u_ref, p_ref, l_ref,
     dq_ref, dk_ref, dv_ref, dg_ref, dbeta_ref, dtq, dtk, dtv, dgain_ref,
 ):
-    step = pl.program_id(0)
     rows = blocks * rows_mb
     masks = [None] + [mask[:, s : s + 1] for s in range(1, CONV)]
     pres, rolls, cs, sig = [], [], [], []
@@ -237,46 +237,682 @@
     return ins, mat, one, otap, full
 
 
-def mixer_forward(proj, beta_pre, taps, gain, mask, segc, segr, blocks):
-    rows = proj.shape[0]
+def lin_index():
+    return lax.axis_index("dp") * lax.axis_size("fsdp") + lax.axis_index("fsdp")
+
+
+def mesh_id(index):
+    inner = lax.axis_size("fsdp")
+    return (lax.div(index, inner), lax.rem(index, inner))
+
+
+def flip(me, bits, number, always=()):
+    result = me
+    for bit in always:
+        own = lax.rem(lax.div(me, 1 << bit), 2)
+        result = result + (1 - 2 * own) * (1 << bit)
+    for i, bit in enumerate(reversed(bits)):
+        own = lax.rem(lax.div(me, 1 << bit), 2)
+        if isinstance(number, int):
+            flag = (number >> i) & 1
+            if flag == 0:
+                continue
+        else:
+            flag = lax.rem(lax.div(number, 1 << i), 2)
+        result = result + flag * (1 - 2 * own) * (1 << bit)
+    return result
+
+
+def routes(shards):
+    bits = shards.bit_length() - 1
+    rest = list(range(4, bits))
+    return [[1, 3, 2] + rest, [2, 1, 3] + rest, [3, 2, 1] + rest]
+
+
+def colours(width, turn):
+    tiles = width // 128
+    sizes = [tiles // 3 + (1 if (c - turn) % 3 < tiles % 3 else 0) for c in range(3)]
+    cuts, at = [], 0
+    for s in sizes:
+        cuts.append((at * 128, s * 128))
+        at += s
+    return cuts
+
+
+def meet(shards, me, everyone):
+    barrier = pltpu.get_barrier_semaphore()
+    if everyone:
+
+        def greet(r, _):
+            pl.semaphore_signal(
+                barrier, inc=1, device_id=mesh_id(lax.rem(me + r, shards)), device_id_type=MESH
+            )
+            return 0
+
+        lax.fori_loop(1, shards, greet, 0)
+        pl.semaphore_wait(barrier, shards - 1)
+    else:
+        bits = shards.bit_length() - 1
+        for bit in range(bits):
+            pl.semaphore_signal(
+                barrier, inc=1, device_id=mesh_id(flip(me, [], 0, (bit,))), device_id_type=MESH
+            )
+        pl.semaphore_wait(barrier, bits)
+
+
+class Exchange:
+    def __init__(self, shards, me, sent, got, send, recv, keep):
+        self.shards, self.me, self.sent, self.got = shards, me, sent, got
+        self.send, self.recv, self.keep = send, recv, keep
+
+    def own(self):
+        return pltpu.make_async_copy(self.sent.at[self.me], self.got.at[self.me], self.keep)
+
+    def start(self):
+        self.own().start()
+
+        def one(r, _):
+            peer = lax.rem(self.me + r, self.shards)
+            pltpu.make_async_remote_copy(
+                src_ref=self.sent.at[peer], dst_ref=self.got.at[self.me], send_sem=self.send,
+                recv_sem=self.recv, device_id=mesh_id(peer), device_id_type=MESH,
+            ).start()
+            return 0
+
+        lax.fori_loop(1, self.shards, one, 0)
+
+    def wait(self):
+        self.own().wait()
+        whole = pl.ds(0, self.shards - 1)
+        pltpu.make_async_remote_copy(
+            src_ref=self.sent.at[whole], dst_ref=self.got.at[whole], send_sem=self.send,
+            recv_sem=self.recv, device_id=mesh_id(self.me), device_id_type=MESH,
+        ).wait()
+
+
+DEAL_AT = 0
+CHUNK = 256
+
+
+def pieces_of(widths, split):
+    result = []
+    for i, width in enumerate(widths):
+        tiles, at = width // 128, 0
+        for j in range(split[i]):
+            size = tiles // split[i] + (1 if j < tiles % split[i] else 0)
+            result.append((i, at * 128, size * 128))
+            at += size
+    return result
+
+
+class Gather:
+    def __init__(self, shards, me, pieces, own, full, sems):
+        self.me, self.pieces, self.own, self.full = me, pieces, own, full
+        self.send, self.recv, self.pair_send, self.pair_recv, self.keep = sems
+        self.stages = shards.bit_length() - 2
+        self.order = routes(shards)
+        self.core = lax.rem(me, 2)
+        self.cuts = [
+            [(at + a, s) for a, s in colours(size, n)] for n, (_, at, size) in enumerate(pieces)
+        ]
+        self.last = len(pieces) + self.stages - 1
+
+    @staticmethod
+    def semaphores(shards, pieces):
+        dma, stages = pltpu.SemaphoreType.DMA, shards.bit_length() - 2
+        number = len(pieces)
+        return [dma((stages, number, 3)), dma((stages, number, 3)), dma((number,)), dma((number,)),
+                dma((number,))]
+
+    def kept(self, i):
+        return pltpu.make_async_copy(
+            self.own[i], self.full[i].at[lax.div(self.me, 2), self.core], self.keep.at[i]
+        )
+
+    def begin(self):
+        for i in range(len(self.own)):
+            self.kept(i).start()
+
+    def partner(self, k, c):
+        return mesh_id(flip(self.me, [], 0, (self.order[c][self.stages - 1 - k],)))
+
+    def group(self, k, n, c):
+        at, size = self.cuts[n][c]
+        some = self.full[self.pieces[n][0]].at[pl.ds(0, 1 << k), 0, :, pl.ds(at, size)]
+        return pltpu.make_async_remote_copy(
+            src_ref=some, dst_ref=some, send_sem=self.send.at[k, n, c],
+            recv_sem=self.recv.at[k, n, c], device_id=self.partner(k, c), device_id_type=MESH,
+        )
+
+    def half(self, n):
+        i, at, size = self.pieces[n]
+        some = self.full[i].at[:, self.core, :, pl.ds(at, size)]
+        return pltpu.make_async_remote_copy(
+            src_ref=some, dst_ref=some, send_sem=self.pair_send.at[n],
+            recv_sem=self.pair_recv.at[n], device_id=mesh_id(flip(self.me, [], 0, (0,))),
+            device_id_type=MESH,
+        )
+
+    def launch(self, k, n):
+        i = self.pieces[n][0]
+        for c in range(3):
+            at, size = self.cuts[n][c]
+            if k > 0:
+                self.group(k - 1, n, c).wait_recv()
+            have = self.order[c][self.stages - k :]
+            for j in range(1 << k):
+                d = flip(self.me, have, j)
+                there = self.full[i].at[lax.div(d, 2), self.core, :, pl.ds(at, size)]
+                pltpu.make_async_remote_copy(
+                    src_ref=self.own[i].at[:, pl.ds(at, size)] if j == 0 else there,
+                    dst_ref=there, send_sem=self.send.at[k, n, c], recv_sem=self.recv.at[k, n, c],
+                    device_id=self.partner(k, c), device_id_type=MESH,
+                ).start()
+
+    def finish(self, n):
+        for c in range(3):
+            self.group(self.stages - 1, n, c).wait_recv()
+        if n == 0 or self.pieces[n - 1][0] != self.pieces[n][0]:
+            self.kept(self.pieces[n][0]).wait()
+        self.half(n).start()
+
+    def step(self, t):
+        for n in range(len(self.pieces)):
+            k = t - n
+            if 0 <= k < self.stages:
+                self.launch(k, n)
+            elif k == self.stages:
+                self.finish(n)
+
+    def end(self):
+        for k in range(self.stages):
+            for n in range(len(self.pieces)):
+                for c in range(3):
+                    self.group(k, n, c).wait_send()
+        for n in range(len(self.pieces)):
+            self.half(n).wait()
+
+
+def first_kernel(shards, pieces, *refs):
+    count = 1 + max(i for i, _, _ in pieces)
+    own, sent, full, got = refs[:count], refs[count], refs[count + 1 : 2 * count + 1], refs[2 * count + 1]
+    sems = refs[2 * count + 2 :]
+    me = lin_index()
+    deal = Exchange(shards, me, sent, got, *sems[5:])
+    weights = Gather(shards, me, pieces, own, full, sems[:5])
+    weights.begin()
+    meet(shards, me, True)
+    deal.start()
+    for t in range(weights.last + 1):
+        weights.step(t)
+    deal.wait()
+    weights.end()
+
+
+def spread(weight, shards):
+    return jax.ShapeDtypeStruct((shards // 2, 2) + weight.shape, weight.dtype)
+
+
+def first(weights, split, message, shards, collective_id):
+    count = len(weights)
+    anywhere = pl.BlockSpec(memory_space=pl.ANY)
+    pieces = pieces_of([w.shape[1] for w in weights], split)
+    dma = pltpu.SemaphoreType.DMA
+    *full, got = pl.pallas_call(
+        functools.partial(first_kernel, shards, pieces),
+        in_specs=[anywhere] * (count + 1),
+        out_specs=[anywhere] * (count + 1),
+        out_shape=[spread(w, shards) for w in weights]
+        + [jax.ShapeDtypeStruct(message.shape, message.dtype)],
+        scratch_shapes=Gather.semaphores(shards, pieces) + [dma, dma, dma],
+        compiler_params=pltpu.CompilerParams(collective_id=collective_id, has_side_effects=True),
+        name="gather_first",
+    )(*weights, message)
+    return [f.reshape(-1, f.shape[-1]) for f in full], got
+
+
+def forward_kernel(
+    shards, pieces, blocks, rows_mb,
+    own_down, own_gu, sent, a1, wq, wk, wv, wg, wout, wbeta, x, gain_two, tq, tk, tv, gain, mask,
+    segc, segr,
+    full_down, full_gu, got, pq, pk, pv, pg, beta, on, o, ainv, u, p, l, resid, a2,
+    *sems,
+):
+    step = pl.program_id(0)
+    steps = HEADS // PAIR
+    me = lin_index()
+    weights = Gather(shards, me, pieces, (own_down, own_gu), (full_down, full_gu), sems[:5])
+    deal = Exchange(shards, me, sent, got, *sems[5:])
+
+    @pl.when(step == 0)
+    def _():
+        weights.begin()
+        meet(shards, me, True)
+        weights.step(0)
+        resid[...] = x[...]
+
+    normed = a1[...]
+    beta[...] = jnp.dot(normed, wbeta[...], preferred_element_type=F32)
+    for out, w in ((pq, wq), (pk, wk), (pv, wv), (pg, wg)):
+        out[...] = jnp.dot(normed, w[...], preferred_element_type=F32)
+    mixer_fwd_kernel(
+        blocks, rows_mb, pq, pk, pv, pg, beta, tq, tk, tv, gain, mask, segc, segr, on, o, ainv, u,
+        p, l,
+    )
+    resid[...] += jnp.dot(on[...], wout[...], preferred_element_type=F32)
+    for s in range(steps):
+
+        @pl.when(step == s)
+        def _(s=s):
+            weights.step(s + 1)
+            if s == DEAL_AT:
+                deal.start()
+            if s == steps - 1:
+                r = resid[...]
+                a2[...] = (rms(r)[0] * gain_two[...]).astype(BF16)
+                for t in range(steps + 1, weights.last + 1):
+                    weights.step(t)
+                deal.wait()
+                weights.end()
+
+
+def forward(
+    w_down, w_gu, message, split, a1, win, wout, wbeta, x, gain_two, taps, gain, mask, segc, segr, blocks,
+    shards, collective_id,
+):
+    rows = x.shape[0]
     rows_mb = rows // blocks
-    ins, mat, one, _, _ = mixer_specs(rows, blocks, rows_mb)
+    width = PAIR * HEAD_DIM
+    pieces = pieces_of([w_down.shape[1], w_gu.shape[1]], split)
+    anywhere = pl.BlockSpec(memory_space=pl.ANY)
+    ins, mat, one, _, full = mixer_specs(rows, blocks, rows_mb)
+    per = D // width
+    wcol = lambda k: pl.BlockSpec((D, width), lambda i, k=k: (0, k * per + i))
     square = jax.ShapeDtypeStruct((HEADS, blocks, rows_mb, rows_mb), F32)
+    wide = jax.ShapeDtypeStruct((rows, D), F32)
+    dma = pltpu.SemaphoreType.DMA
+    full_down, full_gu, got, *rest = pl.pallas_call(
+        functools.partial(forward_kernel, shards, pieces, blocks, rows_mb),
+        grid=(HEADS // PAIR,),
+        in_specs=[
+            anywhere, anywhere, anywhere, full((rows, D)), wcol(0), wcol(1), wcol(2), wcol(3),
+            pl.BlockSpec((width, D), lambda i: (i, 0)), full((D, HEADS)), full((rows, D)),
+            full((1, D)), *ins[5:],
+        ],
+        out_specs=[anywhere, anywhere, anywhere, one, one, one, one, full((rows, HEADS)), one, one, mat, mat,
+                   mat, mat, full((rows, D)), full((rows, D))],
+        out_shape=[
+            spread(w_down, shards), spread(w_gu, shards),
+            jax.ShapeDtypeStruct(message.shape, message.dtype), wide, wide, wide, wide,
+            jax.ShapeDtypeStruct((rows, HEADS), F32), jax.ShapeDtypeStruct((rows, D), BF16), wide,
+            square, square, square, square, wide, jax.ShapeDtypeStruct((rows, D), BF16),
+        ],
+        scratch_shapes=Gather.semaphores(shards, pieces) + [dma, dma, dma],
+        compiler_params=pltpu.CompilerParams(
+            collective_id=collective_id, has_side_effects=True, vmem_limit_bytes=48 << 20
+        ),
+        name="mixer_forward",
+    )(w_down, w_gu, message, a1, win, win, win, win, wout, wbeta, x, gain_two, taps, taps, taps, gain, mask,
+      segc, segr)
+    return full_down.reshape(FF, D), full_gu.reshape(D, 2 * FF), got, rest
+
+
+class Scatter:
+    def __init__(self, shards, me, pieces, whole, mine, other, coming, sems, kept):
+        self.me, self.pieces, self.whole, self.mine = me, pieces, whole, mine
+        self.other, self.coming, self.kept_of = other, coming, kept
+        self.send, self.recv, self.pair_send, self.pair_recv = sems
+        self.stages = shards.bit_length() - 2
+        self.order = routes(shards)
+        self.core = lax.rem(me, 2)
+        self.cuts = [
+            [(at + a, s) for a, s in colours(size, n)] for n, (_, at, size) in enumerate(pieces)
+        ]
+
+    @staticmethod
+    def semaphores(shards, number):
+        dma, stages = pltpu.SemaphoreType.DMA, shards.bit_length() - 2
+        return [dma((stages, number, 3)), dma((stages, number, 3)), dma((number,)), dma((number,))]
+
+    @staticmethod
+    def buffers(shards, shapes):
+        stages = shards.bit_length() - 2
+        return [pltpu.VMEM((shards // 2,) + s, BF16) for s in shapes] + [
+            pltpu.VMEM((1 << (stages - 1 - k),) + s, BF16) for s in shapes for k in range(stages)
+        ]
+
+    @staticmethod
+    def split(shards, count, refs):
+        stages = shards.bit_length() - 2
+        other, refs = refs[:count], refs[count:]
+        return other, [refs[i * stages : (i + 1) * stages] for i in range(count)]
+
+    def pair(self, n):
+        i, at, size = self.pieces[n]
+        return pltpu.make_async_remote_copy(
+            src_ref=self.whole(n, 1 - self.core), dst_ref=self.other[i].at[:, :, pl.ds(at, size)],
+            send_sem=self.pair_send.at[n], recv_sem=self.pair_recv.at[n],
+            device_id=mesh_id(flip(self.me, [], 0, (0,))), device_id_type=MESH,
+        )
+
+    def hop(self, k, n, c, source, spots):
+        i = self.pieces[n][0]
+        at, size = self.cuts[n][c]
+        cols = pl.ds(at, size)
+        return pltpu.make_async_remote_copy(
+            src_ref=self.other[i].at[source, :, cols],
+            dst_ref=self.coming[i][k].at[spots, :, cols],
+            send_sem=self.send.at[k, n, c], recv_sem=self.recv.at[k, n, c],
+            device_id=mesh_id(flip(self.me, [], 0, (self.order[c][k],))), device_id_type=MESH,
+        )
+
+    def group(self, k, n, c):
+        all_of = pl.ds(0, 1 << (self.stages - 1 - k))
+        return self.hop(k, n, c, all_of, all_of)
+
+    def total(self, k, n, c, shard, spot):
+        i = self.pieces[n][0]
+        at, size = self.cuts[n][c]
+        cols = pl.ds(at, size)
+        q = lax.div(shard, 2)
+        value = self.mine(i, q, cols).astype(F32) + self.other[i][q, :, cols].astype(F32)
+        for p in range(k):
+            value = value + self.coming[i][p][spot, :, cols].astype(F32)
+        return value
+
+    def launch(self, k, n):
+        if k == 0:
+            kept = self.kept_of(n)
+            if kept is not None:
+                kept.wait()
+            self.pair(n).wait_recv()
+        for c in range(3):
+            if k > 0:
+                self.group(k - 1, n, c).wait_recv()
+            much = 1 << (self.stages - 1 - k)
+            at, size = self.cuts[n][c]
+
+            def body(j, _, c=c, at=at, size=size):
+                shard = flip(self.me, self.order[c][k + 1 :], j, (self.order[c][k],))
+                q = lax.div(shard, 2)
+                self.other[self.pieces[n][0]][q, :, pl.ds(at, size)] = self.total(
+                    k, n, c, shard, much + j
+                ).astype(BF16)
+                self.hop(k, n, c, q, j).start()
+                return 0
+
+            lax.fori_loop(0, much, body, 0)
+
+    def finish(self, n, write):
+        for c in range(3):
+            self.group(self.stages - 1, n, c).wait_recv()
+            at, size = self.cuts[n][c]
+            write(self.pieces[n][0], at, size, self.total(self.stages, n, c, self.me, 0))
+
+    def end(self, n):
+        for k in range(self.stages):
+            for c in range(3):
+                self.group(k, n, c).wait_send()
+        self.pair(n).wait_send()
+
+
+def backward_kernel(shards, blocks, rows_mb, pieces, *refs):
+    (d_down, df, a2, gate, up, wga, wup, wdn, dy, resid, gain_two, wout, wq, wk, wv, wg, a1, on, x,
+     gain_one, wbeta, *mixer), refs = refs[:38], refs[38:]
+    (g_down, g_gu, dwq, dwk, dwv, dwg, dw_out, d_wbeta, dx, d_two, d_one, dtq, dtk, dtv,
+     d_gain), refs = refs[:15], refs[15:]
+    (mine_down, d_gu, acc, dresid, dz, don, dpq, dpk, dpv, dpg, dbeta, keep), refs = refs[:12], refs[12:]
+    sems, buffers = refs[:4], refs[4:]
+    step = pl.program_id(0)
+    chunks = FF // CHUNK
+    pairs = HEADS // PAIR
+    me = lin_index()
+    core = lax.rem(me, 2)
+    other, coming = Scatter.split(shards, 2, buffers)
+    r_gu = d_gu.shape[2]
+
+    def whole(n, parity):
+        i, at, size = pieces[n]
+        if i == 0:
+            return d_down.at[:, parity, :, pl.ds(at, size)]
+        return d_gu.at[:, parity, :, pl.ds(at, size)]
+
+    def mine(i, q, cols):
+        return mine_down[q, :, cols] if i == 0 else d_gu[q, core, :, cols]
+
+    def kept(n):
+        if n > 0:
+            return None
+        return pltpu.make_async_copy(d_down.at[:, core], mine_down, keep)
+
+    net = Scatter(shards, me, pieces, whole, mine, other, coming, sems, kept)
+
+    def write(i, at, size, value):
+        if i == 0:
+            g_down[:, pl.ds(at, size)] = value
+            return
+        for tile in range(at // 128, (at + size) // 128):
+            chunk, inner = tile * 128 // (2 * CHUNK), tile * 128 % (2 * CHUNK)
+            start = chunk * CHUNK + inner if inner < CHUNK else FF + chunk * CHUNK + inner - CHUNK
+            g_gu[:, start : start + 128] = value[:, tile * 128 - at : tile * 128 - at + 128]
+
+    @pl.when(step == 0)
+    def _():
+        kept(0).start()
+        meet(shards, me, False)
+        net.pair(0).start()
+        acc[...] = jnp.zeros_like(acc)
+
+    @pl.when(step < chunks)
+    def _():
+        dhid = nt(df[...], wdn[...])
+        g = gate[...]
+        s = sigmoid(g)
+        d_gate = (dhid * up[...] * (s * (1.0 + g * (1.0 - s)))).astype(BF16)
+        d_up = (dhid * (g * s)).astype(BF16)
+        acc[...] += nt(d_gate, wga[...]) + nt(d_up, wup[...])
+        for at, part in ((0, d_gate), (CHUNK, d_up)):
+            grad = tn(a2[...], part).reshape(shards // 2, 2, r_gu, CHUNK).astype(BF16)
+            start = pl.multiple_of(step * (2 * CHUNK) + at, CHUNK)
+            d_gu[:, :, :, pl.ds(start, CHUNK)] = grad
+
+    @pl.when(step == chunks - 1)
+    def _():
+        nr, rr = rms(resid[...])
+        da2 = acc[...]
+        d_two[...] = jnp.sum(da2 * nr, axis=0, keepdims=True)
+        dresid[...] = dy[...] + rms_back(nr, rr, gain_two[...] * da2)
+        acc[...] = jnp.zeros_like(acc)
+        dz[...] = dresid[...].astype(BF16)
+
+    @pl.when(step >= chunks)
+    def _():
+        don[...] = nt(dz[...], wout[...])
+        mixer_bwd_kernel(
+            blocks, rows_mb, step - chunks, *mixer[:12], don, *mixer[12:], dpq, dpk, dpv, dpg, dbeta, dtq,
+            dtk, dtv, d_gain,
+        )
+        for dp, w, out in ((dpq, wq, dwq), (dpk, wk, dwk), (dpv, wv, dwv), (dpg, wg, dwg)):
+            acc[...] += nt(dp[...], w[...])
+            out[...] = tn(a1[...], dp[...]).astype(BF16)
+        dw_out[...] = tn(on[...], dz[...]).astype(BF16)
+
+    @pl.when(step == chunks + pairs - 1)
+    def _():
+        d_beta = dbeta[...].astype(BF16)
+        grad = acc[...] + nt(d_beta, wbeta[...])
+        d_wbeta[...] = tn(a1[...], d_beta)
+        nx, rx = rms(x[...])
+        d_one[...] = jnp.sum(grad * nx, axis=0, keepdims=True)
+        dx[...] = (dresid[...] + rms_back(nx, rx, gain_one[...] * grad)).astype(BF16)
+
+    ready = {pieces[n][1] // (2 * CHUNK) + pieces[n][2] // (2 * CHUNK) - 1: n for n in (1, 2)}
+    plan = {}
+    for s, n in ready.items():
+        plan.setdefault(s, []).append((net.pair, n))
+    tail = range(chunks - 1, chunks + pairs)
+    plan.setdefault(3, []).append((net.launch, 0, 0))
+    for place, s in enumerate(tail):
+        for n in range(3):
+            k = place + 1 - n
+            if (k, n) != (0, 0) and 0 <= k < net.stages:
+                plan.setdefault(s, []).append((net.launch, k, n))
+            elif k == net.stages:
+                plan.setdefault(s, []).append((net.finish, n, write))
+    last = tail[-1]
+    for place in range(len(tail), net.stages + 3):
+        for n in range(3):
+            k = place + 1 - n
+            if 0 <= k < net.stages:
+                plan[last].append((net.launch, k, n))
+            elif k == net.stages:
+                plan[last].append((net.finish, n, write))
+    for s, actions in plan.items():
+
+        @pl.when(step == s)
+        def _(actions=actions, s=s):
+            for act, *args in actions:
+                result = act(*args)
+                if act == net.pair:
+                    result.start()
+            if s == last:
+                for n in range(3):
+                    net.end(n)
+
+
+def backward(
+    d_down, df, a2, gu, wgu, wdown, dy, resid, gain_two, wout, win, a1, on, x, gain_one, wbeta, proj,
+    beta_pre, taps, gain, mask, segc, segr, saved, blocks, shards, collective_id,
+):
+    rows = x.shape[0]
+    rows_mb = rows // blocks
+    width = PAIR * HEAD_DIM
+    chunks, pairs = FF // CHUNK, HEADS // PAIR
+    anywhere = pl.BlockSpec(memory_space=pl.ANY)
+    full = lambda shape: pl.BlockSpec(shape, lambda s: (0,) * len(shape))
+    early = lambda s: jnp.minimum(s, chunks - 1)
+    late = lambda s: jnp.maximum(s - chunks, 0)
+    lane_e = lambda r, w, off=0: pl.BlockSpec((r, w), lambda s: (0, off + early(s)))
+    lane_l = lambda r, w, off=0: pl.BlockSpec((r, w), lambda s: (0, off + late(s)))
+    wide_l = lambda off=0: pl.BlockSpec(
+        (D, width), lambda s: (0, off + late(s)), pipeline_mode=pl.Buffered(1)
+    )
+    row_l = lambda r, w: pl.BlockSpec((r, w), lambda s: (late(s), 0))
+    mat = pl.BlockSpec(
+        (PAIR, blocks, rows_mb, rows_mb), lambda s: (late(s), 0, 0, 0), pipeline_mode=pl.Buffered(1)
+    )
+    part_l = pl.BlockSpec(
+        (rows, width), lambda s: (0, late(s)), pipeline_mode=pl.Buffered(1)
+    )
+    per = D // width
+    tap = lambda k: lane_l(CONV, width, k * per)
+    r_down, r_gu = FF // shards, D // shards
+    a, b = chunks // 2 * 2 * CHUNK, 2 * FF
+    pieces = [(0, 0, D), (1, 0, a), (1, a, b - a)]
+    f32 = lambda *shape: jax.ShapeDtypeStruct(shape, F32)
+    bf = lambda *shape: jax.ShapeDtypeStruct(shape, BF16)
+    square = bf(D, D)
+    vm = pltpu.VMEM
     return pl.pallas_call(
-        functools.partial(mixer_fwd_kernel, blocks, rows_mb),
-        grid=(HEADS // PAIR,),
-        in_specs=ins,
-        out_specs=[one, one, mat, mat, mat, mat],
+        functools.partial(backward_kernel, shards, blocks, rows_mb, pieces),
+        grid=(chunks + pairs,),
+        in_specs=[
+            anywhere, full((rows, D)), full((rows, D)), lane_e(rows, CHUNK),
+            lane_e(rows, CHUNK, chunks), lane_e(D, CHUNK), lane_e(D, CHUNK, chunks),
+            pl.BlockSpec((CHUNK, D), lambda s: (early(s), 0)), full((rows, D)), full((rows, D)),
+            full((1, D)), row_l(width, D), wide_l(), wide_l(per), wide_l(2 * per),
+            wide_l(3 * per), full((rows, D)),
+            lane_l(rows, width), full((rows, D)), full((1, D)), full((D, HEADS)),
+            part_l, part_l, part_l, part_l, full((rows, HEADS)), tap(0), tap(1), tap(2), full((1, HEAD_DIM)), full((rows, 8)),
+            full((rows, 1)), full((1, rows)), lane_l(rows, width), mat, mat, mat, mat,
+        ],
+        out_specs=[
+            full((r_down, D)), full((r_gu, 2 * FF)), wide_l(), wide_l(), wide_l(), wide_l(),
+            row_l(width, D), full((D, HEADS)), full((rows, D)),
+            full((1, D)), full((1, D)), lane_l(CONV, width), lane_l(CONV, width),
+            lane_l(CONV, width), full((1, HEAD_DIM)),
+        ],
         out_shape=[
-            jax.ShapeDtypeStruct((rows, D), BF16),
-            jax.ShapeDtypeStruct((rows, D), F32),
-            square, square, square, square,
+            f32(r_down, D), f32(r_gu, 2 * FF), square, square, square, square, square,
+            f32(D, HEADS), bf(rows, D), f32(1, D), f32(1, D), f32(CONV, D), f32(CONV, D),
+            f32(CONV, D), f32(1, HEAD_DIM),
         ],
-        compiler_params=pltpu.CompilerParams(vmem_limit_bytes=48 << 20),
-        name="mixer_fwd",
-    )(proj, proj, proj, proj, beta_pre, taps, taps, taps, gain, mask, segc, segr)
-
-
-def mixer_backward(proj, beta_pre, taps, gain, mask, segc, segr, don, saved, blocks):
-    rows = proj.shape[0]
-    rows_mb = rows // blocks
-    ins, mat, one, otap, full = mixer_specs(rows, blocks, rows_mb)
-    tapshape = jax.ShapeDtypeStruct((CONV, D), F32)
-    wide = jax.ShapeDtypeStruct((rows, D), BF16)
-    return pl.pallas_call(
-        functools.partial(mixer_bwd_kernel, blocks, rows_mb),
-        grid=(HEADS // PAIR,),
-        in_specs=ins + [one, one, mat, mat, mat, mat],
-        out_specs=[one, one, one, one, full((rows, HEADS)), otap, otap, otap, full((1, HEAD_DIM))],
-        out_shape=[
-            wide, wide, wide, wide,
-            jax.ShapeDtypeStruct((rows, HEADS), F32),
-            tapshape, tapshape, tapshape,
-            jax.ShapeDtypeStruct((1, HEAD_DIM), F32),
-        ],
-        compiler_params=pltpu.CompilerParams(vmem_limit_bytes=48 << 20),
-        name="mixer_bwd",
-    )(proj, proj, proj, proj, beta_pre, taps, taps, taps, gain, mask, segc, segr, don, *saved)
+        scratch_shapes=[
+            vm((shards // 2, r_down, D), BF16), vm((shards // 2, 2, r_gu, 2 * FF), BF16),
+            vm((rows, D), F32), vm((rows, D), F32), vm((rows, D), BF16), vm((rows, width), F32),
+            vm((rows, width), BF16), vm((rows, width), BF16), vm((rows, width), BF16),
+            vm((rows, width), BF16), vm((rows, HEADS), F32),
+            pltpu.SemaphoreType.DMA,
+        ] + Scatter.semaphores(shards, 3) + Scatter.buffers(shards, [(r_down, D), (r_gu, 2 * FF)]),
+        compiler_params=pltpu.CompilerParams(
+            collective_id=collective_id, has_side_effects=True, vmem_limit_bytes=60 << 20
+        ),
+        name="backward",
+    )(d_down.reshape(shards // 2, 2, r_down, D), df, a2, gu, gu, wgu, wgu, wdown, dy, resid, gain_two,
+      wout, win, win, win, win, a1, on, x, gain_one, wbeta, *proj, beta_pre, taps, taps, taps, gain,
+      mask, segc, segr, *saved)
+
+
+def scatter_kernel(shards, count, *refs):
+    grads, sent, out, got = refs[:count], refs[count], refs[count + 1 : 2 * count + 1], refs[2 * count + 1]
+    refs = refs[2 * count + 2 :]
+    mine, refs = refs[:count], refs[count:]
+    sems, (keep, *back_sems), buffers = refs[:4], refs[4:8], refs[8:]
+    me = lin_index()
+    core = lax.rem(me, 2)
+    back = Exchange(shards, me, sent, got, *back_sems)
+    other, coming = Scatter.split(shards, count, buffers)
+    pieces = [(i, 0, g.shape[-1]) for i, g in enumerate(grads)]
+
+    def kept(n):
+        return pltpu.make_async_copy(grads[n].at[:, core], mine[n], keep.at[n])
+
+    net = Scatter(
+        shards, me, pieces, lambda n, parity: grads[n].at[:, parity],
+        lambda i, q, cols: mine[i][q, :, cols], other, coming, sems, kept,
+    )
+
+    def write(i, at, size, value):
+        out[i][:, pl.ds(at, size)] = value
+
+    for n in range(count):
+        kept(n).start()
+    meet(shards, me, True)
+    for n in range(count):
+        net.pair(n).start()
+    back.start()
+    for t in range(count + net.stages):
+        for n in range(count):
+            k = t - n
+            if 0 <= k < net.stages:
+                net.launch(k, n)
+            elif k == net.stages:
+                net.finish(n, write)
+    back.wait()
+    for n in range(count):
+        net.end(n)
+
+
+def scatter(grads, message, shards, collective_id):
+    count = len(grads)
+    shapes = [(g.shape[0] // shards, g.shape[1]) for g in grads]
+    anywhere = pl.BlockSpec(memory_space=pl.ANY)
+    dma = pltpu.SemaphoreType.DMA
+    *out, got = pl.pallas_call(
+        functools.partial(scatter_kernel, shards, count),
+        in_specs=[anywhere] * (count + 1),
+        out_specs=[pl.BlockSpec(memory_space=pltpu.VMEM)] * count + [anywhere],
+        out_shape=[jax.ShapeDtypeStruct(s, F32) for s in shapes]
+        + [jax.ShapeDtypeStruct(message.shape, message.dtype)],
+        scratch_shapes=[pltpu.VMEM((shards // 2,) + s, BF16) for s in shapes]
+        + Scatter.semaphores(shards, count) + [dma((count,)), dma, dma, dma]
+        + Scatter.buffers(shards, shapes),
+        compiler_params=pltpu.CompilerParams(
+            collective_id=collective_id, has_side_effects=True, vmem_limit_bytes=60 << 20
+        ),
+        name="scatter_last",
+    )(*[g.reshape((shards // 2, 2) + s) for g, s in zip(grads, shapes)], message)
+    return out, got
 
 
 def nt(left, right):
@@ -330,23 +966,20 @@
         [conv_kernel.reshape(-1), w_beta.reshape(-1), norm_gain, ffn_gain,
          jnp.zeros((share * 128 - small,), BF16)]
     ).reshape(1, share, 128)
-    sorted_rows = nn(sort, jnp.concatenate([tokens, cotangent, teacher, notes], axis=1)).astype(BF16)
+    sorted_rows = nn(sort, jnp.concatenate([tokens, notes], axis=1)).astype(BF16)
     message = jnp.concatenate(
         [sorted_rows.reshape(shards, share, -1), jnp.broadcast_to(packed, (shards, share, 128))],
         axis=2,
     )
-    arrived = lax.all_to_all(message, AXES, split_axis=0, concat_axis=0, tiled=True)
-
-    win = lax.all_gather(w_in, AXES, axis=0, tiled=True)
-    wout = lax.all_gather(w_out, AXES, axis=0, tiled=True)
-    wgu = lax.all_gather(w_gu, AXES, axis=0, tiled=True)
-    wdown = lax.all_gather(w_down, AXES, axis=0, tiled=True)
+    later = nn(sort, jnp.concatenate([cotangent, teacher], axis=1)).astype(BF16)
+    later = later.reshape(shards, share, 2 * D)
+    (win, wout), arrived = first([w_in, w_out], (2, 1), message, shards, 0)
 
     flat = arrived.reshape(rows, -1)
-    info = flat[:, 3 * D : 3 * D + 128].astype(F32)
+    info = flat[:, D : D + 128].astype(F32)
     place = info[:, 1].astype(jnp.int32)
-    counted = jnp.sum(arrived[:, 0, 3 * D + 2].astype(F32))
-    extra = arrived[:, :, 3 * D + 128 :].reshape(shards, share * 128)
+    counted = jnp.sum(arrived[:, 0, D + 2].astype(F32))
+    extra = arrived[:, :, D + 128 :].reshape(shards, share * 128)
     a, b, c = CONV * conv_kernel.shape[1], w_beta.shape[0] * HEADS, norm_gain.shape[0]
     taps = extra[:, :a].reshape(shards, CONV, -1).swapaxes(0, 1).reshape(CONV, 3 * D).astype(F32)
     wbeta = extra[:, a : a + b].reshape(D, HEADS)
@@ -354,11 +987,9 @@
     gain_two = extra[:, a + b + c : a + b + 2 * c].reshape(D).astype(F32)
     deal = (place[None, :] == jnp.arange(rows)[:, None]).astype(BF16)
     deal_t = (place[:, None] == jnp.arange(rows)[None, :]).astype(BF16)
-    dealt = nn(deal, flat[:, : 3 * D + 128])
+    dealt = nn(deal, flat[:, : D + 128])
     x = dealt[:, :D]
-    g = dealt[:, D : 2 * D]
-    t = dealt[:, 2 * D : 3 * D]
-    m = dealt[:, 3 * D : 3 * D + 1]
+    m = dealt[:, D : D + 1]
 
     ends = jnp.cumsum(lengths, axis=1)
     within = jnp.arange(rows_mb, dtype=jnp.int32)
@@ -376,49 +1007,35 @@
 
     nx, rx = rms(x)
     a1 = (nx * gain_one).astype(BF16)
-    proj = nn(a1, win)
-    beta_pre = nn(a1, wbeta)
-    on, *saved = mixer_forward(proj, beta_pre, taps, gain_out, mask, segc, segr, blocks)
-    resid = x + nn(on, wout)
-    nr, rr = rms(resid)
-    a2 = (nr * gain_two).astype(BF16)
+    wdown, wgu, later, (*proj, beta_pre, on, o, ainv, u, p, l, resid, a2) = forward(
+        w_down, w_gu, later, (1, 2), a1, win, wout, wbeta, x, gain_two[None, :], taps, gain_out, mask, segc,
+        segr, blocks, shards, 2,
+    )
+    saved = (o, ainv, u, p, l)
+    later = nn(deal, later.reshape(rows, 2 * D))
+    g, t = later[:, :D], later[:, D:]
     gu = nn(a2, wgu)
     gate, up = gu[:, :FF], gu[:, FF:]
-    sg = sigmoid(gate)
-    hid = (gate * sg * up).astype(BF16)
+    hid = (gate * sigmoid(gate) * up).astype(BF16)
     y = resid + nn(hid, wdown)
     errors = y - t
     loss_part = jnp.sum(m * errors * errors)
     dy = g + (rows * shards / counted) * m * errors
     df = dy.astype(BF16)
-    dhid = nt(df, wdown)
-    dgu = jnp.concatenate(
-        [dhid * up * (sg * (1.0 + gate * (1.0 - sg))), dhid * (gate * sg)], axis=1
-    ).astype(BF16)
-    da2 = nt(dgu, wgu)
-    d_gain_two = jnp.sum(da2 * nr, axis=0)
-    dresid = dy + rms_back(nr, rr, gain_two * da2)
-    dz = dresid.astype(BF16)
-    don = nt(dz, wout)
-    dpq, dpk, dpv, dpg, dbeta, dtq, dtk, dtv, d_gain_out = mixer_backward(
-        proj, beta_pre, taps, gain_out, mask, segc, segr, don, saved, blocks
-    )
-    dproj = jnp.concatenate([dpq, dpk, dpv, dpg], axis=1)
-    dbeta = dbeta.astype(BF16)
-    da1 = nt(dproj, win) + nt(dbeta, wbeta)
-    d_gain_one = jnp.sum(da1 * nx, axis=0)
-    dx = dresid + rms_back(nx, rx, gain_one * da1)
-
-    def scatter(v):
-        return lax.psum_scatter(v, AXES, scatter_dimension=0, tiled=True).astype(F32)
-
-    g_gu = scatter(tn(a2, dgu).astype(BF16))
-    g_down = scatter(tn(hid, df).astype(BF16))
-    g_in = scatter(tn(a1, dproj).astype(BF16))
-    g_out = scatter(tn(on, dz).astype(BF16))
+    (g_down, g_gu, dwq, dwk, dwv, dwg, dw_out, d_wbeta, dx, d_gain_two, d_gain_one, dtq, dtk, dtv,
+     d_gain_out) = backward(
+        tn(hid, df, BF16), df, a2, gu, wgu, wdown, dy, resid, gain_two[None, :], wout, win, a1, on, x,
+        gain_one[None, :], wbeta, proj, beta_pre, taps, gain_out, mask, segc, segr, saved, blocks, shards,
+        1,
+    )
+    back = jnp.concatenate([y.astype(BF16), dx], axis=1)
+    back = nn(deal_t, back).astype(BF16).reshape(shards, share, 2 * D)
+    (g_out, *g_in), back = scatter([dw_out, dwq, dwk, dwv, dwg], back, shards, 3)
+    g_in = jnp.concatenate(g_in, axis=1)
+    back = nn(sort_t, back.reshape(rows, 2 * D)).astype(BF16)
+    output, input_grad = back[:, :D], back[:, D:]
 
     d_taps = jnp.concatenate([dtq, dtk, dtv], axis=1)
-    d_wbeta = tn(a1, dbeta)
     tail = jnp.concatenate([d_gain_out.reshape(-1), loss_part.reshape(1)])
     extra = jnp.concatenate(
         [
@@ -445,13 +1062,6 @@
     g_gain_out = summed[a + b + 2 * c : a + b + 2 * c + HEAD_DIM]
     loss = summed[a + b + 2 * c + HEAD_DIM] / (D * counted)
 
-    def give_back(v):
-        sent = nn(deal_t, v.astype(BF16)).astype(BF16).reshape(shards, share, D)
-        got = lax.all_to_all(sent, AXES, split_axis=0, concat_axis=0, tiled=True)
-        return nn(sort_t, got.reshape(rows, D)).astype(BF16)
-
-    output = give_back(y)
-    input_grad = give_back(dx)
     return (
         output, input_grad, g_in, g_beta, g_taps, g_out, g_gain_one, g_gain_out, g_gain_two, g_gu,
         g_down, loss,

time: 940 us -> 419 us (0.45)
  waiting for transfers between devices: 746 us -> 0.01 us
  Pallas kernels: 40.2 us -> 344 us
  matrix products: 79.5 us -> 26.8 us
  between operations: 17.8 us -> 4.35 us
  starting transfers between devices: 17.2 us -> 6.99 us
    reduce_scatter x4 -> x0, waiting for transfers between devices: 469 us -> none  [scatter(): lax.psum_scatter(v, AXES, scatter_dimension=0, tiled=True).astype(F32)]
    pallas_call x2 -> x4, Pallas kernels: 40.2 us -> 344 us  [the longest x1 104 us: forward(): pl.pallas_call(functools.partial(forward_kernel, shards, pieces, blocks,...]
    all_gather x4 -> x0, waiting for transfers between devices: 192 us -> none  [the longest x1 89.3 us: local(): wgu = lax.all_gather(w_gu, AXES, axis=0, tiled=True)]
    all_to_all x3 -> x0, waiting for transfers between devices: 76.2 us -> none  [the longest x1 51.7 us: local(): lax.all_to_all(message, AXES, split_axis=0, concat_axis=0, tiled=True)]
    dot_general x5 -> x0, matrix products: 23.1 us -> none  [nt(): lax.dot_general(left, right, (((1,), (1,)), ((), ())), preferred_element_...]
    dot_general x5 -> x1, matrix products: 21.9 us -> 4.19 us  [tn(): lax.dot_general(left, right, (((0,), (0,)), ((), ())), preferred_element_...]
    all_to_all x3 -> x0, starting transfers between devices: 13.2 us -> none  [the longest x1 7.3 us: local(): lax.all_to_all(message, AXES, split_axis=0, concat_axis=0, tiled=True)]
    dot_general x11 -> x8, matrix products: 34.6 us -> 22.6 us  [nn(): return jnp.dot(left, right, preferred_element_type=F32)]
  transfers between devices with their start and end apart: 12 -> 1, of which waited for: 12 -> 0; matrix products, arithmetic and copies ran while one was open for 9% -> 1% of each run, Pallas kernels for 4% -> 18%
where the time goes in v2:
time: 419 us; the launch traced here: 418 us
  Pallas kernels  344 us (82%)
  matrix products  26.8 us (6%)
  local copies, waits for them, and re-layouts  18.6 us (4%)
  other arithmetic  16.9 us (4%)
  starting transfers between devices  6.99 us (2%)
  between operations  4.35 us (1%)
    pallas_call x1, Pallas kernels, forward(): pl.pallas_call(functools.partial(forward_kernel, shards, pieces, blocks,...  104 us
    pallas_call x1, Pallas kernels, backward(): pl.pallas_call(functools.partial(backward_kernel, shards, blocks, rows_mb...  94.5 us
    pallas_call x1, Pallas kernels, scatter(): pl.pallas_call(functools.partial(scatter_kernel, shards, count), in_specs...  73.1 us
    pallas_call x1, Pallas kernels, first(): pl.pallas_call(functools.partial(first_kernel, shards, pieces), in_specs=...  73.1 us
    dot_general x8, matrix products, nn(): return jnp.dot(left, right, preferred_element_type=F32)  22.6 us
  transfers between devices with their start and end apart: 1, of which 0 were waited for; matrix products, arithmetic and copies ran while one was open for 1% of the time, Pallas kernels for 18%

profile of v2, /device:TPU:0, one launch (start us, length us, event | category | flops | bytes accessed | tf_op | source)
XLA Modules:
  0.0 417.9 jit_solution(9748666909834020055)
XLA Ops:
  2.6 1.3 convert_reduce_fusion.2
  7.8 1.4 fusion.2
  9.2 1.4 concatenate.74
  11.6 73.1 %gather_first.1 = (bf16[16,2,32,4096]{3,2,1,0:T(8,128)(2,1)}, bf16[16,2,32,1024]{3,2,1,0:T(8,128)(2,1)}, bf16[32,8,1280]{2,1,0:T(8,128)(2,1)}) custom-call(bf16[32,4096]{1,0:T(8,128)(2,1)} %refs_0_.1, bf16[32,1024]{1,0:T(8,128)(2,1)} %refs_1_.1, bf16[32,8,1280]{2,1,0:T(8,128)(2,1)} %pad_maximum_fusion.refs_2_), custom_call_target="tpu_custom_call" | custom-call | tf_op jit(solution)/shard_map/gather_first/pallas_call | solution.py:461
  85.6 1.6 convert_reduce_fusion.1
  90.0 1.4 fusion.14
  92.4 1.1 fusion.32
  93.5 1.4 fusion.1.sent
  95.0 103.6 %mixer_forward.1 = (bf16[16,2,88,1024]{3,2,1,0:T(8,128)(2,1)}, bf16[16,2,32,5632]{3,2,1,0:T(8,128)(2,1)}, bf16[32,8,2048]{2,1,0:T(8,128)(2,1)S(1)}, f32[256,1024...) custom-call(bf16[88,1024]{1,0:T(8,128)(2,1)S(1)} %copy-done.10, ...), custom_call_target="tpu_custom_call" | custom-call | tf_op jit(solution)/shard_map/mixer_forward/pallas_call | solution.py:534
  198.7 2.1 fusion.12
  200.8 6.2 %fusion.35.refs_3_.refs_4_ = f32[256,5632]{1,0:T(8,128)S(1)} fusion(bf16[256,1024]{1,0:T(8,128)(2,1)S(1)} %get-tuple-element.55.refs_2_, bf16[1024,5632]{1,0:T(8,128)(2,1)} %bitcast.73), kind=kOutput, calls=%fused_computation.88 | convolution fusion | flops 2952790016 | bytes 17825792 | tf_op jit(solution)/shard_map/dot_general | solution.py:927
  207.1 2.5 copy-done.15
  211.3 6.9 %fusion.31 = (bf16[256,1024]{1,0:T(8,128)(2,1)S(1)}, f32[256,1024]{1,0:T(8,128)}, f32[]{:T(128)}, bf16[256,1024]{1,0:T(8,128)(2,1)S(1)}) fusion(f32[256,2048]{1,0:T(8,128)} %fusion.12, f32[256]{0:T(256)S(1)} %get-tuple-element.129, f32[256]{0:T(256)S(1)} %get-tuple-element.128, f32[256,1024]{1,0:T(8,128)} %get-tuple-element.58.refs_9_, ...), kind=kOutput, calls=%fused_computation.84 | convolution fusion | flops 1478754304 | bytes 12453892 | tf_op jit(solution)/shard_map/dot_general | solution.py:927
  218.2 4.2 %fusion.36 = bf16[2816,1024]{1,0:T(8,128)(2,1)} fusion(bf16[256,2816]{1,0:T(8,128)(2,1)S(1)} %fusion, bf16[256,1024]{1,0:T(8,128)(2,1)S(1)} %get-tuple-element.130.refs_1_), kind=kOutput, calls=%fused_computation.89 | convolution fusion | flops 1476395008 | bytes 7733248 | tf_op jit(solution)/shard_map/dot_general | solution.py:923
  222.4 94.5 %backward.1 = (f32[88,1024]{1,0:T(8,128)}, f32[32,5632]{1,0:T(8,128)}, bf16[1024,1024]{1,0:T(8,128)(2,1)}, bf16[1024,1024]{1,0:T(8,128)(2,1)}, bf16[1024,1024]{1...) custom-call(bf16[16,2,88,1024]{3,2,1,0:T(8,128)(2,1)} %bitcast.76, ...), custom_call_target="tpu_custom_call" | custom-call | tf_op jit(solution)/shard_map/backward/pallas_call | solution.py:816
  318.0 1.3 reshape.421
  319.8 1.3 reduce.11
  321.2 1.3 reduce.12
  322.6 1.3 pad_maximum_fusion.3
  324.7 7.0 %all-to-all-start = ((f32[32,7,128]{2,1,0:T(8,128)}), f32[32,7,128]{2,1,0:T(8,128)S(1)}, u32[]{:S(2)}, u32[]{:S(2)}) async-start(f32[32,7,128]{2,1,0:T(8,128)} %reshape.426), calls=%async_computation | async-start | bytes 262144 | tf_op jit(solution)/shard_map/all_to_all | solution.py:1053
  332.3 1.5 fusion.3.refs_5_
  333.8 73.1 %scatter_last.1 = (f32[32,1024]{1,0:T(8,128)}, f32[32,1024]{1,0:T(8,128)}, f32[32,1024]{1,0:T(8,128)}, f32[32,1024]{1,0:T(8,128)}, f32[32,1024]{1,0:T(8,128)}, /*index=5*/bf16[32,8,2048]{2,1,0:T(8,128)(2,1)}) custom-call(bf16[16,2,32,1024]{3,2,1,0:T(8,128)(2,1)} %bitcast.85, bf16[16,2,32,1024]{3,2,1,0:T(8,128)(2,1)} %bitcast.81, ...), custom_call_target="tpu_custom_call" | custom-call | tf_op jit(solution)/shard_map/scatter_last/pallas_call | solution.py:901
  407.0 1.8 convolution_convert_fusion
  409.6 1.0 fusion.33
  (127 shorter events, 21.3 us)
Async XLA Ops:
  2.6 92.4 %copy-start.13 = (s32[2,128]{1,0:T(2,128)}, s32[2,128]{1,0:T(2,128)S(1)}, u32[]{:S(2)}) copy-start(s32[2,128]{1,0:T(2,128)S(1)} %broadcast_add_fusion) | copy-start | bytes 3076
  85.6 6.7 %copy-start.27 = (bf16[128]{0:T(256)(128)(2,1)S(1)}, bf16[128]{0:T(256)(128)(2,1)}, u32[]{:S(2)}) copy-start(bf16[128]{0:T(256)(128)(2,1)} %param.26) | copy-start | bytes 772
  88.0 6.9 %copy-start.4 = (s32[256,1]{1,0:T(8,128)}, s32[256,1]{1,0:T(8,128)S(1)}, u32[]{:S(2)}) copy-start(s32[256,1]{1,0:T(8,128)S(1)} %copy.58.segc.refs_31_) | copy-start | bytes 3076
  89.0 6.0 %copy-start.5 = (f32[256,8]{1,0:T(8,128)}, f32[256,8]{1,0:T(8,128)S(1)}, u32[]{:S(2)}) copy-start(f32[256,8]{1,0:T(8,128)S(1)} %copy.57.mask.refs_30_) | copy-start | bytes 24580
  91.5 2.0 copy-start.18
  91.7 3.2 copy-start.12
  92.1 2.9 copy-start.2
  92.3 2.6 copy-start.1
  92.4 2.6 copy-start.14
  92.4 2.6 copy-start.9
  92.4 2.6 copy-start.10
  93.5 105.1 %copy-start = (bf16[256,1024]{1,0:T(8,128)(2,1)}, bf16[256,1024]{1,0:T(8,128)(2,1)S(1)}, u32[]{:S(2)}) copy-start(bf16[256,1024]{1,0:T(8,128)(2,1)S(1)} %get-tuple-element.134.a1.refs_16_) | copy-start | bytes 1572868
  198.6 8.4 %copy-start.3 = (bf16[256,1024]{1,0:T(8,128)(2,1)}, bf16[256,1024]{1,0:T(8,128)(2,1)S(1)}, u32[]{:S(2)}) copy-start(bf16[256,1024]{1,0:T(8,128)(2,1)S(1)} %get-tuple-element.55.refs_2_) | copy-start | bytes 1572868
  198.7 8.4 %copy-start.6 = (f32[256,1024]{1,0:T(8,128)}, f32[256,1024]{1,0:T(8,128)S(1)}, u32[]{:S(2)}) copy-start(f32[256,1024]{1,0:T(8,128)S(1)} %get-tuple-element.61.refs_21_) | copy-start | bytes 3145732
  198.7 8.4 %copy-start.7 = (f32[256,1024]{1,0:T(8,128)}, f32[256,1024]{1,0:T(8,128)S(1)}, u32[]{:S(2)}) copy-start(f32[256,1024]{1,0:T(8,128)S(1)} %get-tuple-element.62.refs_22_) | copy-start | bytes 3145732
  198.7 8.4 %copy-start.8 = (bf16[256,1024]{1,0:T(8,128)(2,1)}, bf16[256,1024]{1,0:T(8,128)(2,1)S(1)}, u32[]{:S(2)}) copy-start(bf16[256,1024]{1,0:T(8,128)(2,1)S(1)} %get-tuple-element.60.refs_17_) | copy-start | bytes 1572868
  198.7 8.4 %copy-start.11 = (f32[256,8]{1,0:T(8,128)}, f32[256,8]{1,0:T(8,128)S(1)}, u32[]{:S(2)}) copy-start(f32[256,8]{1,0:T(8,128)S(1)} %get-tuple-element.65.refs_25_) | copy-start | bytes 24580
  207.1 2.5 copy-start.15
  218.2 4.2 %copy-start.16 = (bf16[256,1024]{1,0:T(8,128)(2,1)}, bf16[256,1024]{1,0:T(8,128)(2,1)S(1)}, u32[]{:S(2)}) copy-start(bf16[256,1024]{1,0:T(8,128)(2,1)S(1)} %get-tuple-element.130.refs_1_) | copy-start | bytes 1572868
  316.9 15.4 %copy-start.20 = (bf16[256,1024]{1,0:T(8,128)(2,1)S(1)}, bf16[256,1024]{1,0:T(8,128)(2,1)}, u32[]{:S(2)}) copy-start(bf16[256,1024]{1,0:T(8,128)(2,1)} %get-tuple-element.76) | copy-start | bytes 1572868
  324.7 86.0 %all-to-all-start = ((f32[32,7,128]{2,1,0:T(8,128)}), f32[32,7,128]{2,1,0:T(8,128)S(1)}, u32[]{:S(2)}, u32[]{:S(2)}) async-start(f32[32,7,128]{2,1,0:T(8,128)} %reshape.426), calls=%async_computation | async-start | bytes 262144 | tf_op jit(solution)/shard_map/all_to_all | solution.py:1053
  408.7 5.8 %copy-start.22 = (f32[32,1024]{1,0:T(8,128)S(1)}, f32[32,1024]{1,0:T(8,128)}, u32[]{:S(2)}) copy-start(f32[32,1024]{1,0:T(8,128)} %get-tuple-element.167) | copy-start | bytes 393220
  408.7 6.5 %copy-start.17 = (f32[32,5632]{1,0:T(8,128)S(1)}, f32[32,5632]{1,0:T(8,128)}, u32[]{:S(2)}) copy-start(f32[32,5632]{1,0:T(8,128)} %get-tuple-element.171) | copy-start | bytes 2162692
  409.6 6.5 %copy-start.21 = (f32[88,1024]{1,0:T(8,128)S(1)}, f32[88,1024]{1,0:T(8,128)}, u32[]{:S(2)}) copy-start(f32[88,1024]{1,0:T(8,128)} %get-tuple-element.172) | copy-start | bytes 1081348
  (5 other events, 9.3 us)

commit v3 on v2

--- a/solution.py
+++ b/solution.py
@@ -246,67 +246,72 @@
     return (lax.div(index, inner), lax.rem(index, inner))
 
 
-def flip(me, bits, number, always=()):
-    result = me
-    for bit in always:
-        own = lax.rem(lax.div(me, 1 << bit), 2)
-        result = result + (1 - 2 * own) * (1 << bit)
-    for i, bit in enumerate(reversed(bits)):
-        own = lax.rem(lax.div(me, 1 << bit), 2)
-        if isinstance(number, int):
-            flag = (number >> i) & 1
-            if flag == 0:
-                continue
-        else:
-            flag = lax.rem(lax.div(number, 1 << i), 2)
-        result = result + flag * (1 - 2 * own) * (1 << bit)
-    return result
+class Here:
+    def __init__(self, shards):
+        self.shards, self.me = shards, lin_index()
+        self.bits = shards.bit_length() - 1
+        own = [lax.rem(lax.div(self.me, 1 << b), 2) for b in range(self.bits)]
+        self.core = own[0]
+        self.change = [(1 - 2 * o) * (1 << b) for b, o in enumerate(own)]
+        self.partner = [mesh_id(self.me + c) for c in self.change]
+
+    def flip(self, bits, number, always=()):
+        result = self.me
+        for bit in always:
+            result = result + self.change[bit]
+        for i, bit in enumerate(reversed(bits)):
+            if isinstance(number, int):
+                if (number >> i) & 1:
+                    result = result + self.change[bit]
+            else:
+                result = result + lax.rem(lax.div(number, 1 << i), 2) * self.change[bit]
+        return result
 
 
 def routes(shards):
     bits = shards.bit_length() - 1
     rest = list(range(4, bits))
-    return [[1, 3, 2] + rest, [2, 1, 3] + rest, [3, 2, 1] + rest]
+    return [[1, 2, 3] + rest, [2, 3, 1] + rest, [3, 1, 2] + rest]
 
 
 def colours(width, turn):
     tiles = width // 128
-    sizes = [tiles // 3 + (1 if (c - turn) % 3 < tiles % 3 else 0) for c in range(3)]
-    cuts, at = [], 0
-    for s in sizes:
-        cuts.append((at * 128, s * 128))
-        at += s
-    return cuts
-
-
-def meet(shards, me, everyone):
+    one, three = round(tiles * 0.36), round(tiles * 0.28)
+    sizes = (one, tiles - one - three, three)
+    return [(sum(sizes[:c]) * 128, sizes[c] * 128) for c in range(3)]
+
+
+def meet(here, everyone):
     barrier = pltpu.get_barrier_semaphore()
     if everyone:
 
         def greet(r, _):
-            pl.semaphore_signal(
-                barrier, inc=1, device_id=mesh_id(lax.rem(me + r, shards)), device_id_type=MESH
-            )
+            peer = lax.rem(here.me + r, here.shards)
+            pl.semaphore_signal(barrier, inc=1, device_id=mesh_id(peer), device_id_type=MESH)
             return 0
 
-        lax.fori_loop(1, shards, greet, 0)
-        pl.semaphore_wait(barrier, shards - 1)
+        lax.fori_loop(1, here.shards, greet, 0)
+        pl.semaphore_wait(barrier, here.shards - 1)
     else:
-        bits = shards.bit_length() - 1
-        for bit in range(bits):
-            pl.semaphore_signal(
-                barrier, inc=1, device_id=mesh_id(flip(me, [], 0, (bit,))), device_id_type=MESH
-            )
-        pl.semaphore_wait(barrier, bits)
+        for partner in here.partner:
+            pl.semaphore_signal(barrier, inc=1, device_id=partner, device_id_type=MESH)
+        pl.semaphore_wait(barrier, here.bits)
+
+
+def spread_order(shards):
+    bits = shards.bit_length() - 1
+    turned = [sum(((i >> b) & 1) << (bits - 1 - b) for b in range(bits)) for i in range(shards)]
+    return turned[1:]
 
 
 class Exchange:
-    def __init__(self, shards, me, sent, got, send, recv, keep):
-        self.shards, self.me, self.sent, self.got = shards, me, sent, got
+    def __init__(self, here, sent, got, send, recv, keep, same=False):
+        self.here, self.shards, self.me, self.got = here, here.shards, here.me, got
+        self.block = (lambda d: sent) if same else (lambda d: sent.at[d])
         self.send, self.recv, self.keep = send, recv, keep
 
     def own(self):
-        return pltpu.make_async_copy(self.sent.at[self.me], self.got.at[self.me], self.keep)
+        return pltpu.make_async_copy(self.block(self.me), self.got.at[self.me], self.keep)
 
     def start(self):
         self.own().start()
@@ -314,24 +319,37 @@
         def one(r, _):
             peer = lax.rem(self.me + r, self.shards)
             pltpu.make_async_remote_copy(
-                src_ref=self.sent.at[peer], dst_ref=self.got.at[self.me], send_sem=self.send,
+                src_ref=self.block(peer), dst_ref=self.got.at[self.me], send_sem=self.send,
                 recv_sem=self.recv, device_id=mesh_id(peer), device_id_type=MESH,
             ).start()
             return 0
 
         lax.fori_loop(1, self.shards, one, 0)
+
+    def start_part(self, part, parts):
+        others = self.shards - 1
+        if part == 0:
+            self.own().start()
+        for r in range(others * part // parts, others * (part + 1) // parts):
+            peer = lax.rem(self.me + spread_order(self.shards)[r], self.shards)
+            pltpu.make_async_remote_copy(
+                src_ref=self.block(peer), dst_ref=self.got.at[self.me], send_sem=self.send,
+                recv_sem=self.recv, device_id=mesh_id(peer), device_id_type=MESH,
+            ).start()
 
     def wait(self):
         self.own().wait()
         whole = pl.ds(0, self.shards - 1)
         pltpu.make_async_remote_copy(
-            src_ref=self.sent.at[whole], dst_ref=self.got.at[whole], send_sem=self.send,
-            recv_sem=self.recv, device_id=mesh_id(self.me), device_id_type=MESH,
+            src_ref=self.got.at[whole], dst_ref=self.got.at[whole], send_sem=self.send,
+            recv_sem=self.recv, device_id=self.here.partner[0], device_id_type=MESH,
         ).wait()
 
 
 DEAL_AT = 0
 CHUNK = 256
+X_STEPS = 5
+GT_FROM = 6
 
 
 def pieces_of(widths, split):
@@ -346,12 +364,12 @@
 
 
 class Gather:
-    def __init__(self, shards, me, pieces, own, full, sems):
-        self.me, self.pieces, self.own, self.full = me, pieces, own, full
+    def __init__(self, here, pieces, own, full, sems):
+        self.here, self.pieces, self.own, self.full = here, pieces, own, full
         self.send, self.recv, self.pair_send, self.pair_recv, self.keep = sems
-        self.stages = shards.bit_length() - 2
-        self.order = routes(shards)
-        self.core = lax.rem(me, 2)
+        self.stages = here.bits - 1
+        self.order = routes(here.shards)
+        self.core = here.core
         self.cuts = [
             [(at + a, s) for a, s in colours(size, n)] for n, (_, at, size) in enumerate(pieces)
         ]
@@ -366,7 +384,7 @@
 
     def kept(self, i):
         return pltpu.make_async_copy(
-            self.own[i], self.full[i].at[lax.div(self.me, 2), self.core], self.keep.at[i]
+            self.own[i], self.full[i].at[lax.div(self.here.me, 2), self.core], self.keep.at[i]
         )
 
     def begin(self):
@@ -374,7 +392,7 @@
             self.kept(i).start()
 
     def partner(self, k, c):
-        return mesh_id(flip(self.me, [], 0, (self.order[c][self.stages - 1 - k],)))
+        return self.here.partner[self.order[c][self.stages - 1 - k]]
 
     def group(self, k, n, c):
         at, size = self.cuts[n][c]
@@ -389,7 +407,7 @@
         some = self.full[i].at[:, self.core, :, pl.ds(at, size)]
         return pltpu.make_async_remote_copy(
             src_ref=some, dst_ref=some, send_sem=self.pair_send.at[n],
-            recv_sem=self.pair_recv.at[n], device_id=mesh_id(flip(self.me, [], 0, (0,))),
+            recv_sem=self.pair_recv.at[n], device_id=self.here.partner[0],
             device_id_type=MESH,
         )
 
@@ -401,7 +419,7 @@
                 self.group(k - 1, n, c).wait_recv()
             have = self.order[c][self.stages - k :]
             for j in range(1 << k):
-                d = flip(self.me, have, j)
+                d = self.here.flip(have, j)
                 there = self.full[i].at[lax.div(d, 2), self.core, :, pl.ds(at, size)]
                 pltpu.make_async_remote_copy(
                     src_ref=self.own[i].at[:, pl.ds(at, size)] if j == 0 else there,
@@ -416,32 +434,41 @@
             self.kept(self.pieces[n][0]).wait()
         self.half(n).start()
 
-    def step(self, t):
+    def slots(self, first, last):
+        return sum(
+            0 <= t - n <= self.stages for t in range(first, last) for n in range(len(self.pieces))
+        )
+
+    def step(self, t, between=None):
         for n in range(len(self.pieces)):
             k = t - n
             if 0 <= k < self.stages:
                 self.launch(k, n)
             elif k == self.stages:
                 self.finish(n)
-
-    def end(self):
+            if between is not None and 0 <= k <= self.stages:
+                between()
+
+    def end(self, arrived=0):
         for k in range(self.stages):
             for n in range(len(self.pieces)):
                 for c in range(3):
                     self.group(k, n, c).wait_send()
         for n in range(len(self.pieces)):
-            self.half(n).wait()
+            self.half(n).wait_send()
+            if n >= arrived:
+                self.half(n).wait_recv()
 
 
 def first_kernel(shards, pieces, *refs):
     count = 1 + max(i for i, _, _ in pieces)
     own, sent, full, got = refs[:count], refs[count], refs[count + 1 : 2 * count + 1], refs[2 * count + 1]
     sems = refs[2 * count + 2 :]
-    me = lin_index()
-    deal = Exchange(shards, me, sent, got, *sems[5:])
-    weights = Gather(shards, me, pieces, own, full, sems[:5])
+    here = Here(shards)
+    deal = Exchange(here, sent, got, *sems[5:])
+    weights = Gather(here, pieces, own, full, sems[:5])
     weights.begin()
-    meet(shards, me, True)
+    meet(here, True)
     deal.start()
     for t in range(weights.last + 1):
         weights.step(t)
@@ -480,14 +507,14 @@
 ):
     step = pl.program_id(0)
     steps = HEADS // PAIR
-    me = lin_index()
-    weights = Gather(shards, me, pieces, (own_down, own_gu), (full_down, full_gu), sems[:5])
-    deal = Exchange(shards, me, sent, got, *sems[5:])
+    here = Here(shards)
+    weights = Gather(here, pieces, (own_down, own_gu), (full_down, full_gu), sems[:5])
+    deal = Exchange(here, sent, got, *sems[5:])
 
     @pl.when(step == 0)
     def _():
         weights.begin()
-        meet(shards, me, True)
+        meet(here, True)
         weights.step(0)
         resid[...] = x[...]
 
@@ -558,13 +585,13 @@
 
 
 class Scatter:
-    def __init__(self, shards, me, pieces, whole, mine, other, coming, sems, kept):
-        self.me, self.pieces, self.whole, self.mine = me, pieces, whole, mine
+    def __init__(self, here, pieces, whole, mine, other, coming, sems, kept):
+        self.here, self.pieces, self.whole, self.mine = here, pieces, whole, mine
         self.other, self.coming, self.kept_of = other, coming, kept
         self.send, self.recv, self.pair_send, self.pair_recv = sems
-        self.stages = shards.bit_length() - 2
-        self.order = routes(shards)
-        self.core = lax.rem(me, 2)
+        self.stages = here.bits - 1
+        self.order = routes(here.shards)
+        self.core = here.core
         self.cuts = [
             [(at + a, s) for a, s in colours(size, n)] for n, (_, at, size) in enumerate(pieces)
         ]
@@ -592,7 +619,7 @@
         return pltpu.make_async_remote_copy(
             src_ref=self.whole(n, 1 - self.core), dst_ref=self.other[i].at[:, :, pl.ds(at, size)],
             send_sem=self.pair_send.at[n], recv_sem=self.pair_recv.at[n],
-            device_id=mesh_id(flip(self.me, [], 0, (0,))), device_id_type=MESH,
+            device_id=self.here.partner[0], device_id_type=MESH,
         )
 
     def hop(self, k, n, c, source, spots):
@@ -603,7 +630,7 @@
             src_ref=self.other[i].at[source, :, cols],
             dst_ref=self.coming[i][k].at[spots, :, cols],
             send_sem=self.send.at[k, n, c], recv_sem=self.recv.at[k, n, c],
-            device_id=mesh_id(flip(self.me, [], 0, (self.order[c][k],))), device_id_type=MESH,
+            device_id=self.here.partner[self.order[c][k]], device_id_type=MESH,
         )
 
     def group(self, k, n, c):
@@ -633,7 +660,7 @@
             at, size = self.cuts[n][c]
 
             def body(j, _, c=c, at=at, size=size):
-                shard = flip(self.me, self.order[c][k + 1 :], j, (self.order[c][k],))
+                shard = self.here.flip(self.order[c][k + 1 :], j, (self.order[c][k],))
                 q = lax.div(shard, 2)
                 self.other[self.pieces[n][0]][q, :, pl.ds(at, size)] = self.total(
                     k, n, c, shard, much + j
@@ -647,13 +674,233 @@
         for c in range(3):
             self.group(self.stages - 1, n, c).wait_recv()
             at, size = self.cuts[n][c]
-            write(self.pieces[n][0], at, size, self.total(self.stages, n, c, self.me, 0))
+            write(self.pieces[n][0], at, size, self.total(self.stages, n, c, self.here.me, 0))
 
     def end(self, n):
         for k in range(self.stages):
             for c in range(3):
                 self.group(k, n, c).wait_send()
         self.pair(n).wait_send()
+
+
+def front_kernel(shards, blocks, rows_mb, split, *refs):
+    (own_in, own_out, own_down, own_gu, small, tokens, later_rows, deal_row, valid_row, lengths, gain), refs = refs[:11], refs[11:]
+    (full_in, full_out, full_down, full_gu, pq, pk, pv, pg, beta, on, o, ainv, u, p, l, resid, a2, x, info, gt, taps,
+     gain_one, gain_two, wbeta, segc, segr, mask, a1), refs = refs[:28], refs[28:]
+    (sent, got, sent_gt, got_gt, got_small, wbuf, wout, deal, w_sem, out_sem), refs = refs[:10], refs[10:]
+    sems, deal_sems, later_sems, small_sems = refs[:5], refs[5:8], refs[8:11], refs[11:14]
+    step = pl.program_id(0)
+    steps = HEADS // PAIR
+    width = PAIR * HEAD_DIM
+    rows = blocks * rows_mb
+    share = rows // shards
+    here = Here(shards)
+    pieces = pieces_of([4 * D, D, D, 2 * FF], split)
+    weights = Gather(here, pieces, (own_in, own_out, own_down, own_gu), (full_in, full_out, full_down, full_gu), sems)
+    first_send = Exchange(here, sent, got, *deal_sems)
+    second_send = Exchange(here, sent_gt, got_gt, *later_sems)
+    small_send = Exchange(here, small, got_small, *small_sems, same=True)
+    of_in = split[0]
+    hidden_from = len(pieces) + weights.stages - steps
+    deal_to, later_from = X_STEPS, GT_FROM
+
+    def trickle(exchange, first, last):
+        parts, done = weights.slots(first, last), [0]
+
+        def at(t):
+            if not first <= t < last:
+                return None
+            done[0] = weights.slots(first, t)
+
+            def one():
+                exchange.start_part(done[0], parts)
+                done[0] += 1
+
+            return one
+
+        return at
+
+    deal_some = trickle(first_send, 1, deal_to)
+    later_some = trickle(second_send, later_from, weights.last + 1)
+
+    def between(t):
+        acts = [f for f in (deal_some(t), later_some(t)) if f is not None]
+        return (lambda: [f() for f in acts]) if acts else None
+
+    def fetch(s, g):
+        return pltpu.make_async_copy(
+            full_in.at[:, :, :, pl.ds(g * D + s * width, width)], wbuf.at[s % 2, g], w_sem.at[s % 2, g]
+        )
+
+    def fetch_out():
+        return pltpu.make_async_copy(full_out, wout, out_sem)
+
+    @pl.when(step == 0)
+    def _():
+        weights.begin()
+        meet(here, True)
+        weights.step(0)
+        small_send.start()
+        row, col = iota2((rows, rows), 0), iota2((rows, rows), 1)
+        column = lambda v: jnp.sum(jnp.where(row == col, v, 0.0), axis=1, keepdims=True)
+        dealt = deal_row[...].astype(F32)
+        target = jnp.floor((dealt + 0.5) * (1.0 / rows))
+        valid = valid_row[...].astype(F32)
+        target_c = column(target)
+        rank = jnp.sum(jnp.where((target == target_c) & (col < row), 1.0, 0.0), axis=1, keepdims=True)
+        slot = target_c * share + rank
+        sort_t = (slot == col.astype(F32)).astype(BF16)
+        lane = iota2((rows, 128), 1)
+        notes = jnp.where(
+            lane == 0, column(valid),
+            jnp.where(lane == 1, column(dealt - target * rows), jnp.where(lane == 2, jnp.sum(valid), 0.0)),
+        ).astype(BF16)
+        sent[:, :, :D] = tn(sort_t, tokens[...]).reshape(shards, share, D).astype(BF16)
+        sent[:, :, D:] = tn(sort_t, notes).reshape(shards, share, 128).astype(BF16)
+        weights.step(1, between(1))
+        half = later_rows.shape[1] // 2
+        for at in (0, half):
+            sent_gt[:, :, at : at + half] = (
+                tn(sort_t, later_rows[:, at : at + half]).reshape(shards, share, half).astype(BF16)
+            )
+        weights.step(2, between(2))
+        at_row, at_col = iota2((rows, 1), 0), iota2((1, rows), 1)
+        seg_c, seg_r = jnp.zeros((rows, 1), F32), jnp.zeros((1, rows), F32)
+        lens = lengths[...].astype(F32)
+        for b in range(blocks):
+            end = jnp.zeros((1, 1), F32) + b * rows_mb
+            for i in range(lengths.shape[1]):
+                seg_c = seg_c + jnp.where(at_row >= b * rows_mb, 1.0, 0.0) * (i == 0)
+                seg_r = seg_r + jnp.where(at_col >= b * rows_mb, 1.0, 0.0) * (i == 0)
+                end = end + lens[b : b + 1, i : i + 1]
+                if i < lengths.shape[1] - 1:
+                    seg_c = seg_c + jnp.where(at_row.astype(F32) >= end, 1.0, 0.0)
+                    seg_r = seg_r + jnp.where(at_col.astype(F32) >= end, 1.0, 0.0)
+        segc[...] = seg_c.astype(jnp.int32)
+        segr[...] = seg_r.astype(jnp.int32)
+        lane8 = iota2((rows, 8), 1)
+        wide = jnp.broadcast_to(seg_c, (rows, 128))
+        marks = jnp.where(lane8 == 0, 1.0, 0.0)
+        for s in range(1, CONV):
+            before = pltpu.roll(wide, s, 0)[:, :1]
+            same = jnp.where((before == seg_c) & (at_row >= s), 1.0, 0.0)
+            marks = marks + jnp.where(lane8 == s, same, 0.0)
+        mask[...] = marks
+        small_send.wait()
+        own_taps, own_gain = 3 * D // shards, D // shards
+        per = 128 // own_gain
+        a, c = iota2((per * 128, per * own_taps), 0), iota2((per * 128, per * own_taps), 1)
+        pick_taps = ((a // 128 == c // own_taps) & (a % 128 == c % own_taps)).astype(BF16)
+        a, c = iota2((per * 128, 128), 0), iota2((per * 128, 128), 1)
+        pick_gain = ((a // 128 == c // own_gain) & (a % 128 == c % own_gain)).astype(BF16)
+        for g in range(shards // per):
+            left = jnp.concatenate([got_small[g * per + i, :, :128].astype(F32) for i in range(per)], axis=1).astype(BF16)
+            right = jnp.concatenate([got_small[g * per + i, :, 128:].astype(F32) for i in range(per)], axis=1).astype(BF16)
+            tap = nn(left, pick_taps)
+            taps[:, g * per * own_taps : (g + 1) * per * own_taps] = tap[:CONV]
+            gains = nn(left, pick_gain)
+            gain_one[:, g * 128 : (g + 1) * 128] = gains[4:5]
+            gain_two[:, g * 128 : (g + 1) * 128] = gains[5:6]
+            wbeta[:, g * 128 : (g + 1) * 128] = nn(right, pick_gain).astype(BF16)
+        for t in range(3, hidden_from):
+            weights.step(t, between(t))
+        first_send.wait()
+        flat = got[...].astype(F32).reshape(rows, D + 128)
+        notes = flat[:, D:]
+        info[...] = notes
+        deal[...] = (notes[:, 1:2] == col.astype(F32)).astype(BF16)
+        x_now = tn(deal[...], flat[:, :D].astype(BF16))
+        x[...] = x_now
+        a1[...] = (rms(x_now)[0] * gain_one[...]).astype(BF16)
+        beta[...] = nt(a1[...], wbeta[...])
+        for n in range(of_in):
+            weights.half(n).wait_recv()
+        for g in range(4):
+            fetch(0, g).start()
+
+    for s in range(steps):
+
+        @pl.when(step == s)
+        def _(s=s):
+            for g in range(4):
+                fetch(s, g).wait()
+            if s + 1 < steps:
+                for g in range(4):
+                    fetch(s + 1, g).start()
+
+    slot_now = lax.rem(step, 2)
+    for g, out in enumerate((pq, pk, pv, pg)):
+        out[...] = nn(a1[...], wbuf[slot_now, g].reshape(D, width))
+    here_cols = pl.ds(pl.multiple_of(step * width, width), width)
+    taps_of = lambda j: taps.at[:, pl.ds(pl.multiple_of(j * D + step * width, width), width)]
+    mixer_fwd_kernel(
+        blocks, rows_mb, pq, pk, pv, pg, beta, taps_of(0), taps_of(1), taps_of(2), gain, mask, segc, segr,
+        on.at[:, here_cols], o, ainv, u, p, l,
+    )
+    for s in range(steps):
+
+        @pl.when(step == s)
+        def _(s=s):
+            weights.step(hidden_from + s, between(hidden_from + s))
+            if s == steps - 1:
+                for n in range(of_in, of_in + split[1]):
+                    weights.half(n).wait_recv()
+                fetch_out().start()
+                second_send.wait()
+                gt[...] = tn(deal[...], got_gt[...].astype(F32).reshape(rows, gt.shape[1]).astype(BF16))
+                fetch_out().wait()
+                r = x[...] + nn(on[...], wout[...].reshape(D, D))
+                resid[...] = r
+                a2[...] = (rms(r)[0] * gain_two[...]).astype(BF16)
+                weights.end(of_in + split[1])
+
+
+def front(weights, small, tokens, later_rows, deal_rows, valid_mask, lengths, gain, shards, collective_id):
+    rows, blocks = tokens.shape[0], lengths.shape[0]
+    rows_mb, share = rows // blocks, rows // shards
+    width = PAIR * HEAD_DIM
+    split = (2, 1, 1, 2)
+    pieces = pieces_of([w.shape[1] for w in weights], split)
+    anywhere = pl.BlockSpec(memory_space=pl.ANY)
+    _, mat, one, _, full = mixer_specs(rows, blocks, rows_mb)
+    f32 = lambda *shape: jax.ShapeDtypeStruct(shape, F32)
+    bf = lambda *shape: jax.ShapeDtypeStruct(shape, BF16)
+    square = f32(HEADS, blocks, rows_mb, rows_mb)
+    wide = f32(rows, D)
+    vm, dma = pltpu.VMEM, pltpu.SemaphoreType.DMA
+    outs = [
+        (spread(w, shards), anywhere) for w in weights
+    ] + [(wide, one)] * 4 + [
+        (f32(rows, HEADS), full((rows, HEADS))), (bf(rows, D), full((rows, D))), (wide, one),
+        (square, mat), (square, mat), (square, mat), (square, mat), (wide, full((rows, D))),
+        (bf(rows, D), full((rows, D))), (wide, full((rows, D))), (f32(rows, 128), full((rows, 128))),
+        (f32(rows, 2 * D), full((rows, 2 * D))), (f32(CONV, 3 * D), full((CONV, 3 * D))),
+        (f32(1, D), full((1, D))), (f32(1, D), full((1, D))), (bf(8, D), full((8, D))),
+        (jax.ShapeDtypeStruct((rows, 1), jnp.int32), full((rows, 1))),
+        (jax.ShapeDtypeStruct((1, rows), jnp.int32), full((1, rows))), (f32(rows, 8), full((rows, 8))),
+        (bf(rows, D), full((rows, D))),
+    ]
+    return pl.pallas_call(
+        functools.partial(front_kernel, shards, blocks, rows_mb, split),
+        grid=(HEADS // PAIR,),
+        in_specs=[anywhere] * 4 + [
+            full(small.shape), full((rows, D)), full((rows, 2 * D)), full((1, rows)), full((1, rows)),
+            full(lengths.shape), full((1, HEAD_DIM)),
+        ],
+        out_specs=[s for _, s in outs],
+        out_shape=[s for s, _ in outs],
+        scratch_shapes=[
+            vm((shards, share, D + 128), BF16), vm((shards, share, D + 128), BF16),
+            vm((shards, share, 2 * D), BF16), vm((shards, share, 2 * D), BF16),
+            vm((shards,) + small.shape, BF16),
+            vm((2, 4, shards // 2, 2, D // shards, width), BF16),
+            vm((shards // 2, 2, D // shards, D), BF16), vm((rows, rows), BF16), dma((2, 4)), dma,
+        ] + Gather.semaphores(shards, pieces) + [dma] * 9,
+        compiler_params=pltpu.CompilerParams(
+            collective_id=collective_id, has_side_effects=True, vmem_limit_bytes=58 << 20
+        ),
+        name="front",
+    )(*weights, small, tokens, later_rows, deal_rows[None, :], valid_mask[None, :], lengths, gain)
 
 
 def backward_kernel(shards, blocks, rows_mb, pieces, *refs):
@@ -666,8 +913,8 @@
     step = pl.program_id(0)
     chunks = FF // CHUNK
     pairs = HEADS // PAIR
-    me = lin_index()
-    core = lax.rem(me, 2)
+    here = Here(shards)
+    core = here.core
     other, coming = Scatter.split(shards, 2, buffers)
     r_gu = d_gu.shape[2]
 
@@ -685,7 +932,7 @@
             return None
         return pltpu.make_async_copy(d_down.at[:, core], mine_down, keep)
 
-    net = Scatter(shards, me, pieces, whole, mine, other, coming, sems, kept)
+    net = Scatter(here, pieces, whole, mine, other, coming, sems, kept)
 
     def write(i, at, size, value):
         if i == 0:
@@ -699,7 +946,7 @@
     @pl.when(step == 0)
     def _():
         kept(0).start()
-        meet(shards, me, False)
+        meet(here, False)
         net.pair(0).start()
         acc[...] = jnp.zeros_like(acc)
 
@@ -858,9 +1105,9 @@
     refs = refs[2 * count + 2 :]
     mine, refs = refs[:count], refs[count:]
     sems, (keep, *back_sems), buffers = refs[:4], refs[4:8], refs[8:]
-    me = lin_index()
-    core = lax.rem(me, 2)
-    back = Exchange(shards, me, sent, got, *back_sems)
+    here = Here(shards)
+    core = here.core
+    back = Exchange(here, sent, got, *back_sems)
     other, coming = Scatter.split(shards, count, buffers)
     pieces = [(i, 0, g.shape[-1]) for i, g in enumerate(grads)]
 
@@ -868,7 +1115,7 @@
         return pltpu.make_async_copy(grads[n].at[:, core], mine[n], keep.at[n])
 
     net = Scatter(
-        shards, me, pieces, lambda n, parity: grads[n].at[:, parity],
+        here, pieces, lambda n, parity: grads[n].at[:, parity],
         lambda i, q, cols: mine[i][q, :, cols], other, coming, sems, kept,
     )
 
@@ -877,7 +1124,7 @@
 
     for n in range(count):
         kept(n).start()
-    meet(shards, me, True)
+    meet(here, True)
     for n in range(count):
         net.pair(n).start()
     back.start()
@@ -945,75 +1192,106 @@
     share = rows // shards
     blocks = lengths.shape[0]
     rows_mb = rows // blocks
+    a, b, c = CONV * conv_kernel.shape[1], w_beta.shape[0] * HEADS, norm_gain.shape[0]
     small = w_beta.shape[0] * HEADS + CONV * conv_kernel.shape[1] + 2 * norm_gain.shape[0]
 
-    target = deal_rows // rows
-    spot = deal_rows % rows
-    ahead = (target[None, :] == target[:, None]) & (
-        jnp.arange(rows)[None, :] < jnp.arange(rows)[:, None]
-    )
-    slot = target * share + jnp.sum(ahead.astype(jnp.int32), axis=1)
-    sort_t = (slot[:, None] == jnp.arange(rows)[None, :]).astype(BF16)
-    sort = (slot[None, :] == jnp.arange(rows)[:, None]).astype(BF16)
-    count_own = jnp.sum(valid_mask.astype(F32))
-    lane = jnp.arange(128)[None, :]
-    notes = jnp.where(
-        lane == 0,
-        valid_mask.astype(F32)[:, None],
-        jnp.where(lane == 1, spot.astype(F32)[:, None], jnp.where(lane == 2, count_own, 0.0)),
-    ).astype(BF16)
-    packed = jnp.concatenate(
-        [conv_kernel.reshape(-1), w_beta.reshape(-1), norm_gain, ffn_gain,
-         jnp.zeros((share * 128 - small,), BF16)]
-    ).reshape(1, share, 128)
-    sorted_rows = nn(sort, jnp.concatenate([tokens, notes], axis=1)).astype(BF16)
-    message = jnp.concatenate(
-        [sorted_rows.reshape(shards, share, -1), jnp.broadcast_to(packed, (shards, share, 128))],
-        axis=2,
-    )
-    later = nn(sort, jnp.concatenate([cotangent, teacher], axis=1)).astype(BF16)
-    later = later.reshape(shards, share, 2 * D)
-    (win, wout), arrived = first([w_in, w_out], (2, 1), message, shards, 0)
-
-    flat = arrived.reshape(rows, -1)
-    info = flat[:, D : D + 128].astype(F32)
-    place = info[:, 1].astype(jnp.int32)
-    counted = jnp.sum(arrived[:, 0, D + 2].astype(F32))
-    extra = arrived[:, :, D + 128 :].reshape(shards, share * 128)
-    a, b, c = CONV * conv_kernel.shape[1], w_beta.shape[0] * HEADS, norm_gain.shape[0]
-    taps = extra[:, :a].reshape(shards, CONV, -1).swapaxes(0, 1).reshape(CONV, 3 * D).astype(F32)
-    wbeta = extra[:, a : a + b].reshape(D, HEADS)
-    gain_one = extra[:, a + b : a + b + c].reshape(D).astype(F32)
-    gain_two = extra[:, a + b + c : a + b + 2 * c].reshape(D).astype(F32)
-    deal = (place[None, :] == jnp.arange(rows)[:, None]).astype(BF16)
-    deal_t = (place[:, None] == jnp.arange(rows)[None, :]).astype(BF16)
-    dealt = nn(deal, flat[:, : D + 128])
-    x = dealt[:, :D]
-    m = dealt[:, D : D + 1]
-
-    ends = jnp.cumsum(lengths, axis=1)
-    within = jnp.arange(rows_mb, dtype=jnp.int32)
-    seg = jnp.sum((within[None, :, None] >= ends[:, None, :]).astype(jnp.int32), axis=2)
-    seg = (seg + (lengths.shape[1] + 1) * jnp.arange(blocks, dtype=jnp.int32)[:, None]).reshape(rows)
-    position = jnp.arange(rows, dtype=jnp.int32)
-    mask = jnp.stack(
-        [jnp.ones((rows,), F32)]
-        + [((position >= s) & (jnp.roll(seg, s) == seg)).astype(F32) for s in range(1, CONV)]
-        + [jnp.zeros((rows,), F32)] * (8 - CONV),
-        axis=1,
-    )
-    segc, segr = seg[:, None], seg[None, :]
-    gain_out = out_gain.astype(F32)[None, :]
-
-    nx, rx = rms(x)
-    a1 = (nx * gain_one).astype(BF16)
-    wdown, wgu, later, (*proj, beta_pre, on, o, ainv, u, p, l, resid, a2) = forward(
-        w_down, w_gu, later, (1, 2), a1, win, wout, wbeta, x, gain_two[None, :], taps, gain_out, mask, segc,
-        segr, blocks, shards, 2,
-    )
-    saved = (o, ainv, u, p, l)
-    later = nn(deal, later.reshape(rows, 2 * D))
-    g, t = later[:, :D], later[:, D:]
+    if share % 8 == 0 and (D // shards) % 16 == 0:
+        half = jnp.pad(
+            jnp.concatenate([conv_kernel, jnp.pad(jnp.stack([norm_gain, ffn_gain]), ((0, 0), (0, conv_kernel.shape[1] - norm_gain.shape[0])))]),
+            ((0, 2), (0, 128 - conv_kernel.shape[1])),
+        )
+        small_block = jnp.concatenate(
+            [half, jnp.pad(w_beta.T, ((0, 0), (0, 128 - w_beta.shape[0])))], axis=1
+        )
+        gain_out = out_gain.astype(F32)[None, :]
+        (win, wout, wdown, wgu, *proj, beta_pre, on, o, ainv, u, p, l, resid, a2, x, info, later, taps,
+         gain_one, gain_two, wbeta, segc, segr, mask, a1) = front(
+            [w_in, w_out, w_down, w_gu], small_block, tokens, jnp.concatenate([cotangent, teacher], axis=1),
+            deal_rows, valid_mask, lengths, gain_out, shards, 0,
+        )
+        win, wout, wdown, wgu = (w.reshape(-1, w.shape[-1]) for w in (win, wout, wdown, wgu))
+        saved = (o, ainv, u, p, l)
+        place = info[:, 1].astype(jnp.int32)
+        counted = jnp.sum(info[::share, 2])
+        g, t = later[:, :D], later[:, D:]
+        target = deal_rows // rows
+        ahead = (target[None, :] == target[:, None]) & (
+            jnp.arange(rows)[None, :] < jnp.arange(rows)[:, None]
+        )
+        slot = target * share + jnp.sum(ahead.astype(jnp.int32), axis=1)
+        sort_t = (slot[:, None] == jnp.arange(rows)[None, :]).astype(BF16)
+        deal_t = (place[:, None] == jnp.arange(rows)[None, :]).astype(BF16)
+        deal = (place[None, :] == jnp.arange(rows)[:, None]).astype(BF16)
+        m = jnp.sum(deal.astype(F32) * info[:, 0][None, :], axis=1, keepdims=True)
+        gain_one, gain_two = gain_one[0], gain_two[0]
+        wbeta = wbeta.T
+    else:
+        target = deal_rows // rows
+        spot = deal_rows % rows
+        ahead = (target[None, :] == target[:, None]) & (
+            jnp.arange(rows)[None, :] < jnp.arange(rows)[:, None]
+        )
+        slot = target * share + jnp.sum(ahead.astype(jnp.int32), axis=1)
+        sort_t = (slot[:, None] == jnp.arange(rows)[None, :]).astype(BF16)
+        sort = (slot[None, :] == jnp.arange(rows)[:, None]).astype(BF16)
+        count_own = jnp.sum(valid_mask.astype(F32))
+        lane = jnp.arange(128)[None, :]
+        notes = jnp.where(
+            lane == 0,
+            valid_mask.astype(F32)[:, None],
+            jnp.where(lane == 1, spot.astype(F32)[:, None], jnp.where(lane == 2, count_own, 0.0)),
+        ).astype(BF16)
+        packed = jnp.concatenate(
+            [conv_kernel.reshape(-1), w_beta.reshape(-1), norm_gain, ffn_gain,
+             jnp.zeros((share * 128 - small,), BF16)]
+        ).reshape(1, share, 128)
+        sorted_rows = nn(sort, jnp.concatenate([tokens, notes], axis=1)).astype(BF16)
+        message = jnp.concatenate(
+            [sorted_rows.reshape(shards, share, -1), jnp.broadcast_to(packed, (shards, share, 128))],
+            axis=2,
+        )
+        later = nn(sort, jnp.concatenate([cotangent, teacher], axis=1)).astype(BF16)
+        later = later.reshape(shards, share, 2 * D)
+        (win, wout), arrived = first([w_in, w_out], (2, 1), message, shards, 0)
+
+        flat = arrived.reshape(rows, -1)
+        info = flat[:, D : D + 128].astype(F32)
+        place = info[:, 1].astype(jnp.int32)
+        counted = jnp.sum(arrived[:, 0, D + 2].astype(F32))
+        extra = arrived[:, :, D + 128 :].reshape(shards, share * 128)
+        taps = extra[:, :a].reshape(shards, CONV, -1).swapaxes(0, 1).reshape(CONV, 3 * D).astype(F32)
+        wbeta = extra[:, a : a + b].reshape(D, HEADS)
+        gain_one = extra[:, a + b : a + b + c].reshape(D).astype(F32)
+        gain_two = extra[:, a + b + c : a + b + 2 * c].reshape(D).astype(F32)
+        deal = (place[None, :] == jnp.arange(rows)[:, None]).astype(BF16)
+        deal_t = (place[:, None] == jnp.arange(rows)[None, :]).astype(BF16)
+        dealt = nn(deal, flat[:, : D + 128])
+        x = dealt[:, :D]
+        m = dealt[:, D : D + 1]
+
+        ends = jnp.cumsum(lengths, axis=1)
+        within = jnp.arange(rows_mb, dtype=jnp.int32)
+        seg = jnp.sum((within[None, :, None] >= ends[:, None, :]).astype(jnp.int32), axis=2)
+        seg = (seg + (lengths.shape[1] + 1) * jnp.arange(blocks, dtype=jnp.int32)[:, None]).reshape(rows)
+        position = jnp.arange(rows, dtype=jnp.int32)
+        mask = jnp.stack(
+            [jnp.ones((rows,), F32)]
+            + [((position >= s) & (jnp.roll(seg, s) == seg)).astype(F32) for s in range(1, CONV)]
+            + [jnp.zeros((rows,), F32)] * (8 - CONV),
+            axis=1,
+        )
+        segc, segr = seg[:, None], seg[None, :]
+        gain_out = out_gain.astype(F32)[None, :]
+
+        nx, rx = rms(x)
+        a1 = (nx * gain_one).astype(BF16)
+        wdown, wgu, later, (*proj, beta_pre, on, o, ainv, u, p, l, resid, a2) = forward(
+            w_down, w_gu, later, (1, 2), a1, win, wout, wbeta, x, gain_two[None, :], taps, gain_out, mask, segc,
+            segr, blocks, shards, 2,
+        )
+        saved = (o, ainv, u, p, l)
+        later = nn(deal, later.reshape(rows, 2 * D))
+        g, t = later[:, :D], later[:, D:]
     gu = nn(a2, wgu)
     gate, up = gu[:, :FF], gu[:, FF:]
     hid = (gate * sigmoid(gate) * up).astype(BF16)

time: 419 us -> 373 us (0.89)
  Pallas kernels: 344 us -> 318 us
  matrix products: 26.8 us -> 20.4 us
  local copies, waits for them, and re-layouts: 18.6 us -> 14 us
  other arithmetic: 16.9 us -> 12.7 us
    pallas_call x2 -> x1, Pallas kernels: 177 us -> 150 us  [front(): pl.pallas_call(functools.partial(front_kernel, shards, blocks, rows_mb, s...]
    dot_general x8 -> x4, matrix products: 22.6 us -> 16.2 us  [nn(): return jnp.dot(left, right, preferred_element_type=F32)]
  transfers between devices with their start and end apart: 1 -> 1, of which waited for: 0 -> 0; matrix products, arithmetic and copies ran while one was open for 1% -> 1% of each run, Pallas kernels for 18% -> 19%
where the time goes in v3:
time: 373 us; the launch traced here: 372 us
  Pallas kernels  318 us (85%)
  matrix products  20.4 us (5%)
  local copies, waits for them, and re-layouts  14 us (4%)
  other arithmetic  12.7 us (3%)
  between operations  4.1 us (1%)
    pallas_call x1, Pallas kernels, front(): pl.pallas_call(functools.partial(front_kernel, shards, blocks, rows_mb, s...  150 us
    pallas_call x1, Pallas kernels, backward(): pl.pallas_call(functools.partial(backward_kernel, shards, blocks, rows_mb...  96.3 us
    pallas_call x1, Pallas kernels, scatter(): pl.pallas_call(functools.partial(scatter_kernel, shards, count), in_specs...  70.8 us
    dot_general x4, matrix products, nn(): return jnp.dot(left, right, preferred_element_type=F32)  16.2 us
  transfers between devices with their start and end apart: 1, of which 0 were waited for; matrix products, arithmetic and copies ran while one was open for 1% of the time, Pallas kernels for 19%

profile of v3, /device:TPU:0, one launch (start us, length us, event | category | flops | bytes accessed | tf_op | source)
XLA Modules:
  0.0 372.3 jit_solution(15039131599717229845)
XLA Ops:
  0.7 1.2 bitcast_convert_fusion.refs_10_.refs_29_
  1.9 2.3 pad_maximum_fusion.refs_6_
  4.9 150.4 %front.1 = (bf16[16,2,32,4096]{3,2,1,0:T(8,128)(2,1)}, bf16[16,2,32,1024]{3,2,1,0:T(8,128)(2,1)}, bf16[16,2,88,1024]{3,2,1,0:T(8,128)(2,1)}, bf16[16,2,32,5632]{...) custom-call(bf16[32,4096]{1,0:T(8,128)(2,1)} %refs_0_.1, ...), custom_call_target="tpu_custom_call" | custom-call | tf_op jit(solution)/shard_map/front/pallas_call | solution.py:883
  155.3 1.1 convert_reduce_fusion.1
  156.4 1.0 slice_reduce_fusion
  157.4 1.0 slice.50
  158.4 6.4 %fusion.26.refs_3_.refs_4_ = f32[256,5632]{1,0:T(8,128)S(1)} fusion(bf16[256,1024]{1,0:T(8,128)(2,1)} %get-tuple-element.61.refs_2_, bf16[1024,5632]{1,0:T(8,128)(2,1)} %bitcast.41), kind=kOutput, calls=%fused_computation.57 | convolution fusion | flops 2952790016 | bytes 17825792 | tf_op jit(solution)/shard_map/dot_general | solution.py:1174
  164.8 0.9 fusion
  165.7 1.7 copy-done
  168.8 6.6 %fusion.23 = (bf16[256,1024]{1,0:T(8,128)(2,1)S(1)}, f32[256,1024]{1,0:T(8,128)}, f32[]{:T(128)}, bf16[256,1024]{1,0:T(8,128)(2,1)S(1)}) fusion(f32[256,2048]{1,0:T(8,128)} %get-tuple-element.63, f32[256]{0:T(256)S(1)} %broadcast_multiply_fusion, f32[256]{0:T(256)S(1)} %multiply_reduce_fusion, f32[256,1024]{1,0:T(8,128)S(1)} %copy-done.2, ...), kind=kOutput, calls=%fused_computation.54 | convolution fusion | flops 1478754304 | bytes 12453892 | tf_op jit(solution)/shard_map/dot_general | solution.py:1174
  175.4 4.2 %fusion.27 = bf16[2816,1024]{1,0:T(8,128)(2,1)} fusion(bf16[256,2816]{1,0:T(8,128)(2,1)S(1)} %fusion, bf16[256,1024]{1,0:T(8,128)(2,1)S(1)} %get-tuple-element.134.refs_1_), kind=kOutput, calls=%fused_computation.58 | convolution fusion | flops 1476395008 | bytes 7733248 | tf_op jit(solution)/shard_map/dot_general | solution.py:1170
  179.6 0.8 copy.31
  180.4 96.3 %backward.1 = (f32[88,1024]{1,0:T(8,128)}, f32[32,5632]{1,0:T(8,128)}, bf16[1024,1024]{1,0:T(8,128)(2,1)}, bf16[1024,1024]{1,0:T(8,128)(2,1)}, bf16[1024,1024]{1...) custom-call(bf16[16,2,88,1024]{3,2,1,0:T(8,128)(2,1)} %bitcast.44, ...), custom_call_target="tpu_custom_call" | custom-call | tf_op jit(solution)/shard_map/backward/pallas_call | solution.py:1063
  277.8 1.3 reshape.127
  279.7 1.3 reduce.11
  281.1 1.3 reduce.12
  282.5 1.3 pad_maximum_fusion.3
  284.5 3.6 all-to-all-start
  289.0 1.5 fusion.1.refs_5_
  290.5 70.8 %scatter_last.1 = (f32[32,1024]{1,0:T(8,128)}, f32[32,1024]{1,0:T(8,128)}, f32[32,1024]{1,0:T(8,128)}, f32[32,1024]{1,0:T(8,128)}, f32[32,1024]{1,0:T(8,128)}, /*index=5*/bf16[32,8,2048]{2,1,0:T(8,128)(2,1)}) custom-call(bf16[16,2,32,1024]{3,2,1,0:T(8,128)(2,1)} %bitcast.52, bf16[16,2,32,1024]{3,2,1,0:T(8,128)(2,1)} %bitcast.48, ...), custom_call_target="tpu_custom_call" | custom-call | tf_op jit(solution)/shard_map/scatter_last/pallas_call | solution.py:1148
  361.3 1.8 convolution_convert_fusion
  363.1 0.8 pad_maximum_fusion.1
  364.0 1.0 fusion.24
  369.6 0.9 copy.40
  (65 shorter events, 8.7 us)
Async XLA Ops:
  0.6 3.6 copy-start.16
  0.7 3.6 copy-start.15
  0.7 3.6 copy-start.14
  0.7 3.6 copy-start.13
  164.8 2.6 copy-start
  164.8 4.0 %copy-start.2 = (f32[256,1024]{1,0:T(8,128)S(1)}, f32[256,1024]{1,0:T(8,128)}, u32[]{:S(2)}) copy-start(f32[256,1024]{1,0:T(8,128)} %get-tuple-element.65.refs_9_) | copy-start | bytes 3145732
  175.4 4.2 %copy-start.1 = (bf16[256,1024]{1,0:T(8,128)(2,1)}, bf16[256,1024]{1,0:T(8,128)(2,1)S(1)}, u32[]{:S(2)}) copy-start(bf16[256,1024]{1,0:T(8,128)(2,1)S(1)} %get-tuple-element.134.refs_1_) | copy-start | bytes 1572868
  175.4 4.2 %copy-start.11 = (bf16[8,1024]{1,0:T(8,128)(2,1)S(1)}, bf16[8,1024]{1,0:T(8,128)(2,1)}, u32[]{:S(2)}) copy-start(bf16[8,1024]{1,0:T(8,128)(2,1)} %get-tuple-element.74) | copy-start | bytes 49156
  276.7 11.3 %copy-start.12 = (s32[256]{0:T(256)S(1)}, s32[256]{0:T(256)}, u32[]{:S(2)}) copy-start(s32[256]{0:T(256)} %param.19) | copy-start | bytes 3076
  276.8 12.2 %copy-start.4 = (bf16[256,1024]{1,0:T(8,128)(2,1)S(1)}, bf16[256,1024]{1,0:T(8,128)(2,1)}, u32[]{:S(2)}) copy-start(bf16[256,1024]{1,0:T(8,128)(2,1)} %get-tuple-element.94) | copy-start | bytes 1572868
  284.5 80.5 %all-to-all-start = ((f32[32,7,128]{2,1,0:T(8,128)}), f32[32,7,128]{2,1,0:T(8,128)S(1)}, u32[]{:S(2)}, u32[]{:S(2)}) async-start(f32[32,7,128]{2,1,0:T(8,128)} %reshape.132), calls=%async_computation | async-start | bytes 262144 | tf_op jit(solution)/shard_map/all_to_all | solution.py:1331
  361.3 1.8 copy-start.7
  361.3 1.8 copy-start.8
  361.3 1.8 copy-start.9
  361.3 1.8 copy-start.10
  363.1 5.8 %copy-start.6 = (f32[32,1024]{1,0:T(8,128)S(1)}, f32[32,1024]{1,0:T(8,128)}, u32[]{:S(2)}) copy-start(f32[32,1024]{1,0:T(8,128)} %get-tuple-element.160) | copy-start | bytes 393220
  363.1 6.5 %copy-start.3 = (f32[32,5632]{1,0:T(8,128)S(1)}, f32[32,5632]{1,0:T(8,128)}, u32[]{:S(2)}) copy-start(f32[32,5632]{1,0:T(8,128)} %get-tuple-element.164) | copy-start | bytes 2162692
  364.0 6.5 %copy-start.5 = (f32[88,1024]{1,0:T(8,128)S(1)}, f32[88,1024]{1,0:T(8,128)}, u32[]{:S(2)}) copy-start(f32[88,1024]{1,0:T(8,128)} %get-tuple-element.165) | copy-start | bytes 1081348

commit v4 on v3

--- a/solution.py
+++ b/solution.py
@@ -125,7 +125,7 @@
 
 
 def mixer_bwd_kernel(
-    blocks, rows_mb, step,
+    blocks, rows_mb, pair, step,
     pq, pk, pv, pg, beta, tq, tk, tv, gain, mask, segc, segr,
     don_ref, o_ref, ainv_ref, u_ref, p_ref, l_ref,
     dq_ref, dk_ref, dv_ref, dg_ref, dbeta_ref, dtq, dtk, dtv, dgain_ref,
@@ -148,7 +148,7 @@
     gsig = sigmoid(gates)
     gate = gates * gsig
     dgate = gsig * (1.0 + gates * (1.0 - gsig))
-    systems = [(h, b) for h in range(PAIR) for b in range(blocks)]
+    systems = [(h, b) for h in range(pair) for b in range(blocks)]
     part = []
     dgain = jnp.zeros((1, HEAD_DIM), F32)
     for h, b in systems:
@@ -157,7 +157,7 @@
         k, ik = l2_norm(ck[rs, hs])
         qn, iq = l2_norm(cq[rs, hs])
         v = cv[rs, hs]
-        bb = jnp.sum(jnp.where(lane == step * PAIR + h, strengths, 0.0), axis=1, keepdims=True)[rs]
+        bb = jnp.sum(jnp.where(lane == step * pair + h, strengths, 0.0), axis=1, keepdims=True)[rs]
         same = segc[rs, :] == segr[:, rs]
         o = o_ref[rs, hs]
         don = don_ref[rs, hs]
@@ -193,7 +193,7 @@
         dbp = db * bb * (1.0 - bb)
         pieces = [dbp if b == c else jnp.zeros((rows_mb, 1), F32) for c in range(blocks)]
         column = jnp.concatenate(pieces, axis=0) if blocks > 1 else dbp
-        dbeta = dbeta + jnp.where(lane == step * PAIR + h, column, 0.0)
+        dbeta = dbeta + jnp.where(lane == step * pair + h, column, 0.0)
         dcs[0].append(iq * (dqs[i] - qn * jnp.sum(qn * dqs[i], axis=-1, keepdims=True)))
         dcs[1].append(ik * (dks[i] - k * jnp.sum(k * dks[i], axis=-1, keepdims=True)))
         dcs[2].append(dv)
@@ -201,7 +201,7 @@
         whole = jnp.concatenate(
             [
                 jnp.concatenate([dcs[j][h * blocks + b] for b in range(blocks)], axis=0)
-                for h in range(PAIR)
+                for h in range(pair)
             ],
             axis=1,
         )
@@ -350,6 +350,9 @@
 CHUNK = 256
 X_STEPS = 5
 GT_FROM = 6
+SLICE = 256
+MIXER_BUFFERS = 2
+DX_PARTS = 6
 
 
 def pieces_of(widths, split):
@@ -676,17 +679,18 @@
             at, size = self.cuts[n][c]
             write(self.pieces[n][0], at, size, self.total(self.stages, n, c, self.here.me, 0))
 
-    def end(self, n):
+    def end(self, n, paired=True):
         for k in range(self.stages):
             for c in range(3):
                 self.group(k, n, c).wait_send()
-        self.pair(n).wait_send()
+        if paired:
+            self.pair(n).wait_send()
 
 
 def front_kernel(shards, blocks, rows_mb, split, *refs):
     (own_in, own_out, own_down, own_gu, small, tokens, later_rows, deal_row, valid_row, lengths, gain), refs = refs[:11], refs[11:]
     (full_in, full_out, full_down, full_gu, pq, pk, pv, pg, beta, on, o, ainv, u, p, l, resid, a2, x, info, gt, taps,
-     gain_one, gain_two, wbeta, segc, segr, mask, a1), refs = refs[:28], refs[28:]
+     gain_one, gain_two, wbeta, segc, segr, mask, a1, a1_t, a2_t), refs = refs[:30], refs[30:]
     (sent, got, sent_gt, got_gt, got_small, wbuf, wout, deal, w_sem, out_sem), refs = refs[:10], refs[10:]
     sems, deal_sems, later_sems, small_sems = refs[:5], refs[5:8], refs[8:11], refs[11:14]
     step = pl.program_id(0)
@@ -813,6 +817,7 @@
         x[...] = x_now
         a1[...] = (rms(x_now)[0] * gain_one[...]).astype(BF16)
         beta[...] = nt(a1[...], wbeta[...])
+        a1_t[...] = a1[...].T
         for n in range(of_in):
             weights.half(n).wait_recv()
         for g in range(4):
@@ -852,6 +857,7 @@
                 r = x[...] + nn(on[...], wout[...].reshape(D, D))
                 resid[...] = r
                 a2[...] = (rms(r)[0] * gain_two[...]).astype(BF16)
+                a2_t[...] = a2[...].T
                 weights.end(of_in + split[1])
 
 
@@ -878,7 +884,7 @@
         (f32(1, D), full((1, D))), (f32(1, D), full((1, D))), (bf(8, D), full((8, D))),
         (jax.ShapeDtypeStruct((rows, 1), jnp.int32), full((rows, 1))),
         (jax.ShapeDtypeStruct((1, rows), jnp.int32), full((1, rows))), (f32(rows, 8), full((rows, 8))),
-        (bf(rows, D), full((rows, D))),
+        (bf(rows, D), full((rows, D))), (bf(D, rows), full((D, rows))), (bf(D, rows), full((D, rows))),
     ]
     return pl.pallas_call(
         functools.partial(front_kernel, shards, blocks, rows_mb, split),
@@ -976,7 +982,7 @@
     def _():
         don[...] = nt(dz[...], wout[...])
         mixer_bwd_kernel(
-            blocks, rows_mb, step - chunks, *mixer[:12], don, *mixer[12:], dpq, dpk, dpv, dpg, dbeta, dtq,
+            blocks, rows_mb, PAIR, step - chunks, *mixer[:12], don, *mixer[12:], dpq, dpk, dpv, dpg, dbeta, dtq,
             dtk, dtv, d_gain,
         )
         for dp, w, out in ((dpq, wq, dwq), (dpk, wk, dwk), (dpv, wv, dwv), (dpg, wg, dwg)):
@@ -1100,6 +1106,309 @@
       mask, segc, segr, *saved)
 
 
+def link_plan(half_way, done, last, heads):
+    return [
+        [3, 8, 10, 12], [half_way + 2, done, done + 2], [done + 1, done + 3], [done + heads // 2 + 2], [last],
+        [last],
+    ]
+
+
+def rear_kernel(shards, blocks, rows_mb, pieces, *refs):
+    (d_down, sent_y, dy, resid, x, a2_t, a1_t, df, gate, up, wga, wup, wdn, gain_two, gain_one, wout, wq, wk, wv, wg,
+     on, wbeta, deal, loss, *mixer), refs = refs[:41], refs[41:]
+    (g_down, g_gu, g_in, g_out, got_y, got_dx, small_sum), refs = refs[:7], refs[7:]
+    (mine_down, mine_gu, mine_in, mine_out, stage_gu, stage_in, stage_out, acc, dresid, held, dz, don, dpq, dpk, dpv,
+     dpg, turned, dbeta, dtaps, d_gain, d_two, sent_dx, small, small_got, keep, load, gu_sem, in_sem, out_sem), refs = refs[:29], refs[29:]
+    y_sems, dx_sems, small_sems, sems, buffers = refs[:3], refs[3:6], refs[6:9], refs[9:13], refs[13:]
+    step = pl.program_id(0)
+    chunks, heads = FF // SLICE, HEADS
+    rows = blocks * rows_mb
+    share, r_gu = rows // shards, D // shards
+    here = Here(shards)
+    core = here.core
+    other, coming = Scatter.split(shards, 4, buffers)
+    mines = (mine_down, mine_gu, mine_in, mine_out)
+    pair_recv = sems[3]
+
+    def whole(n, parity):
+        i, at, size = pieces[n]
+        if i == 0:
+            return d_down.at[:, parity, :, pl.ds(at, size)]
+        return other[i].at[:, :, pl.ds(at, size)]
+
+    def kept(n):
+        if n > 0:
+            return None
+        return pltpu.make_async_copy(d_down.at[:, core], mine_down, keep)
+
+    net = Scatter(
+        here, pieces, whole, lambda i, q, cols: mines[i][q, :, cols], other, coming, sems, kept
+    )
+    give_y = Exchange(here, sent_y, got_y, *y_sems)
+    give_dx = Exchange(here, sent_dx, got_dx, *dx_sems)
+    give_small = Exchange(here, small, small_got, *small_sems)
+
+    def cross(stage, slot, there, send, n):
+        return pltpu.make_async_remote_copy(
+            src_ref=stage.at[slot], dst_ref=there, send_sem=send.at[slot], recv_sem=pair_recv.at[n],
+            device_id=here.partner[0], device_id_type=MESH,
+        )
+
+    def cross_gu(j):
+        cols = pl.ds(pl.multiple_of(j * (2 * SLICE), 2 * SLICE), 2 * SLICE)
+        return cross(stage_gu, lax.rem(j, 2), other[1].at[:, :, cols], gu_sem, 1 + lax.div(j + chunks % 2, (chunks + 1) // 2))
+
+    def cross_in(s):
+        width = 4 * HEAD_DIM
+        cols = pl.ds(pl.multiple_of(s * width, width), width)
+        return cross(stage_in, lax.rem(s, 2), other[2].at[:, :, cols], in_sem, 3 + lax.div(s, heads // 2))
+
+    def cross_out(s):
+        much = shards // 2 // heads
+        return cross(stage_out, lax.rem(s, 2), other[3].at[pl.ds(s * much, much)], out_sem, 5)
+
+    def by_core(value):
+        first, second = value[:, 0], value[:, 1]
+        return (
+            jnp.where(core == 0, first, second).astype(BF16), jnp.where(core == 0, second, first).astype(BF16)
+        )
+
+    def write(i, at, size, value):
+        if i == 0:
+            g_down[:, pl.ds(at, size)] = value
+        elif i == 3:
+            g_out[:, pl.ds(at, size)] = value
+        else:
+            for tile in range(at // 128, (at + size) // 128):
+                if i == 1:
+                    chunk, inner = divmod(tile * 128, 2 * SLICE)
+                    start = chunk * SLICE + inner + (FF - SLICE if inner >= SLICE else 0)
+                else:
+                    start = tile % 4 * D + tile // 4 * HEAD_DIM
+                target = g_gu if i == 1 else g_in
+                target[:, start : start + 128] = value[:, tile * 128 - at : tile * 128 - at + 128]
+
+    load_dy = pltpu.make_async_copy(dy, dresid, load.at[0])
+    load_resid = pltpu.make_async_copy(resid, held, load.at[1])
+    load_x = pltpu.make_async_copy(x, held, load.at[1])
+    load_a2 = pltpu.make_async_copy(a2_t, turned, load.at[2])
+    load_a1 = pltpu.make_async_copy(a1_t, turned, load.at[2])
+
+    @pl.when(step == 0)
+    def _():
+        kept(0).start()
+        load_dy.start()
+        load_resid.start()
+        meet(here, True)
+        net.pair(0).start()
+        give_y.start()
+        acc[...] = jnp.zeros_like(acc)
+        load_a2.start()
+        load_a2.wait()
+
+    @pl.when(step < chunks)
+    def _():
+        dhid = nt(df[...], wdn[...])
+        g = gate[...]
+        s = sigmoid(g)
+        d_gate = (dhid * up[...] * (s * (1.0 + g * (1.0 - s)))).astype(BF16)
+        d_up = (dhid * (g * s)).astype(BF16)
+        acc[...] += nt(d_gate, wga[...]) + nt(d_up, wup[...])
+
+        @pl.when(step >= 2)
+        def _():
+            cross_gu(step - 2).wait_send()
+
+        slot = lax.rem(step, 2)
+        part = jnp.concatenate([d_gate, d_up], axis=1)
+        near, far = by_core(nn(turned[...], part).reshape(shards // 2, 2, r_gu, 2 * SLICE))
+        mine_gu[:, :, pl.ds(pl.multiple_of(step * (2 * SLICE), 2 * SLICE), 2 * SLICE)] = near
+        stage_gu[slot] = far
+        cross_gu(step).start()
+
+    @pl.when(step == chunks - 1)
+    def _():
+        load_dy.wait()
+        load_resid.wait()
+        nr, rr = rms(held[...])
+        da2 = acc[...]
+        d_two[...] = jnp.sum(da2 * nr, axis=0, keepdims=True)
+        dresid[...] = dresid[...] + rms_back(nr, rr, gain_two[...] * da2)
+        dz[...] = dresid[...].astype(BF16)
+        acc[...] = jnp.zeros_like(acc)
+        load_a1.start()
+        load_x.start()
+        load_a1.wait()
+
+    @pl.when(step >= chunks)
+    def _():
+        head = step - chunks
+        don[...] = nt(dz[...], wout[...])
+        taps_of = lambda j: dtaps.at[:, pl.ds(pl.multiple_of(j * D + head * HEAD_DIM, HEAD_DIM), HEAD_DIM)]
+        mixer_bwd_kernel(
+            blocks, rows_mb, 1, head, *mixer[:12], don, *mixer[12:], dpq, dpk, dpv, dpg, dbeta, taps_of(0),
+            taps_of(1), taps_of(2), d_gain,
+        )
+
+        @pl.when(head >= 2)
+        def _():
+            cross_in(head - 2).wait_send()
+            cross_out(head - 2).wait_send()
+
+        slot = lax.rem(head, 2)
+        acc[...] += nt(dpq[...], wq[...]) + nt(dpk[...], wk[...]) + nt(dpv[...], wv[...]) + nt(dpg[...], wg[...])
+        width = 4 * HEAD_DIM
+        part = jnp.concatenate([dpq[...], dpk[...], dpv[...], dpg[...]], axis=1)
+        near, far = by_core(nn(turned[...], part).reshape(shards // 2, 2, r_gu, width))
+        mine_in[:, :, pl.ds(pl.multiple_of(head * width, width), width)] = near
+        stage_in[slot] = far
+        cross_in(head).start()
+        much = shards // 2 // heads
+        near, far = by_core(tn(on[...], dz[...]).reshape(much, 2, r_gu, D))
+        mine_out[pl.ds(head * much, much)] = near
+        stage_out[slot] = far
+        cross_out(head).start()
+
+    def last_rows():
+        d_beta = dbeta[...].astype(BF16)
+        grad = acc[...] + nn(d_beta, wbeta[...])
+        d_wbeta = lax.dot_general(
+            d_beta, turned[...], (((0,), (1,)), ((), ())), preferred_element_type=F32
+        )
+        load_x.wait()
+        nx, rx = rms(held[...])
+        d_one = jnp.sum(grad * nx, axis=0, keepdims=True)
+        dx = (dresid[...] + rms_back(nx, rx, gain_one[...] * grad)).astype(BF16)
+        sent_dx[...] = nn(deal[...], dx).reshape(shards, share, D).astype(BF16)
+        own_taps, own_gain = 3 * D // shards, D // shards
+        per = 128 // own_gain
+        a, c = iota2((per * own_taps, per * 128), 1), iota2((per * own_taps, per * 128), 0)
+        put_taps = ((a // 128 == c // own_taps) & (a % 128 == c % own_taps)).astype(F32)
+        a, c = iota2((128, per * 128), 1), iota2((128, per * 128), 0)
+        put_gain = ((a // 128 == c // own_gain) & (a % 128 == c % own_gain)).astype(F32)
+        lane = iota2((1, 128), 1)
+        row8 = iota2((8, 128), 0)
+        shared = jnp.where(row8 == 6, d_gain[...], jnp.where((row8 == 7) & (lane == 0), loss[...], 0.0))
+        for g in range(shards // per):
+            top = jnp.concatenate(
+                [dtaps[:, g * per * own_taps : (g + 1) * per * own_taps],
+                 jnp.zeros((8 - CONV, per * own_taps), F32)], axis=0
+            )
+            cols = slice(g * 128, (g + 1) * 128)
+            gains = jnp.where(row8 == 4, d_one[:, cols], jnp.where(row8 == 5, d_two[:, cols], 0.0))
+            upper = mm(top, put_taps, 1, 0) + mm(gains, put_gain, 1, 0)
+            lower = mm(d_wbeta[:, cols], put_gain, 1, 0)
+            for i in range(per):
+                small[g * per + i, 0:8, :] = upper[:, i * 128 : (i + 1) * 128] + shared
+                small[g * per + i, 8:16, :] = lower[:, i * 128 : (i + 1) * 128]
+
+    last = chunks + heads - 1
+    half_way, done = chunks // 2 - 1, chunks - 1
+    starts = link_plan(half_way, done, last, heads)
+    timed = []
+    for n in range(len(pieces)):
+        for k in range(net.stages + 1):
+            at = starts[n][k] if k < len(starts[n]) else starts[n][-1] + 2 * (k - len(starts[n]) + 1)
+            timed.append((at, k != net.stages, n, k))
+    timed.sort()
+
+    def act(n, k):
+        if k < net.stages:
+            net.launch(k, n)
+        else:
+            net.finish(n, write)
+
+    for s in sorted({t[0] for t in timed if t[0] < last}):
+
+        @pl.when(step == s)
+        def _(s=s):
+            for at, _, n, k in timed:
+                if at == s:
+                    act(n, k)
+
+    @pl.when(step == last)
+    def _():
+        for at, _, n, k in timed:
+            if at == last:
+                act(n, k)
+        last_rows()
+        give_small.start()
+        tail = [(n, k) for at, _, n, k in timed if at > last]
+        for i, (n, k) in enumerate(tail):
+            act(n, k)
+            if i < DX_PARTS:
+                give_dx.start_part(i, DX_PARTS)
+        give_small.wait()
+        small_sum[...] = jnp.sum(small_got[...], axis=0)
+        give_y.wait()
+        give_dx.wait()
+        for j in (chunks - 2, chunks - 1):
+            cross_gu(j).wait_send()
+        for s in (heads - 2, heads - 1):
+            cross_in(s).wait_send()
+            cross_out(s).wait_send()
+        for n in range(len(pieces)):
+            net.end(n, paired=n == 0)
+
+
+def rear(
+    d_down, sent_y, dy, resid, x, a2_t, a1_t, df, gu, wgu, wdown, gain_two, gain_one, wout, win, on, wbeta, deal, loss,
+    proj, beta_pre, taps, gain, mask, segc, segr, saved, blocks, shards, collective_id,
+):
+    rows = x.shape[0]
+    rows_mb, share = rows // blocks, rows // shards
+    chunks = FF // SLICE
+    anywhere = pl.BlockSpec(memory_space=pl.ANY)
+    once = pl.Buffered(MIXER_BUFFERS)
+    full = lambda shape: pl.BlockSpec(shape, lambda s: (0,) * len(shape))
+    early = lambda s: jnp.minimum(s, chunks - 1)
+    late = lambda s: jnp.maximum(s - chunks, 0)
+    lane_e = lambda r, w, off=0: pl.BlockSpec((r, w), lambda s: (0, off + early(s)))
+    lane_l = lambda r, w, off=0: pl.BlockSpec((r, w), lambda s: (0, off + late(s)), pipeline_mode=once)
+    mat = pl.BlockSpec((1, blocks, rows_mb, rows_mb), lambda s: (late(s), 0, 0, 0), pipeline_mode=pl.Buffered(1))
+    tap = lambda k: pl.BlockSpec((CONV, HEAD_DIM), lambda s: (0, k * HEADS + late(s)))
+    r_down, r = FF // shards, D // shards
+    a, b = chunks // 2 * 2 * SLICE, 4 * D // 2
+    pieces = [(0, 0, D), (1, 0, a), (1, a, 2 * FF - a), (2, 0, b), (2, b, b), (3, 0, D)]
+    shapes = [(r_down, D), (r, 2 * FF), (r, 4 * D), (r, D)]
+    f32 = lambda *shape: jax.ShapeDtypeStruct(shape, F32)
+    bf = lambda *shape: jax.ShapeDtypeStruct(shape, BF16)
+    vm, dma = pltpu.VMEM, pltpu.SemaphoreType.DMA
+    hd = HEAD_DIM
+    half = shards // 2
+    return pl.pallas_call(
+        functools.partial(rear_kernel, shards, blocks, rows_mb, pieces),
+        grid=(chunks + HEADS,),
+        in_specs=[
+            anywhere, anywhere, anywhere, anywhere, anywhere, anywhere, anywhere, full((rows, D)),
+            lane_e(rows, SLICE), lane_e(rows, SLICE, chunks), lane_e(D, SLICE), lane_e(D, SLICE, chunks),
+            pl.BlockSpec((SLICE, D), lambda s: (early(s), 0)), full((1, D)), full((1, D)),
+            pl.BlockSpec((hd, D), lambda s: (late(s), 0), pipeline_mode=pl.Buffered(1)), lane_l(D, hd), lane_l(D, hd, HEADS),
+            lane_l(D, hd, 2 * HEADS), lane_l(D, hd, 3 * HEADS), lane_l(rows, hd),
+            full((HEADS, D)), full((rows, rows)), full((1, 1)),
+            lane_l(rows, hd), lane_l(rows, hd), lane_l(rows, hd), lane_l(rows, hd), full((rows, HEADS)), tap(0),
+            tap(1), tap(2), full((1, hd)), full((rows, 8)), full((rows, 1)), full((1, rows)), lane_l(rows, hd),
+            mat, mat, mat, mat,
+        ],
+        out_specs=[full(s) for s in shapes] + [anywhere, anywhere, full((16, 128))],
+        out_shape=[f32(*s) for s in shapes] + [bf(shards, share, D), bf(shards, share, D), f32(16, 128)],
+        scratch_shapes=[vm((half,) + s, BF16) for s in shapes] + [
+            vm((2, half, r, 2 * SLICE), BF16), vm((2, half, r, 4 * hd), BF16), vm((2, half // HEADS, r, D), BF16),
+            vm((rows, D), F32), vm((rows, D), F32), vm((rows, D), F32), vm((rows, D), BF16), vm((rows, hd), F32),
+            vm((rows, hd), BF16), vm((rows, hd), BF16), vm((rows, hd), BF16), vm((rows, hd), BF16),
+            vm((D, rows), BF16), vm((rows, HEADS), F32), vm((CONV, 3 * D), F32), vm((1, hd), F32), vm((1, D), F32),
+            vm((shards, share, D), BF16), vm((shards, 16, 128), F32), vm((shards, 16, 128), F32),
+            dma, dma((3,)), dma((2,)), dma((2,)), dma((2,)),
+        ] + [dma] * 9 + Scatter.semaphores(shards, len(pieces)) + Scatter.buffers(shards, shapes),
+        compiler_params=pltpu.CompilerParams(
+            collective_id=collective_id, has_side_effects=True, vmem_limit_bytes=62 << 20
+        ),
+        name="rear",
+    )(d_down.reshape(half, 2, r_down, D), sent_y, dy, resid, x, a2_t, a1_t, df, gu, gu, wgu, wgu, wdown, gain_two, gain_one,
+      wout, win, win, win, win, on, wbeta, deal, loss, *proj, beta_pre, taps, taps, taps, gain, mask, segc, segr,
+      *saved)
+
+
 def scatter_kernel(shards, count, *refs):
     grads, sent, out, got = refs[:count], refs[count], refs[count + 1 : 2 * count + 1], refs[2 * count + 1]
     refs = refs[2 * count + 2 :]
@@ -1205,7 +1514,7 @@
         )
         gain_out = out_gain.astype(F32)[None, :]
         (win, wout, wdown, wgu, *proj, beta_pre, on, o, ainv, u, p, l, resid, a2, x, info, later, taps,
-         gain_one, gain_two, wbeta, segc, segr, mask, a1) = front(
+         gain_one, gain_two, wbeta, segc, segr, mask, a1, a1_t, a2_t) = front(
             [w_in, w_out, w_down, w_gu], small_block, tokens, jnp.concatenate([cotangent, teacher], axis=1),
             deal_rows, valid_mask, lengths, gain_out, shards, 0,
         )
@@ -1224,7 +1533,6 @@
         deal = (place[None, :] == jnp.arange(rows)[:, None]).astype(BF16)
         m = jnp.sum(deal.astype(F32) * info[:, 0][None, :], axis=1, keepdims=True)
         gain_one, gain_two = gain_one[0], gain_two[0]
-        wbeta = wbeta.T
     else:
         target = deal_rows // rows
         spot = deal_rows % rows
@@ -1300,45 +1608,60 @@
     loss_part = jnp.sum(m * errors * errors)
     dy = g + (rows * shards / counted) * m * errors
     df = dy.astype(BF16)
-    (g_down, g_gu, dwq, dwk, dwv, dwg, dw_out, d_wbeta, dx, d_gain_two, d_gain_one, dtq, dtk, dtv,
-     d_gain_out) = backward(
-        tn(hid, df, BF16), df, a2, gu, wgu, wdown, dy, resid, gain_two[None, :], wout, win, a1, on, x,
-        gain_one[None, :], wbeta, proj, beta_pre, taps, gain_out, mask, segc, segr, saved, blocks, shards,
-        1,
-    )
-    back = jnp.concatenate([y.astype(BF16), dx], axis=1)
-    back = nn(deal_t, back).astype(BF16).reshape(shards, share, 2 * D)
-    (g_out, *g_in), back = scatter([dw_out, dwq, dwk, dwv, dwg], back, shards, 3)
-    g_in = jnp.concatenate(g_in, axis=1)
-    back = nn(sort_t, back.reshape(rows, 2 * D)).astype(BF16)
-    output, input_grad = back[:, :D], back[:, D:]
-
-    d_taps = jnp.concatenate([dtq, dtk, dtv], axis=1)
-    tail = jnp.concatenate([d_gain_out.reshape(-1), loss_part.reshape(1)])
-    extra = jnp.concatenate(
-        [
-            d_taps.reshape(CONV, shards, -1).swapaxes(0, 1).reshape(shards, a),
-            d_wbeta.reshape(shards, b),
-            d_gain_one.reshape(shards, c),
-            d_gain_two.reshape(shards, c),
-            jnp.broadcast_to(tail[None], (shards, tail.shape[0])),
-        ],
-        axis=1,
-    )
-    padded = -(-extra.shape[1] // 128) * 128
-    extra = jnp.pad(extra, ((0, 0), (0, padded - extra.shape[1])))
-    summed = jnp.sum(
-        lax.all_to_all(
-            extra.reshape(shards, padded // 128, 128), AXES, split_axis=0, concat_axis=0, tiled=True
-        ),
-        axis=0,
-    ).reshape(-1)
-    g_taps = summed[:a].reshape(CONV, -1)
-    g_beta = summed[a : a + b].reshape(-1, HEADS)
-    g_gain_one = summed[a + b : a + b + c]
-    g_gain_two = summed[a + b + c : a + b + 2 * c]
-    g_gain_out = summed[a + b + 2 * c : a + b + 2 * c + HEAD_DIM]
-    loss = summed[a + b + 2 * c + HEAD_DIM] / (D * counted)
+    if share % 8 == 0 and (D // shards) % 16 == 0:
+        sent_y = nn(deal_t, y.astype(BF16)).astype(BF16).reshape(shards, share, D)
+        g_down, g_gu, g_in, g_out, got_y, got_dx, summed = rear(
+            tn(hid, df, BF16), sent_y, dy, resid, x, a2_t, a1_t, df, gu, wgu, wdown, gain_two[None, :], gain_one[None, :],
+            wout, win, on, wbeta, deal_t, loss_part.reshape(1, 1), proj, beta_pre, taps, gain_out, mask, segc,
+            segr, saved, blocks, shards, 1,
+        )
+        output = nn(sort_t, got_y.reshape(rows, D)).astype(BF16)
+        input_grad = nn(sort_t, got_dx.reshape(rows, D)).astype(BF16)
+        own = D // shards
+        g_taps = summed[:CONV, : 3 * own]
+        g_gain_one, g_gain_two = summed[4, :own], summed[5, :own]
+        g_gain_out, loss = summed[6], summed[7, 0] / (D * counted)
+        g_beta = summed[8:, :own].T
+    else:
+        (g_down, g_gu, dwq, dwk, dwv, dwg, dw_out, d_wbeta, dx, d_gain_two, d_gain_one, dtq, dtk, dtv,
+         d_gain_out) = backward(
+            tn(hid, df, BF16), df, a2, gu, wgu, wdown, dy, resid, gain_two[None, :], wout, win, a1, on, x,
+            gain_one[None, :], wbeta, proj, beta_pre, taps, gain_out, mask, segc, segr, saved, blocks, shards,
+            1,
+        )
+        back = jnp.concatenate([y.astype(BF16), dx], axis=1)
+        back = nn(deal_t, back).astype(BF16).reshape(shards, share, 2 * D)
+        (g_out, *g_in), back = scatter([dw_out, dwq, dwk, dwv, dwg], back, shards, 3)
+        g_in = jnp.concatenate(g_in, axis=1)
+        back = nn(sort_t, back.reshape(rows, 2 * D)).astype(BF16)
+        output, input_grad = back[:, :D], back[:, D:]
+
+        d_taps = jnp.concatenate([dtq, dtk, dtv], axis=1)
+        tail = jnp.concatenate([d_gain_out.reshape(-1), loss_part.reshape(1)])
+        extra = jnp.concatenate(
+            [
+                d_taps.reshape(CONV, shards, -1).swapaxes(0, 1).reshape(shards, a),
+                d_wbeta.reshape(shards, b),
+                d_gain_one.reshape(shards, c),
+                d_gain_two.reshape(shards, c),
+                jnp.broadcast_to(tail[None], (shards, tail.shape[0])),
+            ],
+            axis=1,
+        )
+        padded = -(-extra.shape[1] // 128) * 128
+        extra = jnp.pad(extra, ((0, 0), (0, padded - extra.shape[1])))
+        summed = jnp.sum(
+            lax.all_to_all(
+                extra.reshape(shards, padded // 128, 128), AXES, split_axis=0, concat_axis=0, tiled=True
+            ),
+            axis=0,
+        ).reshape(-1)
+        g_taps = summed[:a].reshape(CONV, -1)
+        g_beta = summed[a : a + b].reshape(-1, HEADS)
+        g_gain_one = summed[a + b : a + b + c]
+        g_gain_two = summed[a + b + c : a + b + 2 * c]
+        g_gain_out = summed[a + b + 2 * c : a + b + 2 * c + HEAD_DIM]
+        loss = summed[a + b + 2 * c + HEAD_DIM] / (D * counted)
 
     return (
         output, input_grad, g_in, g_beta, g_taps, g_out, g_gain_one, g_gain_out, g_gain_two, g_gu,

time: 373 us -> 348 us (0.933)
  Pallas kernels: 318 us -> 298 us
    pallas_call x2 -> x1, Pallas kernels: 167 us -> 148 us  [rear(): pl.pallas_call(functools.partial(rear_kernel, shards, blocks, rows_mb, pi...]
    dot_general x4 -> x5, matrix products: 16.2 us -> 15.4 us  [nn(): return jnp.dot(left, right, preferred_element_type=F32)]
  transfers between devices with their start and end apart: 1 -> 0, of which waited for: 0 -> 0; matrix products, arithmetic and copies ran while one was open for 1% -> 0% of each run, Pallas kernels for 19% -> 0%
where the time goes in v4:
time: 348 us; the launch traced here: 347 us
  Pallas kernels  298 us (86%)
  matrix products  19.6 us (6%)
  local copies, waits for them, and re-layouts  15.5 us (4%)
  other arithmetic  9.87 us (3%)
  between operations  3.91 us (1%)
    pallas_call x1, Pallas kernels, front(): pl.pallas_call(functools.partial(front_kernel, shards, blocks, rows_mb, s...  151 us
    pallas_call x1, Pallas kernels, rear(): pl.pallas_call(functools.partial(rear_kernel, shards, blocks, rows_mb, pi...  148 us
    dot_general x5, matrix products, nn(): return jnp.dot(left, right, preferred_element_type=F32)  15.4 us
    unnamed x24, local copies, waits for them, and re-layouts  7.23 us

profile of v4, /device:TPU:0, one launch (start us, length us, event | category | flops | bytes accessed | tf_op | source)
XLA Modules:
  0.0 347.3 jit_solution(15063895839693520393)
XLA Ops:
  0.6 1.2 bitcast_convert_fusion.refs_10_.refs_32_
  1.8 2.3 pad_maximum_fusion.refs_6_
  5.5 1.3 fusion.13.refs_4_
  6.7 150.8 %front.1 = (bf16[16,2,32,4096]{3,2,1,0:T(8,128)(2,1)}, bf16[16,2,32,1024]{3,2,1,0:T(8,128)(2,1)}, bf16[16,2,88,1024]{3,2,1,0:T(8,128)(2,1)}, bf16[16,2,32,5632]{...) custom-call(bf16[32,4096]{1,0:T(8,128)(2,1)} %refs_0_.1, ...), custom_call_target="tpu_custom_call" | custom-call | tf_op jit(solution)/shard_map/front/pallas_call | solution.py:889
  157.6 1.2 convert_reduce_fusion.1
  158.8 1.0 slice_reduce_fusion
  159.9 1.0 slice.42
  162.2 6.5 %fusion.24.refs_8_.refs_9_ = f32[256,5632]{1,0:T(8,128)S(1)} fusion(bf16[256,1024]{1,0:T(8,128)(2,1)} %get-tuple-element.48, bf16[1024,5632]{1,0:T(8,128)(2,1)} %bitcast.42), kind=kOutput, calls=%fused_computation.56 | convolution fusion | flops 2952790016 | bytes 17825792 | tf_op jit(solution)/shard_map/dot_general | solution.py:1483
  168.8 0.9 fusion
  169.6 2.0 copy-done
  171.7 1.1 copy-done.7
  172.7 3.4 fusion.23
  176.2 1.1 fusion.1.refs_1_
  177.3 4.2 %fusion.25 = bf16[2816,1024]{1,0:T(8,128)(2,1)} fusion(bf16[256,2816]{1,0:T(8,128)(2,1)S(1)} %fusion, bf16[256,1024]{1,0:T(8,128)(2,1)S(1)} %get-tuple-element.84.refs_7_), kind=kOutput, calls=%fused_computation.57 | convolution fusion | flops 1476395008 | bytes 7733248 | tf_op jit(solution)/shard_map/dot_general | solution.py:1479
  182.2 147.7 %rear.1 = (f32[88,1024]{1,0:T(8,128)}, f32[32,5632]{1,0:T(8,128)}, f32[32,4096]{1,0:T(8,128)}, f32[32,1024]{1,0:T(8,128)}, bf16[32,8,1024]{2,1,0:T(8,128)(2,1)},...) custom-call(bf16[16,2,88,1024]{3,2,1,0:T(8,128)(2,1)} %bitcast.45, bf16[32,8,1024]{2,1,0:T(8,128)(2,1)} %fusion.1.refs_1_, ...), custom_call_target="tpu_custom_call" | custom-call | tf_op jit(solution)/shard_map/rear/pallas_call | solution.py:1379
  329.9 1.3 slice.51
  332.8 2.2 convolution_convert_fusion
  334.9 2.2 convolution_convert_fusion.1
  337.1 1.3 slice_bitcast_fusion
  338.4 1.3 slice.47
  339.6 1.3 slice_bitcast_fusion.1
  340.9 1.2 slice_bitcast_fusion.2
  342.1 1.9 copy.31
  344.6 0.9 copy.33
  (30 shorter events, 4.5 us)
Async XLA Ops:
  157.6 14.1 %slice-start = ((s8[5767168]{0:T(1024)(128)(4,1)}), s8[1572864]{0:T(1024)(128)(4,1)S(1)}, s32[]{:S(2)}) async-start(s8[5767168]{0:T(1024)(128)(4,1)} %bitcast.47), calls=%async_computation | async-start | bytes 3145728
  162.2 9.4 %slice-start.1 = ((s8[5767168]{0:T(1024)(128)(4,1)}), s8[4194304]{0:T(1024)(128)(4,1)S(1)}, s32[]{:S(2)}) async-start(s8[5767168]{0:T(1024)(128)(4,1)} %bitcast.47), calls=%async_computation.1 | async-start | bytes 8388608
  168.7 2.9 copy-start
  168.7 2.9 copy-start.2
  168.8 4.0 %copy-start.7 = (f32[256,2048]{1,0:T(8,128)S(1)}, f32[256,2048]{1,0:T(8,128)}, u32[]{:S(2)}) copy-start(f32[256,2048]{1,0:T(8,128)} %get-tuple-element.50) | copy-start | bytes 6291460
  176.2 5.3 %copy-start.1 = (bf16[256,1024]{1,0:T(8,128)(2,1)}, bf16[256,1024]{1,0:T(8,128)(2,1)S(1)}, u32[]{:S(2)}) copy-start(bf16[256,1024]{1,0:T(8,128)(2,1)S(1)} %get-tuple-element.84.refs_7_) | copy-start | bytes 1572868
  182.2 150.3 %copy-start.6 = (s32[256]{0:T(256)S(1)}, s32[256]{0:T(256)}, u32[]{:S(2)}) copy-start(s32[256]{0:T(256)} %param.19) | copy-start | bytes 3076
  329.9 14.0 %copy-start.5 = (f32[32,1024]{1,0:T(8,128)S(1)}, f32[32,1024]{1,0:T(8,128)}, u32[]{:S(2)}) copy-start(f32[32,1024]{1,0:T(8,128)} %get-tuple-element.111) | copy-start | bytes 393220
  329.9 14.7 %copy-start.3 = (f32[32,5632]{1,0:T(8,128)S(1)}, f32[32,5632]{1,0:T(8,128)}, u32[]{:S(2)}) copy-start(f32[32,5632]{1,0:T(8,128)} %get-tuple-element.115) | copy-start | bytes 2162692
  329.9 15.5 %copy-start.4 = (f32[88,1024]{1,0:T(8,128)S(1)}, f32[88,1024]{1,0:T(8,128)}, u32[]{:S(2)}) copy-start(f32[88,1024]{1,0:T(8,128)} %get-tuple-element.116) | copy-start | bytes 1081348

commit v5 on v4

--- a/solution.py
+++ b/solution.py
@@ -688,10 +688,10 @@
 
 
 def front_kernel(shards, blocks, rows_mb, split, *refs):
-    (own_in, own_out, own_down, own_gu, small, tokens, later_rows, deal_row, valid_row, lengths, gain), refs = refs[:11], refs[11:]
-    (full_in, full_out, full_down, full_gu, pq, pk, pv, pg, beta, on, o, ainv, u, p, l, resid, a2, x, info, gt, taps,
-     gain_one, gain_two, wbeta, segc, segr, mask, a1, a1_t, a2_t), refs = refs[:30], refs[30:]
-    (sent, got, sent_gt, got_gt, got_small, wbuf, wout, deal, w_sem, out_sem), refs = refs[:10], refs[10:]
+    (own_in, own_out, own_down, own_gu, small, tokens, cotangent, teacher, deal_row, valid_row, lengths, gain), refs = refs[:12], refs[12:]
+    (full_in, full_out, full_down, full_gu, pq, pk, pv, pg, beta, on, o, ainv, u, p, l, resid, a2, x, m, counted, deal, sort_t, gt, taps,
+     gain_one, gain_two, wbeta, segc, segr, mask, a1, a1_t, a2_t), refs = refs[:33], refs[33:]
+    (sent, got, sent_gt, got_gt, got_small, wbuf, wout, w_sem, out_sem), refs = refs[:9], refs[9:]
     sems, deal_sems, later_sems, small_sems = refs[:5], refs[5:8], refs[8:11], refs[11:14]
     step = pl.program_id(0)
     steps = HEADS // PAIR
@@ -753,20 +753,17 @@
         target_c = column(target)
         rank = jnp.sum(jnp.where((target == target_c) & (col < row), 1.0, 0.0), axis=1, keepdims=True)
         slot = target_c * share + rank
-        sort_t = (slot == col.astype(F32)).astype(BF16)
+        sort_t[...] = (slot == col.astype(F32)).astype(BF16)
         lane = iota2((rows, 128), 1)
         notes = jnp.where(
             lane == 0, column(valid),
             jnp.where(lane == 1, column(dealt - target * rows), jnp.where(lane == 2, jnp.sum(valid), 0.0)),
         ).astype(BF16)
-        sent[:, :, :D] = tn(sort_t, tokens[...]).reshape(shards, share, D).astype(BF16)
-        sent[:, :, D:] = tn(sort_t, notes).reshape(shards, share, 128).astype(BF16)
+        sent[:, :, :D] = tn(sort_t[...], tokens[...]).reshape(shards, share, D).astype(BF16)
+        sent[:, :, D:] = tn(sort_t[...], notes).reshape(shards, share, 128).astype(BF16)
         weights.step(1, between(1))
-        half = later_rows.shape[1] // 2
-        for at in (0, half):
-            sent_gt[:, :, at : at + half] = (
-                tn(sort_t, later_rows[:, at : at + half]).reshape(shards, share, half).astype(BF16)
-            )
+        for at, part in ((0, cotangent), (D, teacher)):
+            sent_gt[:, :, at : at + D] = tn(sort_t[...], part[...]).reshape(shards, share, D).astype(BF16)
         weights.step(2, between(2))
         at_row, at_col = iota2((rows, 1), 0), iota2((1, rows), 1)
         seg_c, seg_r = jnp.zeros((rows, 1), F32), jnp.zeros((1, rows), F32)
@@ -811,8 +808,10 @@
         first_send.wait()
         flat = got[...].astype(F32).reshape(rows, D + 128)
         notes = flat[:, D:]
-        info[...] = notes
         deal[...] = (notes[:, 1:2] == col.astype(F32)).astype(BF16)
+        m[...] = tn(deal[...], notes.astype(BF16))[:, :1]
+        firsts = jnp.where(lax.rem(iota2((rows, 1), 0), share) == 0, notes[:, 2:3], 0.0)
+        counted[...] = jnp.sum(firsts, axis=0, keepdims=True)
         x_now = tn(deal[...], flat[:, :D].astype(BF16))
         x[...] = x_now
         a1[...] = (rms(x_now)[0] * gain_one[...]).astype(BF16)
@@ -861,7 +860,7 @@
                 weights.end(of_in + split[1])
 
 
-def front(weights, small, tokens, later_rows, deal_rows, valid_mask, lengths, gain, shards, collective_id):
+def front(weights, small, tokens, cotangent, teacher, deal_rows, valid_mask, lengths, gain, shards, collective_id):
     rows, blocks = tokens.shape[0], lengths.shape[0]
     rows_mb, share = rows // blocks, rows // shards
     width = PAIR * HEAD_DIM
@@ -879,7 +878,8 @@
     ] + [(wide, one)] * 4 + [
         (f32(rows, HEADS), full((rows, HEADS))), (bf(rows, D), full((rows, D))), (wide, one),
         (square, mat), (square, mat), (square, mat), (square, mat), (wide, full((rows, D))),
-        (bf(rows, D), full((rows, D))), (wide, full((rows, D))), (f32(rows, 128), full((rows, 128))),
+        (bf(rows, D), full((rows, D))), (wide, full((rows, D))), (f32(rows, 1), full((rows, 1))),
+        (f32(1, 1), full((1, 1))), (bf(rows, rows), full((rows, rows))), (bf(rows, rows), full((rows, rows))),
         (f32(rows, 2 * D), full((rows, 2 * D))), (f32(CONV, 3 * D), full((CONV, 3 * D))),
         (f32(1, D), full((1, D))), (f32(1, D), full((1, D))), (bf(8, D), full((8, D))),
         (jax.ShapeDtypeStruct((rows, 1), jnp.int32), full((rows, 1))),
@@ -890,7 +890,7 @@
         functools.partial(front_kernel, shards, blocks, rows_mb, split),
         grid=(HEADS // PAIR,),
         in_specs=[anywhere] * 4 + [
-            full(small.shape), full((rows, D)), full((rows, 2 * D)), full((1, rows)), full((1, rows)),
+            full(small.shape), full((rows, D)), full((rows, D)), full((rows, D)), full((1, rows)), full((1, rows)),
             full(lengths.shape), full((1, HEAD_DIM)),
         ],
         out_specs=[s for _, s in outs],
@@ -900,13 +900,13 @@
             vm((shards, share, 2 * D), BF16), vm((shards, share, 2 * D), BF16),
             vm((shards,) + small.shape, BF16),
             vm((2, 4, shards // 2, 2, D // shards, width), BF16),
-            vm((shards // 2, 2, D // shards, D), BF16), vm((rows, rows), BF16), dma((2, 4)), dma,
+            vm((shards // 2, 2, D // shards, D), BF16), dma((2, 4)), dma,
         ] + Gather.semaphores(shards, pieces) + [dma] * 9,
         compiler_params=pltpu.CompilerParams(
             collective_id=collective_id, has_side_effects=True, vmem_limit_bytes=58 << 20
         ),
         name="front",
-    )(*weights, small, tokens, later_rows, deal_rows[None, :], valid_mask[None, :], lengths, gain)
+    )(*weights, small, tokens, cotangent, teacher, deal_rows[None, :], valid_mask[None, :], lengths, gain)
 
 
 def backward_kernel(shards, blocks, rows_mb, pieces, *refs):
@@ -1108,8 +1108,8 @@
 
 def link_plan(half_way, done, last, heads):
     return [
-        [3, 8, 10, 12], [half_way + 2, done, done + 2], [done + 1, done + 3], [done + heads // 2 + 2], [last],
-        [last],
+        [4, 9, 11, 12], [half_way + 3, done + 1, done + 2], [done + 1, done + 3], [done + 6], [last], [last],
+        [done + 5],
     ]
 
 
@@ -1161,11 +1161,11 @@
     def cross_in(s):
         width = 4 * HEAD_DIM
         cols = pl.ds(pl.multiple_of(s * width, width), width)
-        return cross(stage_in, lax.rem(s, 2), other[2].at[:, :, cols], in_sem, 3 + lax.div(s, heads // 2))
+        return cross(stage_in, lax.rem(s, 2), other[2].at[:, :, cols], in_sem, 3 + lax.div(s, heads // 2) + lax.div(s, 3 * heads // 4))
 
     def cross_out(s):
         much = shards // 2 // heads
-        return cross(stage_out, lax.rem(s, 2), other[3].at[pl.ds(s * much, much)], out_sem, 5)
+        return cross(stage_out, s % 2, other[3].at[pl.ds(s * much, much)], out_sem, 6)
 
     def by_core(value):
         first, second = value[:, 0], value[:, 1]
@@ -1253,7 +1253,6 @@
         @pl.when(head >= 2)
         def _():
             cross_in(head - 2).wait_send()
-            cross_out(head - 2).wait_send()
 
         slot = lax.rem(head, 2)
         acc[...] += nt(dpq[...], wq[...]) + nt(dpk[...], wk[...]) + nt(dpv[...], wv[...]) + nt(dpg[...], wg[...])
@@ -1263,11 +1262,20 @@
         mine_in[:, :, pl.ds(pl.multiple_of(head * width, width), width)] = near
         stage_in[slot] = far
         cross_in(head).start()
+
+    @pl.when(step == chunks)
+    def _():
         much = shards // 2 // heads
-        near, far = by_core(tn(on[...], dz[...]).reshape(much, 2, r_gu, D))
-        mine_out[pl.ds(head * much, much)] = near
-        stage_out[slot] = far
-        cross_out(head).start()
+        for s in range(heads):
+            if s >= 2:
+                cross_out(s - 2).wait_send()
+            part = tn(on[:, s * HEAD_DIM : (s + 1) * HEAD_DIM], dz[...])
+            near, far = by_core(part.reshape(much, 2, r_gu, D))
+            mine_out[s * much : (s + 1) * much] = near
+            stage_out[s % 2] = far
+            cross_out(s).start()
+        for s in (heads - 2, heads - 1):
+            cross_out(s).wait_send()
 
     def last_rows():
         d_beta = dbeta[...].astype(BF16)
@@ -1346,7 +1354,6 @@
             cross_gu(j).wait_send()
         for s in (heads - 2, heads - 1):
             cross_in(s).wait_send()
-            cross_out(s).wait_send()
         for n in range(len(pieces)):
             net.end(n, paired=n == 0)
 
@@ -1369,7 +1376,8 @@
     tap = lambda k: pl.BlockSpec((CONV, HEAD_DIM), lambda s: (0, k * HEADS + late(s)))
     r_down, r = FF // shards, D // shards
     a, b = chunks // 2 * 2 * SLICE, 4 * D // 2
-    pieces = [(0, 0, D), (1, 0, a), (1, a, 2 * FF - a), (2, 0, b), (2, b, b), (3, 0, D)]
+    c = b // 2
+    pieces = [(0, 0, D), (1, 0, a), (1, a, 2 * FF - a), (2, 0, b), (2, b, c), (2, b + c, c), (3, 0, D)]
     shapes = [(r_down, D), (r, 2 * FF), (r, 4 * D), (r, D)]
     f32 = lambda *shape: jax.ShapeDtypeStruct(shape, F32)
     bf = lambda *shape: jax.ShapeDtypeStruct(shape, BF16)
@@ -1384,7 +1392,7 @@
             lane_e(rows, SLICE), lane_e(rows, SLICE, chunks), lane_e(D, SLICE), lane_e(D, SLICE, chunks),
             pl.BlockSpec((SLICE, D), lambda s: (early(s), 0)), full((1, D)), full((1, D)),
             pl.BlockSpec((hd, D), lambda s: (late(s), 0), pipeline_mode=pl.Buffered(1)), lane_l(D, hd), lane_l(D, hd, HEADS),
-            lane_l(D, hd, 2 * HEADS), lane_l(D, hd, 3 * HEADS), lane_l(rows, hd),
+            lane_l(D, hd, 2 * HEADS), lane_l(D, hd, 3 * HEADS), full((rows, D)),
             full((HEADS, D)), full((rows, rows)), full((1, 1)),
             lane_l(rows, hd), lane_l(rows, hd), lane_l(rows, hd), lane_l(rows, hd), full((rows, HEADS)), tap(0),
             tap(1), tap(2), full((1, hd)), full((rows, 8)), full((rows, 1)), full((1, rows)), lane_l(rows, hd),
@@ -1409,6 +1417,35 @@
       *saved)
 
 
+def settle_kernel(
+    got_y, got_dx, sort_t, summed, counted, g_down, g_gu, g_in, g_out,
+    output, input_grad, o_in, o_beta, o_taps, o_out, o_one, o_gain, o_two, o_gu, o_down, loss,
+):
+    shards, share, _ = got_y.shape
+    own = o_one.shape[1]
+    for got, out in ((got_y, output), (got_dx, input_grad)):
+        out[...] = nn(sort_t[...], got[...].astype(F32).reshape(shards * share, D).astype(BF16)).astype(BF16)
+    o_in[...], o_out[...], o_gu[...], o_down[...] = g_in[...], g_out[...], g_gu[...], g_down[...]
+    total = summed[...]
+    o_taps[...] = total[:CONV, : 3 * own]
+    o_one[...], o_two[...], o_gain[...] = total[4:5, :own], total[5:6, :own], total[6:7]
+    loss[...] = total[7:8, :1] / (D * counted[...])
+    o_beta[...] = total[8:].T[:own]
+
+
+def settle(got_y, got_dx, sort_t, summed, counted, g_down, g_gu, g_in, g_out):
+    rows = sort_t.shape[0]
+    own = g_in.shape[0]
+    f32 = lambda *shape: jax.ShapeDtypeStruct(shape, F32)
+    row = jax.ShapeDtypeStruct((rows, D), BF16)
+    return pl.pallas_call(
+        settle_kernel,
+        out_shape=[row, row, f32(*g_in.shape), f32(own, HEADS), f32(CONV, 3 * own), f32(*g_out.shape), f32(1, own),
+                   f32(1, HEAD_DIM), f32(1, own), f32(*g_gu.shape), f32(*g_down.shape), f32(1, 1)],
+        name="settle",
+    )(got_y, got_dx, sort_t, summed, counted, g_down, g_gu, g_in, g_out)
+
+
 def scatter_kernel(shards, count, *refs):
     grads, sent, out, got = refs[:count], refs[count], refs[count + 1 : 2 * count + 1], refs[2 * count + 1]
     refs = refs[2 * count + 2 :]
@@ -1513,25 +1550,15 @@
             [half, jnp.pad(w_beta.T, ((0, 0), (0, 128 - w_beta.shape[0])))], axis=1
         )
         gain_out = out_gain.astype(F32)[None, :]
-        (win, wout, wdown, wgu, *proj, beta_pre, on, o, ainv, u, p, l, resid, a2, x, info, later, taps,
-         gain_one, gain_two, wbeta, segc, segr, mask, a1, a1_t, a2_t) = front(
-            [w_in, w_out, w_down, w_gu], small_block, tokens, jnp.concatenate([cotangent, teacher], axis=1),
-            deal_rows, valid_mask, lengths, gain_out, shards, 0,
+        (win, wout, wdown, wgu, *proj, beta_pre, on, o, ainv, u, p, l, resid, a2, x, m, counted, deal_t, sort_t, later,
+         taps, gain_one, gain_two, wbeta, segc, segr, mask, a1, a1_t, a2_t) = front(
+            [w_in, w_out, w_down, w_gu], small_block, tokens, cotangent, teacher, deal_rows, valid_mask, lengths,
+            gain_out, shards, 0,
         )
         win, wout, wdown, wgu = (w.reshape(-1, w.shape[-1]) for w in (win, wout, wdown, wgu))
         saved = (o, ainv, u, p, l)
-        place = info[:, 1].astype(jnp.int32)
-        counted = jnp.sum(info[::share, 2])
+        counted = counted[0, 0]
         g, t = later[:, :D], later[:, D:]
-        target = deal_rows // rows
-        ahead = (target[None, :] == target[:, None]) & (
-            jnp.arange(rows)[None, :] < jnp.arange(rows)[:, None]
-        )
-        slot = target * share + jnp.sum(ahead.astype(jnp.int32), axis=1)
-        sort_t = (slot[:, None] == jnp.arange(rows)[None, :]).astype(BF16)
-        deal_t = (place[:, None] == jnp.arange(rows)[None, :]).astype(BF16)
-        deal = (place[None, :] == jnp.arange(rows)[:, None]).astype(BF16)
-        m = jnp.sum(deal.astype(F32) * info[:, 0][None, :], axis=1, keepdims=True)
         gain_one, gain_two = gain_one[0], gain_two[0]
     else:
         target = deal_rows // rows
@@ -1615,13 +1642,10 @@
             wout, win, on, wbeta, deal_t, loss_part.reshape(1, 1), proj, beta_pre, taps, gain_out, mask, segc,
             segr, saved, blocks, shards, 1,
         )
-        output = nn(sort_t, got_y.reshape(rows, D)).astype(BF16)
-        input_grad = nn(sort_t, got_dx.reshape(rows, D)).astype(BF16)
-        own = D // shards
-        g_taps = summed[:CONV, : 3 * own]
-        g_gain_one, g_gain_two = summed[4, :own], summed[5, :own]
-        g_gain_out, loss = summed[6], summed[7, 0] / (D * counted)
-        g_beta = summed[8:, :own].T
+        (output, input_grad, g_in, g_beta, g_taps, g_out, g_gain_one, g_gain_out, g_gain_two, g_gu, g_down,
+         loss) = settle(got_y, got_dx, sort_t, summed, counted.reshape(1, 1), g_down, g_gu, g_in, g_out)
+        g_gain_one, g_gain_out, g_gain_two = g_gain_one[0], g_gain_out[0], g_gain_two[0]
+        loss = loss[0, 0]
     else:
         (g_down, g_gu, dwq, dwk, dwv, dwg, dw_out, d_wbeta, dx, d_gain_two, d_gain_one, dtq, dtk, dtv,
          d_gain_out) = backward(

time: 348 us -> 330 us (0.948)
  local copies, waits for them, and re-layouts: 15.5 us -> 5.48 us
  matrix products: 19.6 us -> 15.2 us
  other arithmetic: 9.87 us -> 5.74 us
  Pallas kernels: 298 us -> 302 us
    slice x4 -> x0, local copies, waits for them, and re-layouts: 4.53 us -> none  [the longest x1 1.28 us: local(): g_gain_out, loss = (summed[6], summed[7, 0] / (D * counted))]
    dot_general x5 -> x3, matrix products: 15.4 us -> 11 us  [nn(): return jnp.dot(left, right, preferred_element_type=F32)]
    pallas_call x0 -> x1, Pallas kernels: none -> 4.23 us  [settle(): pl.pallas_call(settle_kernel, out_shape=[row, row, f32(*g_in.shape), f32(...]
    unnamed x24 -> x13, local copies, waits for them, and re-layouts: 7.23 us -> 5.48 us
where the time goes in v5:
time: 330 us; the launch traced here: 329 us
  Pallas kernels  302 us (92%)
  matrix products  15.2 us (5%)
  other arithmetic  5.74 us (2%)
  local copies, waits for them, and re-layouts  5.48 us (2%)
    pallas_call x1, Pallas kernels, front(): pl.pallas_call(functools.partial(front_kernel, shards, blocks, rows_mb, s...  151 us
    pallas_call x1, Pallas kernels, rear(): pl.pallas_call(functools.partial(rear_kernel, shards, blocks, rows_mb, pi...  146 us
    dot_general x3, matrix products, nn(): return jnp.dot(left, right, preferred_element_type=F32)  11 us

profile of v5, /device:TPU:0, one launch (start us, length us, event | category | flops | bytes accessed | tf_op | source)
XLA Modules:
  0.0 329.3 jit_solution(249752169133574614)
XLA Ops:
  0.6 1.2 bitcast_convert_fusion.refs_11_.refs_32_
  1.8 0.7 fusion.14
  2.5 0.7 fusion.11
  3.2 1.3 fusion.5.refs_4_
  4.5 151.0 %front.1 = (bf16[16,2,32,4096]{3,2,1,0:T(8,128)(2,1)}, bf16[16,2,32,1024]{3,2,1,0:T(8,128)(2,1)}, bf16[16,2,88,1024]{3,2,1,0:T(8,128)(2,1)}, bf16[16,2,32,5632]{...) custom-call(bf16[32,4096]{1,0:T(8,128)(2,1)} %refs_0_.1, ...), custom_call_target="tpu_custom_call" | custom-call | tf_op jit(solution)/shard_map/front/pallas_call | solution.py:889
  156.0 1.0 fusion.15
  157.1 0.0 copy-start.5
  157.1 6.5 %fusion.17.refs_8_.refs_9_ = f32[256,5632]{1,0:T(8,128)S(1)} fusion(bf16[256,1024]{1,0:T(8,128)(2,1)} %get-tuple-element.63, bf16[1024,5632]{1,0:T(8,128)(2,1)} %bitcast.33), kind=kOutput, calls=%fused_computation.29 | convolution fusion | flops 2952790016 | bytes 17825792 | tf_op jit(solution)/shard_map/dot_general | solution.py:1520
  163.5 0.0 copy-start
  163.5 0.0 copy-start.1
  163.5 0.0 copy-start.3
  163.6 0.9 fusion
  164.4 2.0 copy-done
  166.5 0.0 copy-done.5
  166.5 1.8 copy-done.1
  168.3 0.3 copy-done.3
  168.5 3.4 %fusion.16 = (bf16[256,1024]{1,0:T(8,128)(2,1)S(1)}, f32[256,1024]{1,0:T(8,128)}, f32[]{:T(128)}, bf16[256,1024]{1,0:T(8,128)(2,1)S(1)}) fusion(f32[256,2048]{1,0:T(8,128)S(1)} %copy-done.5, f32[256]{0:T(256)S(1)} %get-tuple-element.139, f32[256]{0:T(256)S(1)} %get-tuple-element.138, f32[256,1024]{1,0:T(8,128)S(1)} %copy-done.3, ...), kind=kOutput, calls=%fused_computation.28 | convolution fusion | flops 1478754304 | bytes 12453892 | tf_op jit(solution)/shard_map/dot_general | solution.py:1520
  172.0 0.0 copy-done.4
  172.0 1.1 fusion.1.refs_1_
  173.1 4.2 %fusion.18 = bf16[2816,1024]{1,0:T(8,128)(2,1)} fusion(bf16[256,2816]{1,0:T(8,128)(2,1)S(1)} %fusion, bf16[256,1024]{1,0:T(8,128)(2,1)S(1)} %get-tuple-element.140.refs_7_), kind=kOutput, calls=%fused_computation.30 | convolution fusion | flops 1476395008 | bytes 7733248 | tf_op jit(solution)/shard_map/dot_general | solution.py:1516
  177.3 0.0 copy-done.2
  177.3 146.4 %rear.1 = (f32[88,1024]{1,0:T(8,128)}, f32[32,5632]{1,0:T(8,128)}, f32[32,4096]{1,0:T(8,128)}, f32[32,1024]{1,0:T(8,128)}, bf16[32,8,1024]{2,1,0:T(8,128)(2,1)},...) custom-call(bf16[16,2,88,1024]{3,2,1,0:T(8,128)(2,1)} %bitcast.36, bf16[32,8,1024]{2,1,0:T(8,128)(2,1)} %fusion.1.refs_1_, ...), custom_call_target="tpu_custom_call" | custom-call | tf_op jit(solution)/shard_map/rear/pallas_call | solution.py:1387
  323.6 4.2 %settle.1 = (bf16[256,1024]{1,0:T(8,128)(2,1)}, bf16[256,1024]{1,0:T(8,128)(2,1)}, f32[32,4096]{1,0:T(8,128)}, f32[32,8]{1,0:T(8,128)}, f32[4,96]{1,0:T(4,128)},...) custom-call(bf16[32,8,1024]{2,1,0:T(8,128)(2,1)} %get-tuple-element., ...), custom_call_target="tpu_custom_call" | custom-call | tf_op jit(solution)/shard_map/settle/pallas_call | solution.py:1441
  327.9 1.4 copy.28
  (2 shorter events, 0.0 us)
Async XLA Ops:
  157.1 9.4 %copy-start.5 = (f32[256,2048]{1,0:T(8,128)S(1)}, f32[256,2048]{1,0:T(8,128)}, u32[]{:S(2)}) copy-start(f32[256,2048]{1,0:T(8,128)} %get-tuple-element.65) | copy-start | bytes 6291460
  163.5 2.9 copy-start
  163.5 4.7 %copy-start.1 = (bf16[16,2,88,1024]{3,2,1,0:T(8,128)(2,1)S(1)}, bf16[16,2,88,1024]{3,2,1,0:T(8,128)(2,1)}, u32[]{:S(2)}) copy-start(bf16[16,2,88,1024]{3,2,1,0:T(8,128)(2,1)} %get-tuple-element.69) | copy-start | bytes 17301508
  163.5 5.0 %copy-start.3 = (f32[256,1024]{1,0:T(8,128)S(1)}, f32[256,1024]{1,0:T(8,128)}, u32[]{:S(2)}) copy-start(f32[256,1024]{1,0:T(8,128)} %get-tuple-element.68.refs_3_) | copy-start | bytes 3145732
  168.5 3.5 %copy-start.4 = (bf16[256,256]{1,0:T(8,128)(2,1)S(1)}, bf16[256,256]{1,0:T(8,128)(2,1)}, u32[]{:S(2)}) copy-start(bf16[256,256]{1,0:T(8,128)(2,1)} %get-tuple-element.70.refs_22_) | copy-start | bytes 393220
  172.0 5.3 %copy-start.2 = (bf16[256,1024]{1,0:T(8,128)(2,1)}, bf16[256,1024]{1,0:T(8,128)(2,1)S(1)}, u32[]{:S(2)}) copy-start(bf16[256,1024]{1,0:T(8,128)(2,1)S(1)} %get-tuple-element.140.refs_7_) | copy-start | bytes 1572868

commit v6 on v5

--- a/solution.py
+++ b/solution.py
@@ -351,6 +351,7 @@
 X_STEPS = 5
 GT_FROM = 6
 SLICE = 256
+FF_STEP = FF // 2
 MIXER_BUFFERS = 2
 DX_PARTS = 6
 
@@ -1359,7 +1360,7 @@
 
 
 def rear(
-    d_down, sent_y, dy, resid, x, a2_t, a1_t, df, gu, wgu, wdown, gain_two, gain_one, wout, win, on, wbeta, deal, loss,
+    d_down, sent_y, dy, resid, x, a2_t, a1_t, df, gate, up, wgu, wdown, gain_two, gain_one, wout, win, on, wbeta, deal, loss,
     proj, beta_pre, taps, gain, mask, segc, segr, saved, blocks, shards, collective_id,
 ):
     rows = x.shape[0]
@@ -1389,7 +1390,7 @@
         grid=(chunks + HEADS,),
         in_specs=[
             anywhere, anywhere, anywhere, anywhere, anywhere, anywhere, anywhere, full((rows, D)),
-            lane_e(rows, SLICE), lane_e(rows, SLICE, chunks), lane_e(D, SLICE), lane_e(D, SLICE, chunks),
+            lane_e(rows, SLICE), lane_e(rows, SLICE), lane_e(D, SLICE), lane_e(D, SLICE, chunks),
             pl.BlockSpec((SLICE, D), lambda s: (early(s), 0)), full((1, D)), full((1, D)),
             pl.BlockSpec((hd, D), lambda s: (late(s), 0), pipeline_mode=pl.Buffered(1)), lane_l(D, hd), lane_l(D, hd, HEADS),
             lane_l(D, hd, 2 * HEADS), lane_l(D, hd, 3 * HEADS), full((rows, D)),
@@ -1412,9 +1413,73 @@
             collective_id=collective_id, has_side_effects=True, vmem_limit_bytes=62 << 20
         ),
         name="rear",
-    )(d_down.reshape(half, 2, r_down, D), sent_y, dy, resid, x, a2_t, a1_t, df, gu, gu, wgu, wgu, wdown, gain_two, gain_one,
+    )(d_down.reshape(half, 2, r_down, D), sent_y, dy, resid, x, a2_t, a1_t, df, gate, up, wgu, wgu, wdown, gain_two, gain_one,
       wout, win, win, win, win, on, wbeta, deal, loss, *proj, beta_pre, taps, taps, taps, gain, mask, segc, segr,
       *saved)
+
+
+def middle_kernel(
+    scale, a2, wga, wup, wdn, resid, later, m, counted, deal,
+    gate, up, df, dy, sent_y, loss, d_down,
+    hid, acc,
+):
+    step = pl.program_id(0)
+    chunks = FF // FF_STEP
+
+    @pl.when(step == 0)
+    def _():
+        acc[...] = resid[...]
+
+    @pl.when(step < chunks)
+    def _():
+        g, u = nn(a2[...], wga[...]), nn(a2[...], wup[...])
+        gate[...], up[...] = g, u
+        h = (g * sigmoid(g) * u).astype(BF16)
+        hid[step] = h
+        acc[...] += nn(h, wdn[...])
+
+    @pl.when(step == chunks - 1)
+    def _():
+        y = acc[...]
+        errors = y - later[:, D:]
+        masked = m[...] * errors
+        loss[...] = jnp.sum(jnp.sum(masked * errors, axis=1, keepdims=True), axis=0, keepdims=True)
+        grad = later[:, :D] + (scale / counted[...]) * masked
+        dy[...] = grad
+        df[...] = grad.astype(BF16)
+        sent_y[...] = nn(deal[...], y.astype(BF16)).reshape(sent_y.shape).astype(BF16)
+
+    @pl.when(step >= chunks)
+    def _():
+        d_down[...] = tn(hid[step - chunks], df[...]).astype(BF16)
+
+
+def middle(a2, wgu, wdown, resid, later, m, counted, deal, shards):
+    rows = a2.shape[0]
+    share, chunks = rows // shards, FF // FF_STEP
+    full = lambda shape: pl.BlockSpec(shape, lambda s: (0,) * len(shape))
+    early = lambda s: jnp.minimum(s, chunks - 1)
+    lane = lambda r, off=0: pl.BlockSpec((r, FF_STEP), lambda s: (0, off + early(s)))
+    f32 = lambda *shape: jax.ShapeDtypeStruct(shape, F32)
+    bf = lambda *shape: jax.ShapeDtypeStruct(shape, BF16)
+    return pl.pallas_call(
+        functools.partial(middle_kernel, float(rows * shards)),
+        grid=(2 * chunks,),
+        in_specs=[
+            full((rows, D)), lane(D), lane(D, chunks), pl.BlockSpec((FF_STEP, D), lambda s: (early(s), 0)),
+            full((rows, D)), full((rows, 2 * D)), full((rows, 1)), full((1, 1)), full((rows, rows)),
+        ],
+        out_specs=[
+            lane(rows), lane(rows), full((rows, D)), full((rows, D)), full((shards, share, D)), full((1, 1)),
+            pl.BlockSpec((FF_STEP, D), lambda s: (jnp.maximum(s - chunks, 0), 0)),
+        ],
+        out_shape=[
+            f32(rows, FF), f32(rows, FF), bf(rows, D), f32(rows, D), bf(shards, share, D), f32(1, 1), bf(FF, D),
+        ],
+        scratch_shapes=[pltpu.VMEM((chunks, rows, FF_STEP), BF16), pltpu.VMEM((rows, D), F32)],
+        compiler_params=pltpu.CompilerParams(vmem_limit_bytes=62 << 20),
+        name="middle",
+    )(a2, wgu, wgu, wdown, resid, later, m, counted, deal)
 
 
 def settle_kernel(
@@ -1430,7 +1495,7 @@
     o_taps[...] = total[:CONV, : 3 * own]
     o_one[...], o_two[...], o_gain[...] = total[4:5, :own], total[5:6, :own], total[6:7]
     loss[...] = total[7:8, :1] / (D * counted[...])
-    o_beta[...] = total[8:].T[:own]
+    o_beta[...] = total[8:, :own]
 
 
 def settle(got_y, got_dx, sort_t, summed, counted, g_down, g_gu, g_in, g_out):
@@ -1440,7 +1505,7 @@
     row = jax.ShapeDtypeStruct((rows, D), BF16)
     return pl.pallas_call(
         settle_kernel,
-        out_shape=[row, row, f32(*g_in.shape), f32(own, HEADS), f32(CONV, 3 * own), f32(*g_out.shape), f32(1, own),
+        out_shape=[row, row, f32(*g_in.shape), f32(HEADS, own), f32(CONV, 3 * own), f32(*g_out.shape), f32(1, own),
                    f32(1, HEAD_DIM), f32(1, own), f32(*g_gu.shape), f32(*g_down.shape), f32(1, 1)],
         name="settle",
     )(got_y, got_dx, sort_t, summed, counted, g_down, g_gu, g_in, g_out)
@@ -1557,8 +1622,6 @@
         )
         win, wout, wdown, wgu = (w.reshape(-1, w.shape[-1]) for w in (win, wout, wdown, wgu))
         saved = (o, ainv, u, p, l)
-        counted = counted[0, 0]
-        g, t = later[:, :D], later[:, D:]
         gain_one, gain_two = gain_one[0], gain_two[0]
     else:
         target = deal_rows // rows
@@ -1627,26 +1690,28 @@
         saved = (o, ainv, u, p, l)
         later = nn(deal, later.reshape(rows, 2 * D))
         g, t = later[:, :D], later[:, D:]
-    gu = nn(a2, wgu)
-    gate, up = gu[:, :FF], gu[:, FF:]
-    hid = (gate * sigmoid(gate) * up).astype(BF16)
-    y = resid + nn(hid, wdown)
-    errors = y - t
-    loss_part = jnp.sum(m * errors * errors)
-    dy = g + (rows * shards / counted) * m * errors
-    df = dy.astype(BF16)
     if share % 8 == 0 and (D // shards) % 16 == 0:
-        sent_y = nn(deal_t, y.astype(BF16)).astype(BF16).reshape(shards, share, D)
+        gate, up, df, dy, sent_y, loss_part, d_down = middle(
+            a2, wgu, wdown, resid, later, m, counted, deal_t, shards
+        )
         g_down, g_gu, g_in, g_out, got_y, got_dx, summed = rear(
-            tn(hid, df, BF16), sent_y, dy, resid, x, a2_t, a1_t, df, gu, wgu, wdown, gain_two[None, :], gain_one[None, :],
-            wout, win, on, wbeta, deal_t, loss_part.reshape(1, 1), proj, beta_pre, taps, gain_out, mask, segc,
-            segr, saved, blocks, shards, 1,
+            d_down, sent_y, dy, resid, x, a2_t, a1_t, df, gate, up, wgu, wdown, gain_two[None, :], gain_one[None, :],
+            wout, win, on, wbeta, deal_t, loss_part, proj, beta_pre, taps, gain_out, mask, segc, segr, saved, blocks,
+            shards, 1,
         )
         (output, input_grad, g_in, g_beta, g_taps, g_out, g_gain_one, g_gain_out, g_gain_two, g_gu, g_down,
-         loss) = settle(got_y, got_dx, sort_t, summed, counted.reshape(1, 1), g_down, g_gu, g_in, g_out)
+         loss) = settle(got_y, got_dx, sort_t, summed, counted, g_down, g_gu, g_in, g_out)
         g_gain_one, g_gain_out, g_gain_two = g_gain_one[0], g_gain_out[0], g_gain_two[0]
-        loss = loss[0, 0]
+        loss, g_beta = loss[0, 0], g_beta.T
     else:
+        gu = nn(a2, wgu)
+        gate, up = gu[:, :FF], gu[:, FF:]
+        hid = (gate * sigmoid(gate) * up).astype(BF16)
+        y = resid + nn(hid, wdown)
+        errors = y - t
+        loss_part = jnp.sum(m * errors * errors)
+        dy = g + (rows * shards / counted) * m * errors
+        df = dy.astype(BF16)
         (g_down, g_gu, dwq, dwk, dwv, dwg, dw_out, d_wbeta, dx, d_gain_two, d_gain_one, dtq, dtk, dtv,
          d_gain_out) = backward(
             tn(hid, df, BF16), df, a2, gu, wgu, wdown, dy, resid, gain_two[None, :], wout, win, a1, on, x,

time: 330 us -> 324 us (0.982)
  Pallas kernels: 302 us -> 319 us
  matrix products: 15.2 us -> 0 us
  local copies, waits for them, and re-layouts: 5.48 us -> 0 us
    pallas_call x0 -> x1, Pallas kernels: none -> 17.7 us  [middle(): pl.pallas_call(functools.partial(middle_kernel, float(rows * shards)), gr...]
    dot_general x4 -> x0, matrix products: 15.2 us -> none  [the longest x3 11 us: nn(): return jnp.dot(left, right, preferred_element_type=F32)]
    unnamed x13 -> x0, local copies, waits for them, and re-layouts: 5.48 us -> none
where the time goes in v6:
time: 324 us
  Pallas kernels  319 us (98%)
  other arithmetic  3.82 us (1%)
    pallas_call x1, Pallas kernels, front(): pl.pallas_call(functools.partial(front_kernel, shards, blocks, rows_mb, s...  151 us
    pallas_call x1, Pallas kernels, rear(): pl.pallas_call(functools.partial(rear_kernel, shards, blocks, rows_mb, pi...  146 us
    pallas_call x1, Pallas kernels, middle(): pl.pallas_call(functools.partial(middle_kernel, float(rows * shards)), gr...  17.7 us

profile of v6, /device:TPU:0, one launch (start us, length us, event | category | flops | bytes accessed | tf_op | source)
XLA Modules:
  0.0 323.8 jit_solution(11200562396187395090)
XLA Ops:
  0.6 1.2 bitcast_convert_fusion.refs_11_.refs_32_
  1.8 0.7 fusion.10
  2.5 0.7 fusion.7
  3.2 1.3 fusion.1.refs_4_
  4.5 150.9 %front.1 = (bf16[16,2,32,4096]{3,2,1,0:T(8,128)(2,1)}, bf16[16,2,32,1024]{3,2,1,0:T(8,128)(2,1)}, bf16[16,2,88,1024]{3,2,1,0:T(8,128)(2,1)}, bf16[16,2,32,5632]{...) custom-call(bf16[32,4096]{1,0:T(8,128)(2,1)} %refs_0_.1, ...), custom_call_target="tpu_custom_call" | custom-call | tf_op jit(solution)/shard_map/front/pallas_call | solution.py:890
  155.4 17.7 %middle.1 = (f32[256,2816]{1,0:T(8,128)}, f32[256,2816]{1,0:T(8,128)}, bf16[256,1024]{1,0:T(8,128)(2,1)}, f32[256,1024]{1,0:T(8,128)}, bf16[32,8,1024]{2,1,0:T(8...) custom-call(bf16[256,1024]{1,0:T(8,128)(2,1)} %get-tuple-element.70.a2, bf16[1024,5632]{1,0:T(8,128)(2,1)} %bitcast.18, ...), custom_call_target="tpu_custom_call" | custom-call | tf_op jit(solution)/shard_map/middle/pallas_call | solution.py:1465
  173.1 146.4 %rear.1 = (f32[88,1024]{1,0:T(8,128)}, f32[32,5632]{1,0:T(8,128)}, f32[32,4096]{1,0:T(8,128)}, f32[32,1024]{1,0:T(8,128)}, bf16[32,8,1024]{2,1,0:T(8,128)(2,1)},...) custom-call(bf16[16,2,88,1024]{3,2,1,0:T(8,128)(2,1)} %bitcast.28, bf16[32,8,1024]{2,1,0:T(8,128)(2,1)} %get-tuple-element.79.refs_1_, ...), custom_call_target="tpu_custom_call" | custom-call | tf_op jit(solution)/shard_map/rear/pallas_call | solution.py:1388
  319.5 4.3 %settle.1 = (bf16[256,1024]{1,0:T(8,128)(2,1)}, bf16[256,1024]{1,0:T(8,128)(2,1)}, f32[32,4096]{1,0:T(8,128)}, f32[8,32]{1,0:T(8,128)}, f32[4,96]{1,0:T(4,128)},...) custom-call(bf16[32,8,1024]{2,1,0:T(8,128)(2,1)} %get-tuple-element., ...), custom_call_target="tpu_custom_call" | custom-call | tf_op jit(solution)/shard_map/settle/pallas_call | solution.py:1506

commit v7 on v6

--- a/solution.py
+++ b/solution.py
@@ -689,9 +689,9 @@
 
 
 def front_kernel(shards, blocks, rows_mb, split, *refs):
-    (own_in, own_out, own_down, own_gu, small, tokens, cotangent, teacher, deal_row, valid_row, lengths, gain), refs = refs[:12], refs[12:]
+    (own_in, own_out, own_down, own_gu, small, tokens, cotangent, teacher, deal_row, valid_row, lengths), refs = refs[:11], refs[11:]
     (full_in, full_out, full_down, full_gu, pq, pk, pv, pg, beta, on, o, ainv, u, p, l, resid, a2, x, m, counted, deal, sort_t, gt, taps,
-     gain_one, gain_two, wbeta, segc, segr, mask, a1, a1_t, a2_t), refs = refs[:33], refs[33:]
+     gain_one, gain_two, wbeta, segc, segr, mask, a1, a1_t, a2_t, gain), refs = refs[:34], refs[34:]
     (sent, got, sent_gt, got_gt, got_small, wbuf, wout, w_sem, out_sem), refs = refs[:9], refs[9:]
     sems, deal_sems, later_sems, small_sems = refs[:5], refs[5:8], refs[8:11], refs[11:14]
     step = pl.program_id(0)
@@ -746,6 +746,7 @@
         meet(here, True)
         weights.step(0)
         small_send.start()
+        gain[...] = small[...].astype(F32)[6:7, :HEAD_DIM]
         row, col = iota2((rows, rows), 0), iota2((rows, rows), 1)
         column = lambda v: jnp.sum(jnp.where(row == col, v, 0.0), axis=1, keepdims=True)
         dealt = deal_row[...].astype(F32)
@@ -861,7 +862,7 @@
                 weights.end(of_in + split[1])
 
 
-def front(weights, small, tokens, cotangent, teacher, deal_rows, valid_mask, lengths, gain, shards, collective_id):
+def front(weights, small, tokens, cotangent, teacher, deal_rows, valid_mask, lengths, shards, collective_id):
     rows, blocks = tokens.shape[0], lengths.shape[0]
     rows_mb, share = rows // blocks, rows // shards
     width = PAIR * HEAD_DIM
@@ -886,13 +887,14 @@
         (jax.ShapeDtypeStruct((rows, 1), jnp.int32), full((rows, 1))),
         (jax.ShapeDtypeStruct((1, rows), jnp.int32), full((1, rows))), (f32(rows, 8), full((rows, 8))),
         (bf(rows, D), full((rows, D))), (bf(D, rows), full((D, rows))), (bf(D, rows), full((D, rows))),
+        (f32(1, HEAD_DIM), full((1, HEAD_DIM))),
     ]
     return pl.pallas_call(
         functools.partial(front_kernel, shards, blocks, rows_mb, split),
         grid=(HEADS // PAIR,),
         in_specs=[anywhere] * 4 + [
             full(small.shape), full((rows, D)), full((rows, D)), full((rows, D)), full((1, rows)), full((1, rows)),
-            full(lengths.shape), full((1, HEAD_DIM)),
+            full(lengths.shape),
         ],
         out_specs=[s for _, s in outs],
         out_shape=[s for s, _ in outs],
@@ -907,7 +909,7 @@
             collective_id=collective_id, has_side_effects=True, vmem_limit_bytes=58 << 20
         ),
         name="front",
-    )(*weights, small, tokens, cotangent, teacher, deal_rows[None, :], valid_mask[None, :], lengths, gain)
+    )(*weights, small, tokens, cotangent, teacher, deal_rows[None, :], valid_mask[None, :], lengths)
 
 
 def backward_kernel(shards, blocks, rows_mb, pieces, *refs):
@@ -1607,18 +1609,18 @@
     small = w_beta.shape[0] * HEADS + CONV * conv_kernel.shape[1] + 2 * norm_gain.shape[0]
 
     if share % 8 == 0 and (D // shards) % 16 == 0:
-        half = jnp.pad(
-            jnp.concatenate([conv_kernel, jnp.pad(jnp.stack([norm_gain, ffn_gain]), ((0, 0), (0, conv_kernel.shape[1] - norm_gain.shape[0])))]),
-            ((0, 2), (0, 128 - conv_kernel.shape[1])),
+        wide = lambda v: jnp.pad(v, ((0, 0), (0, 128 - v.shape[1])))
+        half = jnp.concatenate(
+            [wide(conv_kernel), wide(norm_gain[None, :]), wide(ffn_gain[None, :]), wide(out_gain[None, :]),
+             jnp.zeros((1, 128), BF16)]
         )
         small_block = jnp.concatenate(
             [half, jnp.pad(w_beta.T, ((0, 0), (0, 128 - w_beta.shape[0])))], axis=1
         )
-        gain_out = out_gain.astype(F32)[None, :]
         (win, wout, wdown, wgu, *proj, beta_pre, on, o, ainv, u, p, l, resid, a2, x, m, counted, deal_t, sort_t, later,
-         taps, gain_one, gain_two, wbeta, segc, segr, mask, a1, a1_t, a2_t) = front(
+         taps, gain_one, gain_two, wbeta, segc, segr, mask, a1, a1_t, a2_t, gain_out) = front(
             [w_in, w_out, w_down, w_gu], small_block, tokens, cotangent, teacher, deal_rows, valid_mask, lengths,
-            gain_out, shards, 0,
+            shards, 0,
         )
         win, wout, wdown, wgu = (w.reshape(-1, w.shape[-1]) for w in (win, wout, wdown, wgu))
         saved = (o, ainv, u, p, l)

time: 324 us -> 325 us (level)
  no operation moved by 1% of the time
where the time goes in v7:
time: 325 us; the launch traced here: 324 us
  Pallas kernels  319 us (98%)
    pallas_call x1, Pallas kernels, front(): pl.pallas_call(functools.partial(front_kernel, shards, blocks, rows_mb, s...  151 us
    pallas_call x1, Pallas kernels, rear(): pl.pallas_call(functools.partial(rear_kernel, shards, blocks, rows_mb, pi...  147 us
    pallas_call x1, Pallas kernels, middle(): pl.pallas_call(functools.partial(middle_kernel, float(rows * shards)), gr...  17.7 us

profile of v7, /device:TPU:0, one launch (start us, length us, event | category | flops | bytes accessed | tf_op | source)
XLA Modules:
  0.0 324.1 jit_solution(15067296375458695801)
XLA Ops:
  0.6 0.7 pad.16
  1.3 0.7 pad.17
  2.0 0.7 pad.15
  2.7 0.7 concatenate.6
  3.3 1.3 fusion.1.refs_4_
  4.6 150.9 %front.1 = (bf16[16,2,32,4096]{3,2,1,0:T(8,128)(2,1)}, bf16[16,2,32,1024]{3,2,1,0:T(8,128)(2,1)}, bf16[16,2,88,1024]{3,2,1,0:T(8,128)(2,1)}, bf16[16,2,32,5632]{...) custom-call(bf16[32,4096]{1,0:T(8,128)(2,1)} %refs_0_.1, ...), custom_call_target="tpu_custom_call" | custom-call | tf_op jit(solution)/shard_map/front/pallas_call | solution.py:892
  155.5 17.7 %middle.1 = (f32[256,2816]{1,0:T(8,128)}, f32[256,2816]{1,0:T(8,128)}, bf16[256,1024]{1,0:T(8,128)(2,1)}, f32[256,1024]{1,0:T(8,128)}, bf16[32,8,1024]{2,1,0:T(8...) custom-call(bf16[256,1024]{1,0:T(8,128)(2,1)} %get-tuple-element.71.a2, bf16[1024,5632]{1,0:T(8,128)(2,1)} %bitcast.16, ...), custom_call_target="tpu_custom_call" | custom-call | tf_op jit(solution)/shard_map/middle/pallas_call | solution.py:1467
  173.2 146.5 %rear.1 = (f32[88,1024]{1,0:T(8,128)}, f32[32,5632]{1,0:T(8,128)}, f32[32,4096]{1,0:T(8,128)}, f32[32,1024]{1,0:T(8,128)}, bf16[32,8,1024]{2,1,0:T(8,128)(2,1)},...) custom-call(bf16[16,2,88,1024]{3,2,1,0:T(8,128)(2,1)} %bitcast.26, bf16[32,8,1024]{2,1,0:T(8,128)(2,1)} %get-tuple-element.80.refs_1_, ...), custom_call_target="tpu_custom_call" | custom-call | tf_op jit(solution)/shard_map/rear/pallas_call | solution.py:1390
  319.8 4.3 %settle.1 = (bf16[256,1024]{1,0:T(8,128)(2,1)}, bf16[256,1024]{1,0:T(8,128)(2,1)}, f32[32,4096]{1,0:T(8,128)}, f32[8,32]{1,0:T(8,128)}, f32[4,96]{1,0:T(4,128)},...) custom-call(bf16[32,8,1024]{2,1,0:T(8,128)(2,1)} %get-tuple-element., ...), custom_call_target="tpu_custom_call" | custom-call | tf_op jit(solution)/shard_map/settle/pallas_call | solution.py:1508
  (1 shorter events, 0.0 us)
